TPU v7x, 32 devices: a whole 2x2x4 slice. The times are simulated.
32 devices in a mesh: fsdp: 4 (over z), ctx: 2 (over x), tp: 4 (over y, core).
Axes of the slice: x: 2, y: 2, z: 4, core: 2. Of those that a mesh axis runs over, the one named last changes fastest.
Arguments:
- tokens: bfloat16 [6144, 1600], P(('fsdp', 'ctx')), may hold values from -6 to 6
- segments: int32 [6144], P('fsdp'), may hold values from 0 to 15, never falling along the last dimension, each value on 1 to 768 neighbouring positions
- first_gain: bfloat16 [1600], P('fsdp'), may hold values from 0.5 to 1.5
- first_bias: bfloat16 [1600], P('fsdp'), may hold values from -1.5 to 1.5
- input_weight: bfloat16 [1600, 4800], P('fsdp'), may hold values from -2 to 2
- query_bias: bfloat16 [1600], P('fsdp'), may hold values from -1.5 to 1.5
- value_bias: bfloat16 [1600], P('fsdp'), may hold values from -1.5 to 1.5
- output_weight: bfloat16 [1600, 1600], P('fsdp'), may hold values from -0.625 to 0.625
- output_bias: bfloat16 [1600], P('fsdp'), may hold values from -1.5 to 1.5
- second_gain: bfloat16 [1600], P('fsdp'), may hold values from 0.5 to 1.5
- second_bias: bfloat16 [1600], P('fsdp'), may hold values from -1.5 to 1.5
- up_weight: bfloat16 [1600, 6400], P('fsdp', 'tp'), may hold values from -0.15625 to 0.15625
- up_bias: bfloat16 [6400], P(('tp', 'fsdp')), may hold values from -1.5 to 1.5
- down_weight: bfloat16 [6400, 1600], P('tp', 'fsdp'), may hold values from -0.078125 to 0.078125
- down_bias: bfloat16 [1600], P('fsdp'), may hold values from -1.5 to 1.5
- cotangent: bfloat16 [6144, 1600], P(('fsdp', 'ctx')), may hold values from -6 to 6
Outputs:
- result: bfloat16 [6144, 1600], P(('fsdp', 'ctx'))
- token_gradient: bfloat16 [6144, 1600], P(('fsdp', 'ctx'))
- first_gain_gradient: float32 [1600], P('fsdp')
- first_bias_gradient: float32 [1600], P('fsdp')
- input_weight_gradient: float32 [1600, 4800], P('fsdp')
- query_bias_gradient: float32 [1600], P('fsdp')
- value_bias_gradient: float32 [1600], P('fsdp')
- output_weight_gradient: float32 [1600, 1600], P('fsdp')
- output_bias_gradient: float32 [1600], P('fsdp')
- second_gain_gradient: float32 [1600], P('fsdp')
- second_bias_gradient: float32 [1600], P('fsdp')
- up_weight_gradient: float32 [1600, 6400], P('fsdp', 'tp')
- up_bias_gradient: float32 [6400], P(('tp', 'fsdp'))
- down_weight_gradient: float32 [6400, 1600], P('tp', 'fsdp')
- down_bias_gradient: float32 [1600], P('fsdp')
Inputs may be any that keep to these rules, and one draw needn't show every extreme that they name: `segments`: segment numbers never fall along the tokens; each segment holds 1 to 768 tokens, one exactly 768.
All inputs are finite; a program needn't handle non-finite values.
Results may differ from a plain program's by a relative error of at most 0.012.
Values may be sent and summed in bfloat16 or wider, within the bound.
No kernel may reach another device: no remote copies, remote signals or barrier semaphores. Data moves between devices by JAX's collectives and lax.ppermute only.
A program may use at most 256 MiB of HBM per device.

v0:
```python
from functools import partial

import jax
import jax.numpy as jnp
from jax import lax
from jax.sharding import PartitionSpec as P

HEADS = 25
HEAD = 64


EPS = 1e-05
NEGATIVE = -1e30


def norm_forward(values, gain, offset):
    centre = values - jnp.mean(values, -1, keepdims=True)
    inverse = lax.rsqrt(jnp.mean(centre * centre, -1, keepdims=True) + EPS)
    unit = centre * inverse
    return (unit * gain + offset, unit, inverse)


def norm_backward(upstream, unit, inverse, gain):
    scaled = upstream * gain
    inner = (
        scaled
        - jnp.mean(scaled, -1, keepdims=True)
        - unit * jnp.mean(scaled * unit, -1, keepdims=True)
    )
    return (inner * inverse, jnp.sum(upstream * unit, 0), jnp.sum(upstream, 0))


def contract_rows(left, right):
    return lax.dot_general(
        left, right, (((0,), (0,)), ((), ())), preferred_element_type=jnp.float32
    )


def gelu_tanh(values):
    return jax.nn.gelu(values, approximate=True)


def to_heads(values, count):
    return values.reshape(count, HEADS, HEAD).transpose(1, 0, 2)


def from_heads(values, count):
    return values.transpose(1, 0, 2).reshape(count, HEADS * HEAD)


def head_forward(allowed, triple):
    head_query, head_key, head_value = triple
    scores = jnp.einsum(
        "qd,kd->qk", head_query, head_key, preferred_element_type=jnp.float32
    ) * HEAD ** (-0.5)
    scores = jnp.where(allowed, scores, NEGATIVE)
    highest = jnp.max(scores, -1, keepdims=True)
    expo = jnp.exp(scores - highest)
    summed = jnp.sum(expo, -1, keepdims=True)
    weights = (expo / summed).astype(jnp.bfloat16)
    mixed = jnp.dot(weights, head_value, preferred_element_type=jnp.float32)
    return (mixed, (highest + jnp.log(summed))[:, 0])


def head_backward(allowed, quintet):
    head_query, head_key, head_value, head_grad, log_total = quintet
    scores = jnp.einsum(
        "qd,kd->qk", head_query, head_key, preferred_element_type=jnp.float32
    ) * HEAD ** (-0.5)
    scores = jnp.where(allowed, scores, NEGATIVE)
    probs = jnp.exp(scores - log_total[:, None])
    grad_value = contract_rows(probs.astype(jnp.bfloat16), head_grad)
    grad_probs = jnp.einsum("qd,kd->qk", head_grad, head_value, preferred_element_type=jnp.float32)
    centred = grad_probs - jnp.sum(probs * grad_probs, -1, keepdims=True)
    grad_scores = (probs * centred).astype(jnp.bfloat16)
    grad_query = jnp.dot(grad_scores, head_key, preferred_element_type=jnp.float32) * HEAD ** (-0.5)
    grad_key = contract_rows(grad_scores, head_query) * HEAD ** (-0.5)
    return (grad_query, grad_key, grad_value)


def on_device(
    tokens,
    segments,
    first_gain,
    first_bias,
    input_weight,
    query_bias,
    value_bias,
    output_weight,
    output_bias,
    second_gain,
    second_bias,
    up_weight,
    up_bias,
    down_weight,
    down_bias,
    cotangent,
):
    row_count = tokens.shape[0]
    key_count = segments.shape[0]
    cycle_index = lax.axis_index("ctx")
    gain_one, bias_one, weight_in, bias_query, bias_value, weight_out, bias_out = (
        lax.all_gather(first_gain, "fsdp", axis=0, tiled=True),
        lax.all_gather(first_bias, "fsdp", axis=0, tiled=True),
        lax.all_gather(input_weight, "fsdp", axis=0, tiled=True),
        lax.all_gather(query_bias, "fsdp", axis=0, tiled=True),
        lax.all_gather(value_bias, "fsdp", axis=0, tiled=True),
        lax.all_gather(output_weight, "fsdp", axis=0, tiled=True),
        lax.all_gather(output_bias, "fsdp", axis=0, tiled=True),
    )
    gain_two, bias_two, weight_up, bias_up, weight_down, bias_down = (
        lax.all_gather(second_gain, "fsdp", axis=0, tiled=True),
        lax.all_gather(second_bias, "fsdp", axis=0, tiled=True),
        lax.all_gather(up_weight, "fsdp", axis=0, tiled=True),
        lax.all_gather(up_bias, "fsdp", axis=0, tiled=True),
        lax.all_gather(down_weight, "fsdp", axis=1, tiled=True),
        lax.all_gather(down_bias, "fsdp", axis=0, tiled=True),
    )
    gain_one_f = gain_one.astype(jnp.float32)
    gain_two_f = gain_two.astype(jnp.float32)
    width = tokens.shape[1]
    inputs = tokens.astype(jnp.float32)
    normed_one, unit_one, inverse_one = norm_forward(
        inputs, gain_one_f, bias_one.astype(jnp.float32)
    )
    normed_one = normed_one.astype(jnp.bfloat16)
    joined = jnp.dot(normed_one, weight_in, preferred_element_type=jnp.float32)
    queries = (joined[:, :width] + bias_query.astype(jnp.float32)).astype(jnp.bfloat16)
    keys_own = joined[:, width : 2 * width].astype(jnp.bfloat16)
    values_own = (joined[:, 2 * width :] + bias_value.astype(jnp.float32)).astype(jnp.bfloat16)
    keys_all, values_all = (
        lax.all_gather(keys_own, "ctx", axis=0, tiled=True),
        lax.all_gather(values_own, "ctx", axis=0, tiled=True),
    )
    query_places = cycle_index * row_count + jnp.arange(row_count)
    labels_query = lax.dynamic_slice_in_dim(segments, cycle_index * row_count, row_count)
    allowed = (labels_query[:, None] == segments[None, :]) & (
        jnp.arange(key_count)[None, :] <= query_places[:, None]
    )
    query_heads = to_heads(queries, row_count)
    key_heads = to_heads(keys_all, key_count)
    value_heads = to_heads(values_all, key_count)
    mixture, log_total = lax.map(
        partial(head_forward, allowed), (query_heads, key_heads, value_heads)
    )
    mixture = from_heads(mixture, row_count).astype(jnp.bfloat16)
    middle = (
        inputs
        + jnp.dot(mixture, weight_out, preferred_element_type=jnp.float32)
        + bias_out.astype(jnp.float32)
    )
    normed_own, unit_two, inverse_two = norm_forward(
        middle, gain_two_f, bias_two.astype(jnp.float32)
    )
    normed_own = normed_own.astype(jnp.bfloat16)
    preact = jnp.dot(normed_own, weight_up, preferred_element_type=jnp.float32) + bias_up.astype(
        jnp.float32
    )
    activated = gelu_tanh(preact).astype(jnp.bfloat16)
    partial_out = jnp.dot(activated, weight_down, preferred_element_type=jnp.float32)
    summed_out = lax.psum(partial_out.astype(jnp.bfloat16), "tp").astype(jnp.float32)
    result_own = (middle + summed_out + bias_down.astype(jnp.float32)).astype(jnp.bfloat16)
    back_in, back_out = (
        lax.all_gather(input_weight, "fsdp", axis=0, tiled=True),
        lax.all_gather(output_weight, "fsdp", axis=0, tiled=True),
    )
    back_up, back_down = (
        lax.all_gather(up_weight, "fsdp", axis=0, tiled=True),
        lax.all_gather(down_weight, "fsdp", axis=1, tiled=True),
    )
    upstream = cotangent.astype(jnp.float32)
    grad_bias_down = jnp.sum(upstream, 0)
    grad_down = contract_rows(activated, cotangent)
    grad_activated = jnp.einsum(
        "rd,fd->rf", cotangent, back_down, preferred_element_type=jnp.float32
    )
    unused, gelu_pull = jax.vjp(gelu_tanh, preact)
    grad_preact = gelu_pull(grad_activated)[0].astype(jnp.bfloat16)
    grad_up = contract_rows(normed_own, grad_preact)
    grad_bias_up = jnp.sum(grad_preact.astype(jnp.float32), 0)
    grad_normed_part = jnp.einsum(
        "rf,df->rd", grad_preact, back_up, preferred_element_type=jnp.float32
    )
    grad_normed_two = lax.psum(grad_normed_part, "tp")
    grad_from_two, grad_gain_two, grad_bias_two = norm_backward(
        grad_normed_two, unit_two, inverse_two, gain_two_f
    )
    grad_middle = cotangent.astype(jnp.float32) + grad_from_two
    grad_branch = grad_middle.astype(jnp.bfloat16)
    grad_bias_out = jnp.sum(grad_branch.astype(jnp.float32), 0)
    grad_out = contract_rows(mixture, grad_branch)
    grad_mixture = jnp.einsum(
        "re,de->rd", grad_branch, back_out, preferred_element_type=jnp.float32
    ).astype(jnp.bfloat16)
    grad_heads = to_heads(grad_mixture, row_count)
    grad_q, grad_k, grad_v = lax.map(
        partial(head_backward, allowed),
        (query_heads, key_heads, value_heads, grad_heads, log_total),
    )
    grad_q, grad_k, grad_v = (grad_q, grad_k, grad_v)
    grad_keys, grad_values = (
        lax.psum_scatter(
            from_heads(grad_k, key_count).astype(jnp.bfloat16),
            "ctx",
            scatter_dimension=0,
            tiled=True,
        ).astype(jnp.float32),
        lax.psum_scatter(
            from_heads(grad_v, key_count).astype(jnp.bfloat16),
            "ctx",
            scatter_dimension=0,
            tiled=True,
        ).astype(jnp.float32),
    )
    grad_queries = from_heads(grad_q, row_count).astype(jnp.bfloat16)
    grad_keys = grad_keys.astype(jnp.bfloat16)
    grad_values = grad_values.astype(jnp.bfloat16)
    grad_joined = jnp.concatenate([grad_queries, grad_keys, grad_values], axis=1)
    grad_in = contract_rows(normed_one, grad_joined)
    grad_bias_query = jnp.sum(grad_queries.astype(jnp.float32), 0)
    grad_bias_value = jnp.sum(grad_values.astype(jnp.float32), 0)
    grad_normed_one = jnp.einsum(
        "re,de->rd", grad_joined, back_in, preferred_element_type=jnp.float32
    )
    grad_from_one, grad_gain_one, grad_bias_one = norm_backward(
        grad_normed_one, unit_one, inverse_one, gain_one_f
    )
    gradient_own = (grad_middle + grad_from_one).astype(jnp.bfloat16)
    result, token_gradient = (result_own, gradient_own)
    shards = (
        lax.psum_scatter(grad_gain_one, "fsdp", scatter_dimension=0, tiled=True),
        lax.psum_scatter(grad_bias_one, "fsdp", scatter_dimension=0, tiled=True),
        lax.psum_scatter(grad_in, "fsdp", scatter_dimension=0, tiled=True),
        lax.psum_scatter(grad_bias_query, "fsdp", scatter_dimension=0, tiled=True),
        lax.psum_scatter(grad_bias_value, "fsdp", scatter_dimension=0, tiled=True),
        lax.psum_scatter(grad_out, "fsdp", scatter_dimension=0, tiled=True),
        lax.psum_scatter(grad_bias_out, "fsdp", scatter_dimension=0, tiled=True),
        lax.psum_scatter(grad_gain_two, "fsdp", scatter_dimension=0, tiled=True),
        lax.psum_scatter(grad_bias_two, "fsdp", scatter_dimension=0, tiled=True),
        lax.psum_scatter(grad_up, "fsdp", scatter_dimension=0, tiled=True),
        lax.psum_scatter(grad_bias_up, "fsdp", scatter_dimension=0, tiled=True),
        lax.psum_scatter(grad_down, "fsdp", scatter_dimension=1, tiled=True),
        lax.psum_scatter(grad_bias_down, "fsdp", scatter_dimension=0, tiled=True),
    )
    (
        shard_gain_one,
        shard_bias_one,
        shard_in,
        shard_query,
        shard_value,
        shard_out,
        shard_bias_out,
        shard_gain_two,
        shard_bias_two,
        shard_up,
        shard_bias_up,
        shard_down,
        shard_bias_down,
    ) = lax.psum(
        (
            shards[0],
            shards[1],
            shards[2],
            shards[3],
            shards[4],
            shards[5],
            shards[6],
            shards[7],
            shards[8],
            shards[9],
            shards[10],
            shards[11],
            shards[12],
        ),
        "ctx",
    )
    return (
        result,
        token_gradient,
        shard_gain_one,
        shard_bias_one,
        shard_in,
        shard_query,
        shard_value,
        shard_out,
        shard_bias_out,
        shard_gain_two,
        shard_bias_two,
        shard_up,
        shard_bias_up,
        shard_down,
        shard_bias_down,
    )


def solution(mesh):
    return jax.shard_map(
        on_device,
        mesh=mesh,
        in_specs=(
            P(("fsdp", "ctx"), None),
            P("fsdp"),
            P("fsdp"),
            P("fsdp"),
            P("fsdp", None),
            P("fsdp"),
            P("fsdp"),
            P("fsdp", None),
            P("fsdp"),
            P("fsdp"),
            P("fsdp"),
            P("fsdp", "tp"),
            P(("tp", "fsdp")),
            P("tp", "fsdp"),
            P("fsdp"),
            P(("fsdp", "ctx"), None),
        ),
        out_specs=(
            P(("fsdp", "ctx"), None),
            P(("fsdp", "ctx"), None),
            P("fsdp"),
            P("fsdp"),
            P("fsdp", None),
            P("fsdp"),
            P("fsdp"),
            P("fsdp", None),
            P("fsdp"),
            P("fsdp"),
            P("fsdp"),
            P("fsdp", "tp"),
            P(("tp", "fsdp")),
            P("tp", "fsdp"),
            P("fsdp"),
        ),
        check_vma=False,
    )
```

profile of v0, /device:TPU:0, one launch (start us, length us, event | category | flops | bytes accessed | tf_op | source)
XLA Modules:
  0.0 2809.9 jit_solution(5696364689711752278)
XLA Ops:
  17.8 35.6 %all-reduce.21 = (bf16[1600]{0:T(1024)(128)(2,1)S(1)}, bf16[1600]{0:T(1024)(128)(2,1)S(1)}, bf16[1600]{0:T(1024)(128)(2,1)S(1)}, bf16[1600]{0:T(1024)(128)(2,1)S...) all-reduce(bf16[1600]{0:T(1024)(128)(2,1)S(1)} %dynamic-update-slic, ...), channel_id=1, replica_groups=mesh['fsdp'=4,'ctx'=2,'tp'=4] {'fsdp'}, use_global_device_ids=true, to_apply=%add.1 | all-reduce | flops 14400 | bytes 57600
  54.7 225.6 %all-gather.7.cloned.1.call-done = bf16[1600,4800]{1,0:T(8,128)(2,1)} async-done(((bf16[400,4800]{1,0:T(8,128)(2,1)}), bf16[1600,4800]{1,0:T(8,128)(2,1)}) %all-gather.7.cloned.1.call-update) | async-done | bytes 15360016 | tf_op jit(solution)/shard_map/all_gather | solution.py:105
  280.3 20.5 fusion.83
  300.8 5.8 fusion.73
  312.9 5.9 copy.35
  318.9 51.2 %all-gather.11.cloned.1.call-done = bf16[1536,1600]{0,1:T(8,128)(2,1)} async-done(((bf16[768,1600]{0,1:T(8,128)(2,1)}), bf16[1536,1600]{0,1:T(8,128)(2,1)}) %all-gather.11.cloned.1.call-update) | async-done | bytes 4915216 | tf_op jit(solution)/shard_map/all_gather | solution.py:133
  370.0 10.2 copy.37
  380.2 56.8 %all-gather.9.cloned.1.call-done = bf16[1536,1600]{0,1:T(8,128)(2,1)} async-done(((bf16[768,1600]{0,1:T(8,128)(2,1)}), bf16[1536,1600]{0,1:T(8,128)(2,1)}) %all-gather.9.cloned.1.call-update) | async-done | bytes 4915216 | tf_op jit(solution)/shard_map/all_gather | solution.py:132
  437.0 10.1 copy.36
  448.9 242.7 %while.28 = (s32[]{:T(128)}, bf16[25,768,64]{1,2,0:T(8,128)(2,1)}, f32[25,768]{1,0:T(8,128)S(1)}, bf16[25,768,64]{2,1,0:T(8,128)(2,1)}, bf16[25,1536,64]{2,1,0:T...) while((s32[]{:T(128)}, bf16[25,768,64]{1,2,0:T(8,128)(2,1)}, ...), condition=%wide.region_5.6_spmd.clone, body=%wide.region_2.5_spmd.clone.sunk | while | flops 314965248 | bytes 34261132 | solution.py:143
  454.4 4.2 fusion.128
  473.8 4.2 fusion.128
  483.5 4.2 fusion.128
  502.9 4.2 fusion.128
  541.7 4.3 fusion.128
  561.2 4.2 fusion.128
  580.6 4.2 fusion.128
  609.7 4.2 fusion.128
  658.2 4.2 fusion.128
  687.3 4.2 fusion.128
  691.6 8.6 fusion.91
  703.0 11.5 fusion.86
  714.5 21.7 all-gather.17.cloned.1.call-done
  736.2 21.6 convert_reduce_fusion.2
  759.3 6.3 fusion.92
  765.7 10.7 convolution_convert_fusion.1
  776.5 84.8 %all-reduce.28.cloned.1.call-done = f32[768,1600]{0,1:T(8,128)} async-done(((f32[768,1600]{0,1:T(8,128)}), f32[768,1600]{0,1:T(8,128)}) %all-reduce.28.cloned.1.call-update) | async-done | bytes 4915216 | tf_op jit(solution)/shard_map/psum | solution.py:184
  861.3 5.8 multiply_reduce_fusion.1
  867.1 54.6 %all-reduce.26.cloned.1.call-done = bf16[768,1600]{0,1:T(8,128)(2,1)} async-done(((bf16[768,1600]{0,1:T(8,128)(2,1)}), bf16[768,1600]{0,1:T(8,128)(2,1)}) %all-reduce.26.cloned.1.call-update) | async-done | bytes 2457616 | tf_op jit(solution)/shard_map/psum | solution.py:161
  921.7 7.5 convert_reduce_fusion.3
  929.2 9.0 convolution_convert_fusion
  942.5 293.1 %while.29 = (s32[]{:T(128)}, bf16[25,768,64]{1,2,0:T(8,128)(2,1)S(1)}, bf16[25,1536,64]{1,2,0:T(8,128)(2,1)}, bf16[25,1536,64]{1,2,0:T(8,128)(2,1)}, bf16[25,768...) while((s32[]{:T(128)}, ...), condition=%wide.region_14.15_spmd.clone, body=%wide.region_12.14_spmd.clone.sunk | while | flops 769277184 | bytes 38371456 | solution.py:196
  1237.5 12.1 fusion.85
  1251.2 10.4 fusion.87
  1263.3 9.7 fusion.79
  1273.3 24.8 reduce-scatter.7.cloned.1.call-done
  1298.1 64.4 %reduce-scatter.9.cloned.1.call-done = bf16[768,1600]{0,1:T(8,128)(2,1)} async-done(((bf16[1536,1600]{0,1:T(8,128)(2,1)}), bf16[768,1600]{0,1:T(8,128)(2,1)}) %reduce-scatter.9.cloned.1.call-update) | async-done | bytes 2457616 | tf_op jit(solution)/shard_map/reduce_scatter | solution.py:208
  1362.5 22.0 fusion.75
  1384.6 161.4 %reduce-scatter.15.cloned.1.call-done = f32[400,1600]{1,0:T(8,128)} async-done(((f32[1600,1600]{1,0:T(8,128)}), f32[400,1600]{1,0:T(8,128)}) %reduce-scatter.15.cloned.1.call-update) | async-done | bytes 2560016 | tf_op jit(solution)/shard_map/reduce_scatter | solution.py:240
  1545.9 184.3 %reduce-scatter.17.cloned.1.call-done = f32[1600,400]{0,1:T(8,128)} async-done(((f32[1600,1600]{0,1:T(8,128)}), f32[1600,400]{0,1:T(8,128)}) %reduce-scatter.17.cloned.1.call-update) | async-done | bytes 2560016 | tf_op jit(solution)/shard_map/reduce_scatter | solution.py:242
  1730.2 184.5 %reduce-scatter.13.cloned.1.call-done = f32[400,1600]{1,0:T(8,128)} async-done(((f32[1600,1600]{1,0:T(8,128)}), f32[400,1600]{1,0:T(8,128)}) %reduce-scatter.13.cloned.1.call-update) | async-done | bytes 2560016 | tf_op jit(solution)/shard_map/reduce_scatter | solution.py:236
  1914.7 514.2 %reduce-scatter.11.cloned.1.call-done = f32[400,4800]{1,0:T(8,128)} async-done(((f32[1600,4800]{1,0:T(8,128)}), f32[400,4800]{1,0:T(8,128)}) %reduce-scatter.11.cloned.1.call-update) | async-done | bytes 7680016 | tf_op jit(solution)/shard_map/reduce_scatter | solution.py:233
  2433.9 22.9 fusion.63
  2456.8 21.1 all-reduce.18
  2478.6 9.7 all-reduce.19
  2488.3 5.9 fusion.62
  2494.1 296.2 %all-reduce.30.cloned.1.call-done = (f32[400,4800]{1,0:T(8,128)}, f32[400,1600]{1,0:T(8,128)}, f32[400,1600]{1,0:T(8,128)}, f32[1600,400]{0,1:T(8,128)}) async-done(((f32[400,4800]{1,0:T(8,128)}, f32[400,1600]{1,0:T(8,128)}, f32[400,1600]{1,0:T(8,128)}, f32[1600,400]{0,1:T(8,128)}), (f32[400,4800]{1,0:T(8,128)}, f32[400,1600]{1,0:T(8,128)}, f32[400,1600]{1,0:T(8,128)}, ...) | async-done | bytes 15360016 | tf_op jit(solution)/shard_map/psum | solution.py:259
  2790.4 7.1 copy.82
  (513 shorter events, 535.7 us)
Async XLA Ops:
  7.2 46.3 %copy-start.2 = (bf16[768,1600]{0,1:T(8,128)(2,1)S(1)}, bf16[768,1600]{0,1:T(8,128)(2,1)}, u32[]{:S(2)}) copy-start(bf16[768,1600]{0,1:T(8,128)(2,1)} %param.20) | copy-start | bytes 7372804
  7.2 273.1 %all-gather.7.cloned.1.call-start = ((), (), s32[]{:S(2)}) async-start(), calls=%async_computation.6 | async-start | bytes 19456000 | tf_op jit(solution)/shard_map/all_gather | solution.py:105
  7.9 362.1 %all-gather.11.cloned.1.call-start = ((), (), s32[]{:S(2)}) async-start(), calls=%async_computation.8 | async-start | bytes 7372800 | tf_op jit(solution)/shard_map/all_gather | solution.py:133
  53.4 247.3 %copy-start.16 = (f32[1600]{0:T(1024)}, f32[1600]{0:T(1024)S(1)}, u32[]{:S(2)}) copy-start(f32[1600]{0:T(1024)S(1)} %convert_element_type.137) | copy-start | bytes 19204
  53.5 247.3 %copy-start.23 = (f32[1600]{0:T(1024)}, f32[1600]{0:T(1024)S(1)}, u32[]{:S(2)}) copy-start(f32[1600]{0:T(1024)S(1)} %convert_element_type.138) | copy-start | bytes 19204
  53.9 246.8 %copy-start.12 = (f32[768]{0:T(1024)}, f32[768]{0:T(1024)S(1)}, u32[]{:S(2)}) copy-start(f32[768]{0:T(1024)S(1)} %broadcast_multiply_fusion.5) | copy-start | bytes 9220
  54.7 246.1 %copy-start.20 = (f32[768]{0:T(1024)}, f32[768]{0:T(1024)S(1)}, u32[]{:S(2)}) copy-start(f32[768]{0:T(1024)S(1)} %add_rsqrt_fusion.1) | copy-start | bytes 9220
  306.6 6.3 copy-start.25
  306.6 130.5 %all-gather.9.cloned.1.call-start = ((), (), s32[]{:S(2)}) async-start(), calls=%async_computation.7 | async-start | bytes 7372800 | tf_op jit(solution)/shard_map/all_gather | solution.py:132
  310.7 380.8 %all-gather.13.cloned.1.call-start = ((), (), s32[]{:S(2)}) async-start(), calls=%async_computation.9 | async-start | bytes 6656000 | tf_op jit(solution)/shard_map/all_gather | solution.py:108
  311.3 391.7 %all-gather.15.cloned.1.call-start = ((), (), s32[]{:S(2)}) async-start(), calls=%async_computation.10 | async-start | bytes 6656000 | tf_op jit(solution)/shard_map/all_gather | solution.py:114
  311.9 424.3 %all-gather.17.cloned.1.call-start = ((), (), s32[]{:S(2)}) async-start(), calls=%async_computation.11 | async-start | bytes 6656000 | tf_op jit(solution)/shard_map/all_gather | solution.py:116
  312.5 548.8 %all-reduce.28.cloned.1.call-start = ((), (), s32[]{:S(2)}) async-start(), calls=%async_computation.13 | async-start | bytes 9830400 | tf_op jit(solution)/shard_map/psum | solution.py:184
  451.4 2.1 copy-start
  461.1 2.1 copy-start
  470.8 2.1 copy-start
  480.5 2.1 copy-start
  490.3 2.1 copy-start
  499.9 2.1 copy-start
  577.6 2.1 copy-start
  606.7 2.1 copy-start
  655.2 2.1 copy-start
  684.3 2.1 copy-start
  700.2 2.2 copy-start.1
  703.0 33.2 %copy-start.9 = (bf16[768,1600]{0,1:T(8,128)(2,1)S(1)}, bf16[768,1600]{0,1:T(8,128)(2,1)}, u32[]{:S(2)}) copy-start(bf16[768,1600]{0,1:T(8,128)(2,1)} %param.35) | copy-start | bytes 7372804
  736.2 23.1 copy-start.26
  765.6 156.1 %all-reduce.26.cloned.1.call-start = ((), (), s32[]{:S(2)}) async-start(), calls=%async_computation.12 | async-start | bytes 4915200 | tf_op jit(solution)/shard_map/psum | solution.py:161
  776.4 521.7 %reduce-scatter.7.cloned.1.call-start = ((), (), s32[]{:S(2)}) async-start(), calls=%async_computation.14 | async-start | bytes 7372800 | tf_op jit(solution)/shard_map/reduce_scatter | solution.py:202
  929.2 9.0 copy-start.4
  1235.6 126.8 %reduce-scatter.9.cloned.1.call-start = ((), (), s32[]{:S(2)}) async-start(), calls=%async_computation.15 | async-start | bytes 7372800 | tf_op jit(solution)/shard_map/reduce_scatter | solution.py:208
  1237.0 308.9 %reduce-scatter.15.cloned.1.call-start = ((), (), s32[]{:S(2)}) async-start(), calls=%async_computation.18 | async-start | bytes 13312000 | tf_op jit(solution)/shard_map/reduce_scatter | solution.py:240
  1249.6 480.7 %reduce-scatter.17.cloned.1.call-start = ((), (), s32[]{:S(2)}) async-start(), calls=%async_computation.19 | async-start | bytes 13312000 | tf_op jit(solution)/shard_map/reduce_scatter | solution.py:242
  1261.7 653.0 %reduce-scatter.13.cloned.1.call-start = ((), (), s32[]{:S(2)}) async-start(), calls=%async_computation.17 | async-start | bytes 13312000 | tf_op jit(solution)/shard_map/reduce_scatter | solution.py:236
  1273.0 89.4 %copy-start.3 = (bf16[768,1600]{0,1:T(8,128)(2,1)S(1)}, bf16[768,1600]{0,1:T(8,128)(2,1)}, u32[]{:S(2)}) copy-start(bf16[768,1600]{0,1:T(8,128)(2,1)} %param.20) | copy-start | bytes 7372804
  1273.0 89.4 %copy-start.13 = (f32[768]{0:T(1024)S(1)}, f32[768]{0:T(1024)}, u32[]{:S(2)}) copy-start(f32[768]{0:T(1024)} %copy-done.12) | copy-start | bytes 9220
  1273.0 89.4 %copy-start.17 = (f32[1600]{0:T(1024)S(1)}, f32[1600]{0:T(1024)}, u32[]{:S(2)}) copy-start(f32[1600]{0:T(1024)} %copy-done.16) | copy-start | bytes 19204
  1273.1 89.4 %copy-start.21 = (f32[768]{0:T(1024)S(1)}, f32[768]{0:T(1024)}, u32[]{:S(2)}) copy-start(f32[768]{0:T(1024)} %copy-done.20) | copy-start | bytes 9220
  1273.1 89.4 %copy-start.24 = (f32[1600]{0:T(1024)S(1)}, f32[1600]{0:T(1024)}, u32[]{:S(2)}) copy-start(f32[1600]{0:T(1024)} %copy-done.23) | copy-start | bytes 19204
  1273.1 1155.8 %reduce-scatter.11.cloned.1.call-start = ((), (), s32[]{:S(2)}) async-start(), calls=%async_computation.16 | async-start | bytes 38912000 | tf_op jit(solution)/shard_map/reduce_scatter | solution.py:233
  1384.5 1405.9 %all-reduce.30.cloned.1.call-start = ((), (), s32[]{:S(2)}) async-start(), calls=%async_computation.20 | async-start | bytes 31539200 | tf_op jit(solution)/shard_map/psum | solution.py:259
  2433.8 23.0 copy-start.14
  2433.8 23.0 copy-start.15
  2433.8 23.0 copy-start.18
  2433.8 23.0 copy-start.19
  2433.8 23.0 copy-start.22
  2790.4 7.1 copy-start.8
  2797.5 2.7 copy-start.7
  2797.5 4.2 copy-start.6
  (19 other events, 38.1 us)
Sparse Core Ops, SparseCore 0:
  9.6 270.6 all-gather.6
  306.7 63.2 all-gather.10
  372.2 64.8 all-gather.8
  438.5 99.3 all-gather.12
  539.3 97.6 all-gather.14
  638.5 97.6 all-gather.16
  765.7 95.5 all-reduce.27
  864.2 57.4 all-reduce.25
  1235.8 62.2 reduce-scatter.6
  1300.2 62.1 reduce-scatter.8
  1364.8 181.0 reduce-scatter.14
  1548.1 182.0 reduce-scatter.16
  1732.6 182.0 reduce-scatter.12
  1916.9 511.8 reduce-scatter.10
  2431.3 359.0 all-reduce.29
where the time goes:
time: 2820 us; the launch traced here: 2810 us
  waiting for transfers between devices  1930 us (68%)
  matrix products  613 us (22%)
  local copies, waits for them, and re-layouts  122 us (4%)
  blocking collectives  66.4 us (2%)
  other arithmetic  62.1 us (2%)
    reduce_scatter x1, waiting for transfers between devices, on_device(): lax.psum_scatter(grad_in, 'fsdp', scatter_dimension=0, tiled=True)  514 us
    psum x1, waiting for transfers between devices, on_device(): lax.psum((shards[0], shards[1], shards[2], shards[3], shards[4], shards[5...  296 us
    all_gather x1, waiting for transfers between devices, on_device(): lax.all_gather(input_weight, 'fsdp', axis=0, tiled=True)  226 us
    reduce_scatter x1, waiting for transfers between devices, on_device(): lax.psum_scatter(grad_out, 'fsdp', scatter_dimension=0, tiled=True)  184 us
    reduce_scatter x1, waiting for transfers between devices, on_device(): lax.psum_scatter(grad_down, 'fsdp', scatter_dimension=1, tiled=True)  184 us
    dot_general x54, matrix products, contract_rows(): lax.dot_general(left, right, (((0,), (0,)), ((), ())), preferred_element_...  164 us
    reduce_scatter x1, waiting for transfers between devices, on_device(): lax.psum_scatter(grad_up, 'fsdp', scatter_dimension=0, tiled=True)  161 us
    dot_general x25, matrix products, head_forward(): mixed = jnp.dot(weights, head_value, preferred_element_type=jnp.float32)  105 us
  transfers between devices with their start and end apart: 15, of which 13 were waited for; matrix products, arithmetic and copies ran while one was open for 13% of the time, Pallas kernels for 0%

commit v1 on v0

v1 whole, which is shorter than its diff:
```python
from functools import partial

import jax
import jax.numpy as jnp
from jax import lax
from jax.experimental import pallas as pl
from jax.experimental.layout import Layout, with_layout_constraint
from jax.experimental.pallas import tpu as pltpu
from jax.sharding import PartitionSpec as P


HEADS = 25
HEAD = 64
PAIR = 2 * HEAD
BLOCK = 256

EPS = 1e-05
NEGATIVE = -1e30
SCALE = HEAD ** (-0.5)

bf16 = jnp.bfloat16
f32 = jnp.float32


def norm_forward(values, gain, offset):
    centre = values - jnp.mean(values, -1, keepdims=True)
    inverse = lax.rsqrt(jnp.mean(centre * centre, -1, keepdims=True) + EPS)
    unit = centre * inverse
    return (unit * gain + offset, unit, inverse)


def norm_backward(upstream, unit, inverse, gain):
    scaled = upstream * gain
    inner = (
        scaled
        - jnp.mean(scaled, -1, keepdims=True)
        - unit * jnp.mean(scaled * unit, -1, keepdims=True)
    )
    return (inner * inverse, jnp.sum(upstream * unit, 0), jnp.sum(upstream, 0))


def gelu_tanh(values):
    return jax.nn.gelu(values, approximate=True)


def dot_rows(left, right):
    return lax.dot_general(left, right, (((0,), (0,)), ((), ())), preferred_element_type=f32)


def dot_lanes(left, right):
    return lax.dot_general(left, right, (((1,), (1,)), ((), ())), preferred_element_type=f32)


def dot(left, right):
    return jnp.dot(left, right, preferred_element_type=f32)


def lane_mask(which):
    lanes = lax.broadcasted_iota(jnp.int32, (1, PAIR), 1)
    return (lanes // HEAD == which).astype(f32)


def masked_pair(block, scale):
    wide = block.astype(f32)
    return [(wide * (lane_mask(h) * scale)).astype(bf16) for h in range(2)]


def allowed_block(key_block, query_block, rows, start):
    keys = key_block * BLOCK + lax.broadcasted_iota(jnp.int32, (BLOCK, BLOCK), 0)
    places = (
        rows + query_block * BLOCK + lax.broadcasted_iota(jnp.int32, (BLOCK, BLOCK), 1)
    )
    return (keys >= start) & (keys <= places)


def forward_kernel(
    low_ref, live_ref, start_ref, q_ref, k_ref, v_ref, o_ref, ot_ref, log_ref, vtbuf
):
    rows = q_ref.shape[0]
    pair = pl.program_id(0)
    live = (pair < pl.num_programs(0) - 1) | (live_ref[0] > 0)

    @pl.when(jnp.logical_not(live))
    def _():
        o_ref[...] = jnp.zeros_like(o_ref)
        ot_ref[...] = jnp.zeros_like(ot_ref)
        log_ref[...] = jnp.zeros_like(log_ref)

    @pl.when(live)
    def _():
        vtbuf[...] = v_ref[...].astype(f32).T.astype(bf16)
        for qb in range(rows // BLOCK):
            span = slice(qb * BLOCK, (qb + 1) * BLOCK)
            queries = masked_pair(q_ref[span, :], SCALE)
            start = start_ref[:, span]

            def step(kb, carry):
                base = pl.multiple_of(kb * BLOCK, BLOCK)
                keys = k_ref[pl.ds(base, BLOCK), :]
                allowed = allowed_block(kb, qb, rows, start)
                out = []
                for h in range(2):
                    highest, summed, total = carry[3 * h : 3 * h + 3]
                    scores = jnp.where(allowed, dot_lanes(keys, queries[h]), NEGATIVE)
                    higher = jnp.maximum(highest, jnp.max(scores, 0, keepdims=True))
                    fade = jnp.exp(highest - higher)
                    expo = jnp.exp(scores - higher)
                    summed = summed * fade + jnp.sum(expo, 0, keepdims=True)
                    values = vtbuf[h * HEAD : (h + 1) * HEAD, pl.ds(base, BLOCK)]
                    total = total * fade + dot(values, expo.astype(bf16))
                    out += [higher, summed, total]
                return tuple(out)

            empty = (
                jnp.full((1, BLOCK), NEGATIVE, f32),
                jnp.zeros((1, BLOCK), f32),
                jnp.zeros((HEAD, BLOCK), f32),
            )
            done = lax.fori_loop(low_ref[qb], rows // BLOCK + qb + 1, step, empty + empty)
            for h in range(2):
                highest, summed, total = done[3 * h : 3 * h + 3]
                ot_ref[h * HEAD : (h + 1) * HEAD, span] = total / summed
                log_ref[0, h : h + 1, span] = highest + jnp.log(summed)
            o_ref[span, :] = ot_ref[:, span].T.astype(bf16)


def backward_kernel(
    low_ref,
    live_ref,
    start_ref,
    q_ref,
    k_ref,
    v_ref,
    g_ref,
    ot_ref,
    log_ref,
    dq_ref,
    dk_ref,
    dv_ref,
    ktbuf,
    dkbuf,
    dvbuf,
):
    rows = q_ref.shape[0]
    pair = pl.program_id(0)
    live = (pair < pl.num_programs(0) - 1) | (live_ref[0] > 0)
    dkbuf[...] = jnp.zeros_like(dkbuf)
    dvbuf[...] = jnp.zeros_like(dvbuf)

    @pl.when(jnp.logical_not(live))
    def _():
        dq_ref[...] = jnp.zeros_like(dq_ref)

    @pl.when(live)
    def _():
        ktbuf[...] = k_ref[...].astype(f32).T.astype(bf16)
        for qb in range(rows // BLOCK):
            span = slice(qb * BLOCK, (qb + 1) * BLOCK)
            queries = masked_pair(q_ref[span, :], SCALE)
            grads = masked_pair(g_ref[span, :], 1.0)
            start = start_ref[:, span]
            turned = g_ref[span, :].astype(f32).T * ot_ref[:, span]
            inner = [jnp.sum(turned[h * HEAD : (h + 1) * HEAD], 0, keepdims=True) for h in range(2)]
            log_total = [log_ref[0, h : h + 1, span] for h in range(2)]

            def step(kb, carry):
                base = pl.multiple_of(kb * BLOCK, BLOCK)
                here = pl.ds(base, BLOCK)
                keys, values = k_ref[here, :], v_ref[here, :]
                allowed = allowed_block(kb, qb, rows, start)
                out = []
                grad_keys, grad_values = dkbuf[here, :], dvbuf[here, :]
                for h in range(2):
                    scores = jnp.where(allowed, dot_lanes(keys, queries[h]), NEGATIVE)
                    probs = jnp.exp(scores - log_total[h])
                    grad_probs = dot_lanes(values, grads[h])
                    grad_scores = (probs * (grad_probs - inner[h])).astype(bf16)
                    grad_values += dot(probs.astype(bf16), grads[h])
                    grad_keys += dot(grad_scores, queries[h])
                    turned_keys = ktbuf[h * HEAD : (h + 1) * HEAD, here]
                    out.append(carry[h] + dot(turned_keys, grad_scores))
                dkbuf[here, :] = grad_keys
                dvbuf[here, :] = grad_values
                return tuple(out)

            empty = jnp.zeros((HEAD, BLOCK), f32)
            done = lax.fori_loop(low_ref[qb], rows // BLOCK + qb + 1, step, (empty, empty))
            dq_ref[span, :] = (jnp.concatenate(done, 0) * SCALE).T.astype(bf16)

    dk_ref[...] = dkbuf[...].astype(bf16)
    dv_ref[...] = dvbuf[...].astype(bf16)


def column_spec(rows):
    return pl.BlockSpec((rows, PAIR), lambda p: (0, p))


def attention_forward(low, live, start, queries, keys, values):
    rows, width = queries.shape
    pairs = width // PAIR
    smem = pl.BlockSpec(memory_space=pltpu.SMEM)
    return pl.pallas_call(
        forward_kernel,
        grid=(pairs,),
        in_specs=[
            smem,
            smem,
            pl.BlockSpec((1, rows), lambda p: (0, 0)),
            column_spec(rows),
            column_spec(2 * rows),
            column_spec(2 * rows),
        ],
        out_specs=[
            column_spec(rows),
            pl.BlockSpec((PAIR, rows), lambda p: (p, 0)),
            pl.BlockSpec((1, 2, rows), lambda p: (p, 0, 0)),
        ],
        out_shape=[
            jax.ShapeDtypeStruct((rows, pairs * PAIR), bf16),
            jax.ShapeDtypeStruct((pairs * PAIR, rows), f32),
            jax.ShapeDtypeStruct((pairs, 2, rows), f32),
        ],
        scratch_shapes=[pltpu.VMEM((PAIR, 2 * rows), bf16)],
        cost_estimate=pl.CostEstimate(
            flops=2 * 2 * rows * rows * pairs * PAIR,
            bytes_accessed=rows * pairs * PAIR * 16,
            transcendentals=rows * rows * pairs * 2,
        ),
        name="attention_forward",
    )(low, live, start, queries, keys, values)


def attention_backward(low, live, start, queries, keys, values, grad, turned, log_total):
    rows, width = queries.shape
    pairs = width // PAIR
    smem = pl.BlockSpec(memory_space=pltpu.SMEM)
    return pl.pallas_call(
        backward_kernel,
        grid=(pairs,),
        in_specs=[
            smem,
            smem,
            pl.BlockSpec((1, rows), lambda p: (0, 0)),
            column_spec(rows),
            column_spec(2 * rows),
            column_spec(2 * rows),
            column_spec(rows),
            pl.BlockSpec((PAIR, rows), lambda p: (p, 0)),
            pl.BlockSpec((1, 2, rows), lambda p: (p, 0, 0)),
        ],
        out_specs=[column_spec(rows)] + [column_spec(2 * rows)] * 2,
        out_shape=[jax.ShapeDtypeStruct((count, pairs * PAIR), bf16) for count in (rows, 2 * rows, 2 * rows)],
        scratch_shapes=[
            pltpu.VMEM((PAIR, 2 * rows), bf16),
            pltpu.VMEM((2 * rows, PAIR), f32),
            pltpu.VMEM((2 * rows, PAIR), f32),
        ],
        cost_estimate=pl.CostEstimate(
            flops=5 * 2 * rows * rows * pairs * PAIR,
            bytes_accessed=rows * pairs * PAIR * 24,
            transcendentals=rows * rows * pairs * 2,
        ),
        name="attention_backward",
    )(low, live, start, queries, keys, values, grad, turned, log_total)


def row_major(values):
    return with_layout_constraint(values, Layout(major_to_minor=tuple(range(values.ndim))))


def cut_rows(values):
    *rest, rows, columns = values.shape
    block = next((b for b in (200, 192) if rows % b == 0), rows)
    return values.reshape(*rest, rows // block, block, columns)


def moved(values, axis, pairs):
    return row_major(lax.ppermute(row_major(cut_rows(values)), axis, pairs)).reshape(values.shape)


def across(values, axis, step):
    size = lax.axis_size(axis)
    return moved(values, axis, [(i, i ^ step) for i in range(size)])


def tied(values, *others):
    return lax.optimization_barrier((values, *others))[0]


def place(buffer, piece, index):
    return lax.dynamic_update_slice(buffer, piece[None], (index,) + (0,) * piece.ndim)


def leave_kernel(o_ref):
    pass


def unfilled(shape, dtype):
    return pl.pallas_call(
        leave_kernel,
        out_specs=pl.BlockSpec(memory_space=pl.ANY),
        out_shape=jax.ShapeDtypeStruct(shape, dtype),
        name="unfilled",
    )()


def ring(own, axis):
    size = lax.axis_size(axis)
    held, out = own, []
    for _ in range(size - 1):
        held = moved(held, axis, [(i, (i + 1) % size) for i in range(size)])
        out.append(held)
    return out


def gather_halves(shard, parts):
    size, here = lax.axis_size("fsdp"), lax.axis_index("fsdp")
    side = lax.axis_index("ctx")
    rows, columns = shard.shape
    width = columns // parts
    halves = shard.reshape(2, rows // 2, columns)
    own = lax.dynamic_index_in_dim(halves, side, 0, False)
    if size > 4:
        mine = lax.all_gather(own, "fsdp", axis=0)
        theirs = across(mine, "ctx", 1)
        both = jnp.where(side == 0, jnp.stack([mine, theirs], 1), jnp.stack([theirs, mine], 1))
        both = both.reshape(size * rows, columns)
        return [both[:, i * width : (i + 1) * width] for i in range(parts)], [mine] * (size - 1)
    whole = [
        lax.dynamic_update_slice(
            unfilled((2 * size, rows // 2, width), shard.dtype),
            halves[:, :, i * width : (i + 1) * width],
            (2 * here, 0, 0),
        )
        for i in range(parts)
    ]
    pieces = ring(own, "fsdp")
    for back, piece in enumerate(pieces, 1):
        other = across(piece, "ctx", 1)
        at = 2 * ((here + size - back) % size)
        for i in range(parts):
            span = slice(i * width, (i + 1) * width)
            whole[i] = place(whole[i], piece[:, span], at + side)
            whole[i] = place(whole[i], other[:, span], at + 1 - side)
    return [part.reshape(size * rows, width) for part in whole], pieces


def gather_direct(values):
    size, here = lax.axis_size("fsdp"), lax.axis_index("fsdp")
    if size > 4:
        return lax.all_gather(values, "fsdp", axis=0)
    whole = place(jnp.zeros((size, *values.shape), values.dtype), values, here)
    for back in range(1, size):
        piece = lax.ppermute(values, "fsdp", [(i, (i + back) % size) for i in range(size)])
        whole = place(whole, piece, (here + size - back) % size)
    return whole


def gather_whole(shard, after=()):
    size, here = lax.axis_size("fsdp"), lax.axis_index("fsdp")
    rows, columns = shard.shape
    own = tied(shard, *after)
    if size > 4:
        return lax.all_gather(own, "fsdp", axis=0, tiled=True), [own] * (size - 1)
    whole = place(unfilled((size, rows, columns), shard.dtype), own, here)
    pieces = ring(own, "fsdp")
    for back, piece in enumerate(pieces, 1):
        whole = place(whole, piece, (here + size - back) % size)
    return whole.reshape(size * rows, columns), pieces


def gather_pair(own, after=()):
    mine = row_major(lax.all_gather(tied(own, *after), "fsdp", axis=0, tiled=True))
    theirs = across(mine, "ctx", 1)
    return mine, theirs


def from_tp(own):
    beside = across(own, "tp", 2)
    return [own, across(own, "tp", 1), beside, across(beside, "tp", 1)]


FOLD = (0, 2, 1, 3)


def scatter_tp(terms):
    rows = terms[0][0].shape[0]

    def product(span):
        return sum(dot_lanes(left[span], right) for left, right in terms)

    gone = across(row_major(product(slice(rows // 2, rows)).astype(bf16)), "tp", 1)
    keep = row_major(product(slice(0, rows // 2)))
    far = keep[rows // 4 :] + gone[rows // 4 :].astype(f32)
    come = across(far.astype(bf16), "tp", 2)
    return keep[: rows // 4] + gone[: rows // 4].astype(f32) + come.astype(f32)


def by_xor(entries, index):
    odd, far = index % 2 == 1, index // 2 == 1
    a = [jnp.where(odd, entries[j ^ 1], entries[j]) for j in range(4)]
    return [jnp.where(far, a[j ^ 2], a[j]) for j in range(4)]


def assemble_kernel(index_ref, a_ref, b_ref, c_ref, d_ref, o_ref):
    j = pl.program_id(0) ^ index_ref[0]
    for step, piece in enumerate((a_ref, b_ref, c_ref, d_ref)):

        @pl.when(j == step)
        def _():
            o_ref[...] = piece[...].astype(o_ref.dtype)


def natural(entries, index, dtype):
    rows, columns = entries[0].shape
    return pl.pallas_call(
        assemble_kernel,
        grid=(len(entries),),
        in_specs=[pl.BlockSpec(memory_space=pltpu.SMEM)]
        + [pl.BlockSpec((rows, columns), lambda j: (0, 0))] * len(entries),
        out_specs=pl.BlockSpec((rows, columns), lambda j: (j, 0)),
        out_shape=jax.ShapeDtypeStruct((len(entries) * rows, columns), dtype),
        cost_estimate=pl.CostEstimate(
            flops=0, bytes_accessed=4 * len(entries) * rows * columns, transcendentals=0
        ),
        name="assemble",
    )(index.reshape(1), *entries)


def picked(stacked, index):
    return jnp.concatenate(
        [lax.dynamic_index_in_dim(stacked, index ^ j, 0, False) for j in FOLD], 0
    )


def spread_fsdp(both):
    return row_major(lax.psum_scatter(row_major(both), "fsdp", scatter_dimension=0, tiled=True))


def ring_sum(parts):
    size, here = lax.axis_size("fsdp"), lax.axis_index("fsdp")
    if size > 4:
        return lax.psum_scatter(parts, "fsdp", scatter_dimension=1)
    own = lambda back: lax.dynamic_index_in_dim(parts, (here + size - back) % size, 1, False)
    held = own(1)
    for back in range(2, size + 1):
        come = moved(held.astype(bf16), "fsdp", [(i, (i + 1) % size) for i in range(size)])
        held = come.astype(f32) + own(back % size).astype(f32)
    return held.astype(bf16)


def finish_rows(terms):
    size = lax.axis_size("fsdp")
    count, rows, columns = terms.shape
    mine = ring_sum(terms.reshape(count, size, rows // size, columns))
    return (mine.astype(f32) + across(mine, "ctx", 1).astype(f32)).astype(bf16)


def join_kernel(step, index_ref, *refs):
    o_ref = refs[-1]
    pieces = refs[:-1]
    count = pieces[0].shape[0]
    me = index_ref[0]
    out = []
    for part in range(count):
        for s in range(len(pieces)):
            value = pieces[0][part].astype(f32)
            for j in range(1, len(pieces)):
                value = jnp.where(me ^ s == j, pieces[j][part].astype(f32), value)
            out.append(value if s == len(pieces) - 1 else value[:, :step])
    o_ref[...] = jnp.concatenate(out, 1)


def join_windows(pieces, index, step):
    count, rows, reach = pieces[0].shape
    width = count * (step * (len(pieces) - 1) + reach)
    tall = rows // 5 if rows % 40 == 0 else rows
    return pl.pallas_call(
        partial(join_kernel, step),
        grid=(rows // tall,),
        in_specs=[pl.BlockSpec(memory_space=pltpu.SMEM)]
        + [pl.BlockSpec((count, tall, reach), lambda r: (0, r, 0))] * len(pieces),
        out_specs=pl.BlockSpec((tall, width), lambda r: (r, 0)),
        out_shape=jax.ShapeDtypeStruct((rows, width), f32),
        cost_estimate=pl.CostEstimate(flops=0, bytes_accessed=6 * rows * width, transcendentals=0),
        name="join_windows",
    )(index.reshape(1), *pieces)


def scatter_vectors(vectors, extra):
    size, here = lax.axis_size("fsdp"), lax.axis_index("fsdp")
    total = jnp.concatenate([vectors, extra[None]], 0)
    total = total + across(total, "ctx", 1)
    vectors, extra = total[:-1], total[-1:]
    vectors = vectors + across(vectors, "tp", 1)
    vectors = vectors + across(vectors, "tp", 2)
    total = jnp.concatenate([vectors, extra], 0)
    if size > 4:
        return lax.psum_scatter(total, "fsdp", scatter_dimension=1, tiled=True)
    count, width = total.shape
    parts = total.reshape(count, size, width // size).transpose(1, 0, 2)
    out = lax.dynamic_index_in_dim(parts, here, 0, False)
    for back in range(1, size):
        piece = lax.dynamic_index_in_dim(parts, (here + back) % size, 0, False)
        out = out + lax.ppermute(piece, "fsdp", [(i, (i + back) % size) for i in range(size)])
    return out


def on_device(
    tokens,
    segments,
    first_gain,
    first_bias,
    input_weight,
    query_bias,
    value_bias,
    output_weight,
    output_bias,
    second_gain,
    second_bias,
    up_weight,
    up_bias,
    down_weight,
    down_bias,
    cotangent,
):
    rows, width = tokens.shape
    members, me = lax.axis_size("tp"), lax.axis_index("tp")
    side = lax.axis_index("ctx")
    few = rows // members
    step = HEADS // members * HEAD
    reach = width - step * (members - 1)
    window = -(-reach // PAIR) * PAIR
    margin = window - reach

    def window_in(part):
        return jnp.pad(
            lax.dynamic_slice_in_dim(input_weight, part * width + me * step, reach, 1), ((0, 0), (0, margin))
        )

    hidden = up_weight.shape[1]
    cut = hidden // 2 // 128 * 128
    half = hidden - cut
    once = jnp.arange(half) < cut

    def halves(low, high):
        low = jnp.where(once.reshape((-1,) if low.ndim == 1 else (1, -1)), low, 0).astype(low.dtype)
        return jnp.where(side == 0, low, high), jnp.where(side == 0, high, low)

    def whole_of(mine, theirs):
        low, high = jnp.where(side == 0, mine, theirs), jnp.where(side == 0, theirs, mine)
        return jnp.concatenate([low[..., :cut], high], -1)

    windows_in = jnp.concatenate([window_in(part) for part in range(3)], 1)
    (weight_q, weight_k, weight_v), pieces_in = gather_halves(windows_in, 3)
    weight_out, _ = gather_whole(
        lax.dynamic_slice_in_dim(output_weight, me * step, reach, 1), (pieces_in[1],)
    )
    up_mine, up_theirs = gather_pair(halves(up_weight[:, :half], up_weight[:, cut:])[0], (pieces_in[0],))
    down_mine, down_theirs = gather_pair(halves(down_weight[:half].T, down_weight[cut:].T)[0], (pieces_in[0],))
    windows_out = from_tp(weight_out)

    small = [first_gain, first_bias, query_bias, value_bias, output_bias, second_gain, second_bias, up_bias, down_bias]
    small = jnp.stack(tied(small, windows_in))
    small = gather_direct(small).transpose(1, 0, 2).reshape(small.shape[0], width)
    gain_one, bias_one, bias_query, bias_value, bias_out, gain_two, bias_two, bias_up, bias_down = small.astype(f32)
    bias_mine, bias_theirs = halves(bias_up[:half], bias_up[cut:])

    def window_of(vector):
        return lax.dynamic_slice_in_dim(jnp.pad(vector, (0, margin)), me * step, window, 0)

    segments = tied(segments, pieces_in[0])
    labels = lax.dynamic_slice_in_dim(segments, side * rows, rows)
    start = jnp.sum((segments[:, None] < labels[None, :]).astype(jnp.int32), 0) + rows * (1 - side)
    low = start[::BLOCK] // BLOCK
    live = (me == members - 1).astype(jnp.int32).reshape(1)
    start = start.reshape(1, rows)

    earlier = lax.ppermute(tokens, "ctx", [(0, 1)])
    normed_one, normed_early = (
        norm_forward(part.astype(f32), gain_one, bias_one)[0].astype(bf16) for part in (tokens, earlier)
    )
    normed_all = jnp.concatenate([normed_early, normed_one], 0)
    keys = dot(normed_all, weight_k).astype(bf16)
    values = (dot(normed_all, weight_v) + window_of(bias_value)).astype(bf16)
    queries = (dot(normed_one, weight_q) + window_of(bias_query)).astype(bf16)
    upstream = picked(tied(cotangent, pieces_in[1]).reshape(members, few, width), me)
    queries, upstream = lax.optimization_barrier((queries, upstream))
    mixed, turned, log_total = attention_forward(low, live, start, queries, keys, values)

    def to_tp(pieces):
        come = [pieces[0]] + [across(pieces[j], "tp", j) for j in range(1, members)]
        return by_xor(come, me)

    blocks = mixed[:, :reach].reshape(members, few, reach)
    come = to_tp([lax.dynamic_index_in_dim(blocks, me ^ j, 0, False) for j in range(members)])
    mixture = jnp.concatenate([come[j][:, :step] for j in range(members - 1)] + [come[members - 1]], 1)

    own_tokens = lax.dynamic_slice_in_dim(tokens, me * few, few).astype(f32)
    branch = by_xor([dot(mixture, part) for part in windows_out], me)
    branch = jnp.concatenate([branch[j][:, :step] for j in range(members - 1)] + [branch[members - 1]], 1)
    middle = own_tokens + branch + bias_out
    normed, unit_two, inverse_two = norm_forward(middle, gain_two, bias_two)
    normed_two = from_tp(normed.astype(bf16))
    normed_two = jnp.concatenate([normed_two[j] for j in FOLD], 0)

    def hidden_half(weight_up, weight_down, bias):
        grad_activated = dot(upstream, weight_down)
        preact = dot(normed_two, weight_up) + bias
        activated, gelu_pull = jax.vjp(gelu_tanh, preact)
        return activated.astype(bf16), gelu_pull(grad_activated)[0].astype(bf16)

    act_mine, pre_mine = hidden_half(up_mine, down_mine, bias_mine)
    act_theirs, pre_theirs = hidden_half(up_theirs, down_theirs, bias_theirs)
    grad_normed = scatter_tp([(pre_mine, up_mine), (pre_theirs, up_theirs)])
    down_gone = dot_rows(upstream, act_theirs).astype(bf16)
    up_gone = dot_rows(normed_two, pre_theirs).astype(bf16)
    up_kept = dot_rows(normed_two, pre_mine).astype(bf16)
    grad_normed = tied(grad_normed, down_gone, up_gone, up_kept)
    own_upstream = upstream[:few].astype(f32)
    grad_two, grad_gain_two, grad_bias_two = norm_backward(grad_normed, unit_two, inverse_two, gain_two)
    grad_middle = own_upstream + grad_two
    grad_branch = grad_middle.astype(bf16)

    inner = jnp.arange(reach) < step

    def columns_for(index):
        return lax.dynamic_slice_in_dim(grad_branch, index * step, reach, 1)

    branch_windows = [columns_for(me ^ j) for j in range(members)]
    grad_mixture = jnp.zeros((few, width), f32)
    for j in range(members):
        once = jnp.where(inner | ((me ^ j) == members - 1), branch_windows[j], 0).astype(bf16)
        grad_mixture += dot_lanes(once, windows_out[j])
    grad_mixture = jnp.pad(grad_mixture.astype(bf16), ((0, 0), (0, margin)))
    come = to_tp([lax.dynamic_slice_in_dim(grad_mixture, (me ^ j) * step, window, 1) for j in range(members)])
    grad_mixed = jnp.concatenate(come, 0)

    up_gone, up_kept = spread_fsdp(up_gone), spread_fsdp(up_kept)
    other_gone, other_kept = across(up_gone, "ctx", 1), across(up_kept, "ctx", 1)
    down_kept = dot_rows(upstream, act_mine) + across(down_gone, "ctx", 1).astype(f32)
    down_kept = down_kept.astype(bf16)
    down_sum = spread_fsdp(down_kept)
    shard_down = whole_of(down_sum, across(down_sum, "ctx", 1)).astype(f32).T
    shard_up = whole_of(
        up_kept.astype(f32) + other_gone.astype(f32),
        up_gone.astype(f32) + other_kept.astype(f32),
    )
    late_mine, late_theirs = tied((act_mine, act_theirs), grad_mixture)
    result = scatter_tp([(late_mine, down_mine), (late_theirs, down_theirs)])
    result = (middle + result + bias_down).astype(bf16)
    result = natural(from_tp(result), me, bf16)

    def branch_product(j):
        return dot_rows(mixture, branch_windows[j])

    come = across(jnp.stack([branch_product(1), branch_product(3)]).astype(bf16), "tp", 1).astype(f32)
    near = branch_product(0) + come[0]
    far = (branch_product(2) + come[1]).astype(bf16)
    near = (near + across(far, "tp", 2).astype(f32)).astype(bf16)
    shard_out = join_windows(from_tp(finish_rows(near[None])), me, step)

    grad_mixed = tied(grad_mixed, down_kept)
    grad_q, grad_k, grad_v = attention_backward(
        low, live, start, queries, keys, values, grad_mixed, turned, log_total
    )
    grad_in = jnp.stack(
        [
            row_major(dot_rows(left, grad[:, :reach]).astype(bf16).reshape(4, -1, reach)).reshape(width, reach)
            for left, grad in ((normed_one, grad_q), (normed_all, grad_k), (normed_all, grad_v))
        ]
    )
    shard_in = join_windows(from_tp(finish_rows(grad_in)), me, step)

    def turned_rows(grad):
        return picked(grad.reshape(members, few, window), me)

    grad_early = scatter_tp(
        [(turned_rows(grad[:rows]), weight) for grad, weight in ((grad_k, weight_k), (grad_v, weight_v))]
    )
    grad_normed = scatter_tp(
        [
            (turned_rows(grad), weight)
            for grad, weight in ((grad_q, weight_q), (grad_k[rows:], weight_k), (grad_v[rows:], weight_v))
        ]
    )
    grad_normed += moved(grad_early.astype(bf16), "ctx", [(1, 0)]).astype(f32)
    _, unit_one, inverse_one = norm_forward(own_tokens, gain_one, bias_one)
    grad_one, grad_gain_one, grad_bias_one = norm_backward(grad_normed, unit_one, inverse_one, gain_one)
    gradient = (grad_middle + grad_one).astype(bf16)
    gradient = natural(from_tp(gradient), me, bf16)

    def spread(columns):
        wide = jnp.zeros((width + margin,), f32)
        columns = jnp.where(jnp.arange(window) < jnp.where(me == members - 1, reach, step), columns, 0.0)
        return lax.dynamic_update_slice_in_dim(wide, columns, me * step, 0)[:width]

    vectors = jnp.stack(
        [
            grad_gain_one,
            grad_bias_one,
            spread(jnp.sum(grad_q.astype(f32), 0)),
            spread(jnp.sum(grad_v.astype(f32), 0)),
            jnp.sum(grad_branch.astype(f32), 0),
            grad_gain_two,
            grad_bias_two,
            jnp.sum(own_upstream, 0),
        ]
    )
    grad_bias_up = whole_of(jnp.sum(pre_mine.astype(f32), 0), jnp.sum(pre_theirs.astype(f32), 0))
    vectors = scatter_vectors(vectors, grad_bias_up)
    return (
        result,
        gradient,
        vectors[0],
        vectors[1],
        shard_in,
        vectors[2],
        vectors[3],
        shard_out,
        vectors[4],
        vectors[5],
        vectors[6],
        shard_up,
        vectors[8],
        shard_down,
        vectors[7],
    )


def solution(mesh):
    return jax.shard_map(
        on_device,
        mesh=mesh,
        in_specs=(
            P(("fsdp", "ctx"), None),
            P("fsdp"),
            P("fsdp"),
            P("fsdp"),
            P("fsdp", None),
            P("fsdp"),
            P("fsdp"),
            P("fsdp", None),
            P("fsdp"),
            P("fsdp"),
            P("fsdp"),
            P("fsdp", "tp"),
            P(("tp", "fsdp")),
            P("tp", "fsdp"),
            P("fsdp"),
            P(("fsdp", "ctx"), None),
        ),
        out_specs=(
            P(("fsdp", "ctx"), None),
            P(("fsdp", "ctx"), None),
            P("fsdp"),
            P("fsdp"),
            P("fsdp", None),
            P("fsdp"),
            P("fsdp"),
            P("fsdp", None),
            P("fsdp"),
            P("fsdp"),
            P("fsdp"),
            P("fsdp", "tp"),
            P(("tp", "fsdp")),
            P("tp", "fsdp"),
            P("fsdp"),
        ),
        check_vma=False,
    )
```

time: 2820 us -> 836 us (0.30)
  waiting for transfers between devices: 1930 us -> 297 us
  matrix products: 613 us -> 132 us
  starting transfers between devices: 1.4 us -> 165 us
  blocking collectives: 66.4 us -> 0 us
  Pallas kernels: 0 us -> 50.3 us
  local copies, waits for them, and re-layouts: 122 us -> 76.8 us
    reduce_scatter x6 -> x3, waiting for transfers between devices: 1130 us -> 0.01 us  [spread_fsdp(): lax.psum_scatter(row_major(both), 'fsdp', scatter_dimension=0, tiled=True)]
    dot_general x187 -> x44, matrix products: 613 us -> 132 us  [the longest x22 57.4 us: dot_lanes(): lax.dot_general(left, right, (((1,), (1,)), ((), ())), preferred_element_...]
    psum x3 -> x0, waiting for transfers between devices: 436 us -> none  [the longest x1 296 us: on_device(): lax.psum((shards[0], shards[1], shards[2], shards[3], shards[4], shards[5...]
    all_gather x6 -> x2, waiting for transfers between devices: 355 us -> 0.01 us  [gather_pair(): lax.all_gather(tied(own, *after), 'fsdp', axis=0, tiled=True)]
    ppermute x0 -> x68, waiting for transfers between devices: none -> 297 us  [the longest x61 297 us: moved(): lax.ppermute(row_major(cut_rows(values)), axis, pairs)]
    ppermute x0 -> x68, starting transfers between devices: none -> 165 us  [the longest x61 154 us: moved(): lax.ppermute(row_major(cut_rows(values)), axis, pairs)]
    unnamed x2 -> x0, blocking collectives: 56.7 us -> none
    while x50 -> x0, local copies, waits for them, and re-layouts: 52.8 us -> none
  transfers between devices with their start and end apart: 15 -> 73, of which waited for: 13 -> 25; matrix products, arithmetic and copies ran while one was open for 13% -> 35% of each run, Pallas kernels for 0% -> 5%
where the time goes in v1:
time: 836 us; the launch traced here: 828 us
  waiting for transfers between devices  297 us (36%)
  starting transfers between devices  165 us (20%)
  matrix products  132 us (16%)
  other arithmetic  89.6 us (11%)
  local copies, waits for them, and re-layouts  76.8 us (9%)
  Pallas kernels  50.3 us (6%)
  between operations  16.2 us (2%)
    ppermute x61, waiting for transfers between devices, moved(): lax.ppermute(row_major(cut_rows(values)), axis, pairs)  297 us
    ppermute x61, starting transfers between devices, moved(): lax.ppermute(row_major(cut_rows(values)), axis, pairs)  154 us
    dot_general x22, matrix products, dot_lanes(): lax.dot_general(left, right, (((1,), (1,)), ((), ())), preferred_element_...  57.4 us
    dot_general x11, matrix products, dot(): return jnp.dot(left, right, preferred_element_type=f32)  39.9 us
    dot_general x11, matrix products, dot_rows(): lax.dot_general(left, right, (((0,), (0,)), ((), ())), preferred_element_...  35.1 us
    unnamed x212, local copies, waits for them, and re-layouts  18.4 us
  transfers between devices with their start and end apart: 73, of which 25 were waited for; matrix products, arithmetic and copies ran while one was open for 35% of the time, Pallas kernels for 5%

profile of v1, /device:TPU:0, one launch (start us, length us, event | category | flops | bytes accessed | tf_op | source)
XLA Modules:
  0.0 827.7 jit_solution(11044507331537332760)
XLA Ops:
  15.5 15.1 %collective-permute-done = bf16[1,200,1536]{2,1,0:T(8,128)(2,1)S(1)} collective-permute-done((bf16[1,200,1536]{2,1,0:T(8,128)(2,1)}, bf16[1,200,1536]{2,1,0:T(8,128)(2,1)S(1)}, u32[]{:S(2)}, u32[]{:S(2)}) %collective-permute-start) | collective-permute-done | bytes 614432 | tf_op jit(solution)/shard_map/ppermute | solution.py:278
  34.8 4.8 collective-permute-start.9
  52.3 27.6 %collective-permute-done.5 = bf16[1,200,1536]{2,1,0:T(8,128)(2,1)} collective-permute-done((bf16[1,200,1536]{2,1,0:T(8,128)(2,1)S(1)}, bf16[1,200,1536]{2,1,0:T(8,128)(2,1)}, u32[]{:S(2)}, u32[]{:S(2)}) %collective-permute-start.5) | collective-permute-done | bytes 614432 | tf_op jit(solution)/shard_map/ppermute | solution.py:278
  79.9 4.4 copy.85
  84.3 11.6 %collective-permute-start.13 = (bf16[2,200,448]{2,1,0:T(8,128)(2,1)S(1)}, bf16[2,200,448]{2,1,0:T(8,128)(2,1)S(1)}, u32[]{:S(2)}, u32[]{:S(2)}) collective-permute-start(bf16[2,200,448]{2,1,0:T(8,128)(2,1)S(1)} %bitcast.495), channel_id=1, source_target_pairs={{0,8},{8,16},{16,24},{24,0},{1,9},{9,17},{17,25},{25,1},{2,10},{10... | collective-permute-start | bytes 1075208 | tf_op jit(solution)/shard_map/ppermute | solution.py:278
  99.3 6.0 collective-permute-done.4
  113.0 14.0 %collective-permute-done.7 = bf16[1,200,1536]{2,1,0:T(8,128)(2,1)S(1)} collective-permute-done((bf16[1,200,1536]{2,1,0:T(8,128)(2,1)}, bf16[1,200,1536]{2,1,0:T(8,128)(2,1)S(1)}, u32[]{:S(2)}, u32[]{:S(2)}) %collective-permute-start.7) | collective-permute-done | bytes 614432 | tf_op jit(solution)/shard_map/ppermute | solution.py:278
  128.2 15.6 %collective-permute-done.14 = bf16[2,200,448]{2,1,0:T(8,128)(2,1)S(1)} collective-permute-done((bf16[2,200,448]{2,1,0:T(8,128)(2,1)S(1)}, bf16[2,200,448]{2,1,0:T(8,128)(2,1)S(1)}, u32[]{:S(2)}, u32[]{:S(2)}) %collective-permute-start.14) | collective-permute-done | bytes 358432 | tf_op jit(solution)/shard_map/ppermute | solution.py:278
  143.7 7.4 collective-permute-start.15
  152.0 20.6 %collective-permute-done.15 = bf16[2,200,448]{2,1,0:T(8,128)(2,1)S(1)} collective-permute-done((bf16[2,200,448]{2,1,0:T(8,128)(2,1)S(1)}, bf16[2,200,448]{2,1,0:T(8,128)(2,1)S(1)}, u32[]{:S(2)}, u32[]{:S(2)}) %collective-permute-start.15) | collective-permute-done | bytes 358432 | tf_op jit(solution)/shard_map/ppermute | solution.py:278
  191.4 17.3 %collective-permute-done.16 = bf16[8,200,448]{2,1,0:T(8,128)(2,1)} collective-permute-done((bf16[8,200,448]{2,1,0:T(8,128)(2,1)}, bf16[8,200,448]{2,1,0:T(8,128)(2,1)}, u32[]{:S(2)}, u32[]{:S(2)}) %collective-permute-start.16) | collective-permute-done | bytes 1433632 | tf_op jit(solution)/shard_map/ppermute | solution.py:278
  211.2 15.1 %attention_forward.1 = (bf16[768,512]{1,0:T(8,128)(2,1)}, f32[512,768]{1,0:T(8,128)}, f32[4,2,768]{2,1,0:T(2,128)}) custom-call(s32[3]{0:T(128)} %and_select_fusion.low_ref, s32[1]{0:T(128)} %bitcast.3.live_ref, s32[1,768]{1,0:T(1,128)} %add.616.start_ref, bf16[768,512]{1,0:T(8,128)(2,1)} %add_convert_fusion.3.q_ref, ...), custom_call_target="tpu_custom_call" | custom-call | flops 1207959552 | bytes 6291456 | tf_op jit(solution)/shard_map/attention_forward/pallas_call | solution.py:202
  227.5 5.5 collective-permute-start.10
  247.2 5.7 collective-permute-start.22
  263.9 11.3 %collective-permute-done.19 = bf16[1,192,1600]{2,1,0:T(8,128)(2,1)S(1)} collective-permute-done((bf16[1,192,1600]{2,1,0:T(8,128)(2,1)S(1)}, bf16[1,192,1600]{2,1,0:T(8,128)(2,1)S(1)}, u32[]{:S(2)}, u32[]{:S(2)}) %collective-permute-start.19) | collective-permute-done | bytes 614432 | tf_op jit(solution)/shard_map/ppermute | solution.py:278
  277.3 5.6 convert_reduce_fusion.5
  283.9 4.7 convolution_convert_fusion
  288.7 5.3 fusion.87
  295.7 81.2 %collective-permute-done.23 = bf16[8,200,832]{2,1,0:T(8,128)(2,1)} collective-permute-done((bf16[8,200,832]{2,1,0:T(8,128)(2,1)}, bf16[8,200,832]{2,1,0:T(8,128)(2,1)}, u32[]{:S(2)}, u32[]{:S(2)}) %collective-permute-start.23) | collective-permute-done | bytes 2662432 | tf_op jit(solution)/shard_map/ppermute | solution.py:278
  376.9 4.7 fusion.221
  381.6 6.4 convert_reduce_fusion.4
  388.1 5.5 fusion.15
  395.5 4.6 fusion.16
  404.5 5.3 copy.88
  415.2 5.1 convolution_add_fusion.10
  420.3 5.1 convolution_add_fusion.8
  425.5 4.4 convolution_convert_fusion.1
  436.7 13.2 %collective-permute-done.25 = bf16[1,192,1600]{2,1,0:T(8,128)(2,1)} collective-permute-done((bf16[1,192,1600]{2,1,0:T(8,128)(2,1)}, bf16[1,192,1600]{2,1,0:T(8,128)(2,1)}, u32[]{:S(2)}, u32[]{:S(2)}) %collective-permute-start.25) | collective-permute-done | bytes 614432 | tf_op jit(solution)/shard_map/ppermute | solution.py:278
  452.0 10.2 %collective-permute-done.27 = bf16[1,192,1600]{2,1,0:T(8,128)(2,1)S(1)} collective-permute-done((bf16[1,192,1600]{2,1,0:T(8,128)(2,1)S(1)}, bf16[1,192,1600]{2,1,0:T(8,128)(2,1)S(1)}, u32[]{:S(2)}, u32[]{:S(2)}) %collective-permute-start.27) | collective-permute-done | bytes 614432 | tf_op jit(solution)/shard_map/ppermute | solution.py:278
  498.9 6.3 fusion.4
  505.2 15.0 %attention_backward.1 = (bf16[768,512]{1,0:T(8,128)(2,1)}, bf16[1536,512]{1,0:T(8,128)(2,1)}, bf16[1536,512]{1,0:T(8,128)(2,1)}) custom-call(s32[3]{0:T(128)} %and_select_fusion.low_ref, s32[1]{0:T(128)} %bitcast.3.live_ref, s32[1,768]{1,0:T(1,128)} %add.616.start_ref, bf16[768,512]{1,0:T(8,128)(2,1)} %add_convert_fusion.3.q_ref, ...), custom_call_target="tpu_custom_call" | custom-call | flops 3019898880 | bytes 9437184 | tf_op jit(solution)/shard_map/attention_backward/pallas_call | solution.py:237
  539.4 13.8 %collective-permute-start.49 = (bf16[3,2,200,448]{3,2,1,0:T(8,128)(2,1)}, bf16[3,2,200,448]{3,2,1,0:T(8,128)(2,1)}, u32[]{:S(2)}, u32[]{:S(2)}) collective-permute-start(bf16[3,2,200,448]{3,2,1,0:T(8,128)(2,1)} %bitcast.141), channel_id=1, source_target_pairs={{0,8},{8,16},{16,24},{24,0},{1,9},{9,17},{17,25},{25,1},{2,10},{10... | collective-permute-start | bytes 3225608 | tf_op jit(solution)/shard_map/ppermute | solution.py:278
  573.8 4.6 copy.95
  579.9 5.5 collective-permute-start.38
  589.3 10.3 %collective-permute-start.50 = (bf16[3,2,200,448]{3,2,1,0:T(8,128)(2,1)}, bf16[3,2,200,448]{3,2,1,0:T(8,128)(2,1)}, u32[]{:S(2)}, u32[]{:S(2)}) collective-permute-start(bf16[3,2,200,448]{3,2,1,0:T(8,128)(2,1)} %fusion.36), channel_id=1, source_target_pairs={{0,8},{8,16},{16,24},{24,0},{1,9},{9,17},{17,25},{25,1},{2,10},{10... | collective-permute-start | bytes 3225608 | tf_op jit(solution)/shard_map/ppermute | solution.py:278
  600.9 11.2 %collective-permute-start.36 = (bf16[1,192,1600]{2,1,0:T(8,128)(2,1)S(1)}, bf16[1,192,1600]{2,1,0:T(8,128)(2,1)}, u32[]{:S(2)}, u32[]{:S(2)}) collective-permute-start(bf16[1,192,1600]{2,1,0:T(8,128)(2,1)S(1)} %fusion.80), channel_id=1, source_target_pairs={{0,2},{1,3},{2,0},{3,1},{4,6},{5,7},{6,4},{7,5},{8,10},{9,11},{10,... | collective-permute-start | bytes 1843208 | tf_op jit(solution)/shard_map/ppermute | solution.py:278
  612.1 29.9 %collective-permute-start.66 = (bf16[2,200,832]{2,1,0:T(8,128)(2,1)}, bf16[2,200,832]{2,1,0:T(8,128)(2,1)}, u32[]{:S(2)}, u32[]{:S(2)}) collective-permute-start(bf16[2,200,832]{2,1,0:T(8,128)(2,1)} %bitcast.498), channel_id=1, source_target_pairs={{0,4},{4,0},{1,5},{5,1},{2,6},{6,2},{3,7},{7,3},{8,12},{12,8},{9,1... | collective-permute-start | bytes 1996808 | tf_op jit(solution)/shard_map/ppermute | solution.py:278
  653.2 4.8 copy.92
  676.6 5.5 collective-permute-start.41
  690.1 4.6 copy.93
  694.6 5.1 add_convert_fusion
  707.3 7.9 collective-permute-done.58
  727.8 9.1 %collective-permute-start.65 = (bf16[2,200,832]{2,1,0:T(8,128)(2,1)}, bf16[2,200,832]{2,1,0:T(8,128)(2,1)S(1)}, u32[]{:S(2)}, u32[]{:S(2)}) collective-permute-start(bf16[2,200,832]{2,1,0:T(8,128)(2,1)} %bitcast.499), channel_id=1, source_target_pairs={{0,4},{4,0},{1,5},{5,1},{2,6},{6,2},{3,7},{7,3},{8,12},{12,8},{9,1... | collective-permute-start | bytes 1996808 | tf_op jit(solution)/shard_map/ppermute | solution.py:278
  739.1 8.8 %collective-permute-done.60 = bf16[1,2,200,448]{3,2,1,0:T(8,128)(2,1)S(1)} collective-permute-done((bf16[1,2,200,448]{3,2,1,0:T(8,128)(2,1)}, bf16[1,2,200,448]{3,2,1,0:T(8,128)(2,1)S(1)}, u32[]{:S(2)}, u32[]{:S(2)}) %collective-permute-start.60) | collective-permute-done | bytes 358432 | tf_op jit(solution)/shard_map/ppermute | solution.py:278
  756.8 14.0 %collective-permute-done.52 = bf16[3,2,200,448]{3,2,1,0:T(8,128)(2,1)S(1)} collective-permute-done((bf16[3,2,200,448]{3,2,1,0:T(8,128)(2,1)}, bf16[3,2,200,448]{3,2,1,0:T(8,128)(2,1)S(1)}, u32[]{:S(2)}, u32[]{:S(2)}) %collective-permute-start.52) | collective-permute-done | bytes 1075232 | tf_op jit(solution)/shard_map/ppermute | solution.py:278
  793.7 4.5 collective-permute-done.63
  803.7 4.8 join_windows.3
  812.5 8.2 join_windows.2
  (539 shorter events, 294.5 us)
Async XLA Ops:
  7.2 240.0 %all-gather.3.cloned.1.call-start = ((), (), s32[]{:S(2)}) async-start(), calls=%async_computation.3 | async-start | bytes 3584000 | tf_op jit(solution)/shard_map/all_gather | solution.py:373
  30.6 222.3 %all-gather.5.cloned.1.call-start = ((), (), s32[]{:S(2)}) async-start(), calls=%async_computation.4 | async-start | bytes 3584000 | tf_op jit(solution)/shard_map/all_gather | solution.py:373
  34.8 140.0 %collective-permute-start.9 = (bf16[768,1600]{0,1:T(8,128)(2,1)}, bf16[768,1600]{0,1:T(8,128)(2,1)}, u32[]{:S(2)}, u32[]{:S(2)}) collective-permute-start(bf16[768,1600]{0,1:T(8,128)(2,1)} %param.16), channel_id=1, source_target_pairs={{0,4},{1,5},{2,6},{3,7},{8,12},{9,13},{10,14},{11,15},{16,20},{17,... | collective-permute-start | bytes 7372808 | tf_op jit(solution)/shard_map/ppermute | solution.py:579
  49.0 31.0 %collective-permute-start.5 = (bf16[1,200,1536]{2,1,0:T(8,128)(2,1)S(1)}, bf16[1,200,1536]{2,1,0:T(8,128)(2,1)}, u32[]{:S(2)}, u32[]{:S(2)}) collective-permute-start(bf16[1,200,1536]{2,1,0:T(8,128)(2,1)S(1)} %copy-done.60), channel_id=1, source_target_pairs={{0,8},{8,16},{16,24},{24,0},{1,9},{9,17},{17,25},{25,1},{2,10},{10... | collective-permute-start | bytes 1843208 | tf_op jit(solution)/shard_map/ppermute | solution.py:278
  50.3 55.0 %collective-permute-start.4 = (bf16[1,200,1536]{2,1,0:T(8,128)(2,1)S(1)}, bf16[1,200,1536]{2,1,0:T(8,128)(2,1)S(1)}, u32[]{:S(2)}, u32[]{:S(2)}) collective-permute-start(bf16[1,200,1536]{2,1,0:T(8,128)(2,1)S(1)} %copy-done.60), channel_id=1, source_target_pairs={{0,4},{4,0},{1,5},{5,1},{2,6},{6,2},{3,7},{7,3},{8,12},{12,8},{9,1... | collective-permute-start | bytes 1843208 | tf_op jit(solution)/shard_map/ppermute | solution.py:278
  51.4 560.7 %reduce-scatter.4.cloned.1.call-start = ((), (), s32[]{:S(2)}) async-start(), calls=%async_computation.5 | async-start | bytes 3584000 | tf_op jit(solution)/shard_map/reduce_scatter | solution.py:437
  84.3 27.3 %collective-permute-start.13 = (bf16[2,200,448]{2,1,0:T(8,128)(2,1)S(1)}, bf16[2,200,448]{2,1,0:T(8,128)(2,1)S(1)}, u32[]{:S(2)}, u32[]{:S(2)}) collective-permute-start(bf16[2,200,448]{2,1,0:T(8,128)(2,1)S(1)} %bitcast.495), channel_id=1, source_target_pairs={{0,8},{8,16},{16,24},{24,0},{1,9},{9,17},{17,25},{25,1},{2,10},{10... | collective-permute-start | bytes 1075208 | tf_op jit(solution)/shard_map/ppermute | solution.py:278
  95.9 32.2 %collective-permute-start.6 = (bf16[1,200,1536]{2,1,0:T(8,128)(2,1)}, bf16[1,200,1536]{2,1,0:T(8,128)(2,1)S(1)}, u32[]{:S(2)}, u32[]{:S(2)}) collective-permute-start(bf16[1,200,1536]{2,1,0:T(8,128)(2,1)} %collective-permute-done.5), channel_id=1, source_target_pairs={{0,4},{4,0},{1,5},{5,1},{2,6},{6,2},{3,7},{7,3},{8,12},{12,8},{9,1... | collective-permute-start | bytes 1843208 | tf_op jit(solution)/shard_map/ppermute | solution.py:278
  95.9 31.0 %collective-permute-start.7 = (bf16[1,200,1536]{2,1,0:T(8,128)(2,1)}, bf16[1,200,1536]{2,1,0:T(8,128)(2,1)S(1)}, u32[]{:S(2)}, u32[]{:S(2)}) collective-permute-start(bf16[1,200,1536]{2,1,0:T(8,128)(2,1)} %collective-permute-done.5), channel_id=1, source_target_pairs={{0,8},{8,16},{16,24},{24,0},{1,9},{9,17},{17,25},{25,1},{2,10},{10... | collective-permute-start | bytes 1843208 | tf_op jit(solution)/shard_map/ppermute | solution.py:278
  111.6 32.1 %collective-permute-start.14 = (bf16[2,200,448]{2,1,0:T(8,128)(2,1)S(1)}, bf16[2,200,448]{2,1,0:T(8,128)(2,1)S(1)}, u32[]{:S(2)}, u32[]{:S(2)}) collective-permute-start(bf16[2,200,448]{2,1,0:T(8,128)(2,1)S(1)} %collective-permute-done.13), channel_id=1, source_target_pairs={{0,8},{8,16},{16,24},{24,0},{1,9},{9,17},{17,25},{25,1},{2,10},{10... | collective-permute-start | bytes 1075208 | tf_op jit(solution)/shard_map/ppermute | solution.py:278
  126.9 55.9 %collective-permute-start.8 = (bf16[1,200,1536]{2,1,0:T(8,128)(2,1)S(1)}, bf16[1,200,1536]{2,1,0:T(8,128)(2,1)S(1)}, u32[]{:S(2)}, u32[]{:S(2)}) collective-permute-start(bf16[1,200,1536]{2,1,0:T(8,128)(2,1)S(1)} %collective-permute-done.7), channel_id=1, source_target_pairs={{0,4},{4,0},{1,5},{5,1},{2,6},{6,2},{3,7},{7,3},{8,12},{12,8},{9,1... | collective-permute-start | bytes 1843208 | tf_op jit(solution)/shard_map/ppermute | solution.py:278
  143.7 28.9 %collective-permute-start.15 = (bf16[2,200,448]{2,1,0:T(8,128)(2,1)S(1)}, bf16[2,200,448]{2,1,0:T(8,128)(2,1)S(1)}, u32[]{:S(2)}, u32[]{:S(2)}) collective-permute-start(bf16[2,200,448]{2,1,0:T(8,128)(2,1)S(1)} %collective-permute-done.14), channel_id=1, source_target_pairs={{0,8},{8,16},{16,24},{24,0},{1,9},{9,17},{17,25},{25,1},{2,10},{10... | collective-permute-start | bytes 1075208 | tf_op jit(solution)/shard_map/ppermute | solution.py:278
  173.4 35.3 %collective-permute-start.16 = (bf16[8,200,448]{2,1,0:T(8,128)(2,1)}, bf16[8,200,448]{2,1,0:T(8,128)(2,1)}, u32[]{:S(2)}, u32[]{:S(2)}) collective-permute-start(bf16[8,200,448]{2,1,0:T(8,128)(2,1)} %bitcast.50), channel_id=1, source_target_pairs={{0,2},{1,3},{2,0},{3,1},{4,6},{5,7},{6,4},{7,5},{8,10},{9,11},{10,... | collective-permute-start | bytes 4300808 | tf_op jit(solution)/shard_map/ppermute | solution.py:278
  174.8 69.7 %collective-permute-start.18 = (bf16[8,200,448]{2,1,0:T(8,128)(2,1)}, bf16[8,200,448]{2,1,0:T(8,128)(2,1)}, u32[]{:S(2)}, u32[]{:S(2)}) collective-permute-start(bf16[8,200,448]{2,1,0:T(8,128)(2,1)} %bitcast.50), channel_id=1, source_target_pairs={{0,1},{1,0},{2,3},{3,2},{4,5},{5,4},{6,7},{7,6},{8,9},{9,8},{10,11... | collective-permute-start | bytes 4300808 | tf_op jit(solution)/shard_map/ppermute | solution.py:278
  208.7 44.3 %collective-permute-start.17 = (bf16[8,200,448]{2,1,0:T(8,128)(2,1)}, bf16[8,200,448]{2,1,0:T(8,128)(2,1)}, u32[]{:S(2)}, u32[]{:S(2)}) collective-permute-start(bf16[8,200,448]{2,1,0:T(8,128)(2,1)} %collective-permute-done.16), channel_id=1, source_target_pairs={{0,1},{1,0},{2,3},{3,2},{4,5},{5,4},{6,7},{7,6},{8,9},{9,8},{10,11... | collective-permute-start | bytes 4300808 | tf_op jit(solution)/shard_map/ppermute | solution.py:278
  247.2 134.4 %collective-permute-start.22 = (bf16[8,200,832]{2,1,0:T(8,128)(2,1)}, bf16[8,200,832]{2,1,0:T(8,128)(2,1)}, u32[]{:S(2)}, u32[]{:S(2)}) collective-permute-start(bf16[8,200,832]{2,1,0:T(8,128)(2,1)} %bitcast.531), channel_id=1, source_target_pairs={{0,4},{4,0},{1,5},{5,1},{2,6},{6,2},{3,7},{7,3},{8,12},{12,8},{9,1... | collective-permute-start | bytes 7987208 | tf_op jit(solution)/shard_map/ppermute | solution.py:278
  252.9 124.0 %collective-permute-start.23 = (bf16[8,200,832]{2,1,0:T(8,128)(2,1)}, bf16[8,200,832]{2,1,0:T(8,128)(2,1)}, u32[]{:S(2)}, u32[]{:S(2)}) collective-permute-start(bf16[8,200,832]{2,1,0:T(8,128)(2,1)} %bitcast.532), channel_id=1, source_target_pairs={{0,4},{4,0},{1,5},{5,1},{2,6},{6,2},{3,7},{7,3},{8,12},{12,8},{9,1... | collective-permute-start | bytes 7987208 | tf_op jit(solution)/shard_map/ppermute | solution.py:278
  288.7 439.1 %reduce-scatter.6.cloned.1.call-start = ((), (), s32[]{:S(2)}) async-start(), calls=%async_computation.6 | async-start | bytes 3584000 | tf_op jit(solution)/shard_map/reduce_scatter | solution.py:437
  393.6 36.3 %collective-permute-start.24 = (bf16[2,192,1600]{2,1,0:T(8,128)(2,1)}, bf16[2,192,1600]{2,1,0:T(8,128)(2,1)}, u32[]{:S(2)}, u32[]{:S(2)}) collective-permute-start(bf16[2,192,1600]{2,1,0:T(8,128)(2,1)} %bitcast.64), channel_id=1, source_target_pairs={{0,1},{1,0},{2,3},{3,2},{4,5},{5,4},{6,7},{7,6},{8,9},{9,8},{10,11... | collective-permute-start | bytes 3686408 | tf_op jit(solution)/shard_map/ppermute | solution.py:278
  400.0 32.8 %collective-permute-start.26 = (bf16[2,192,1600]{2,1,0:T(8,128)(2,1)}, bf16[2,192,1600]{2,1,0:T(8,128)(2,1)}, u32[]{:S(2)}, u32[]{:S(2)}) collective-permute-start(bf16[2,192,1600]{2,1,0:T(8,128)(2,1)} %bitcast.69), channel_id=1, source_target_pairs={{0,1},{1,0},{2,3},{3,2},{4,5},{5,4},{6,7},{7,6},{8,9},{9,8},{10,11... | collective-permute-start | bytes 3686408 | tf_op jit(solution)/shard_map/ppermute | solution.py:278
  409.8 89.1 %collective-permute-start.34 = (bf16[8,200,832]{2,1,0:T(8,128)(2,1)}, bf16[8,200,832]{2,1,0:T(8,128)(2,1)}, u32[]{:S(2)}, u32[]{:S(2)}) collective-permute-start(bf16[8,200,832]{2,1,0:T(8,128)(2,1)} %bitcast.488), channel_id=1, source_target_pairs={{0,4},{4,0},{1,5},{5,1},{2,6},{6,2},{3,7},{7,3},{8,12},{12,8},{9,1... | collective-permute-start | bytes 7987208 | tf_op jit(solution)/shard_map/ppermute | solution.py:278
  432.4 348.8 %reduce-scatter.8.cloned.1.call-start = ((), (), s32[]{:S(2)}) async-start(), calls=%async_computation.7 | async-start | bytes 3584000 | tf_op jit(solution)/shard_map/reduce_scatter | solution.py:437
  434.6 27.7 %collective-permute-start.27 = (bf16[1,192,1600]{2,1,0:T(8,128)(2,1)S(1)}, bf16[1,192,1600]{2,1,0:T(8,128)(2,1)S(1)}, u32[]{:S(2)}, u32[]{:S(2)}) collective-permute-start(bf16[1,192,1600]{2,1,0:T(8,128)(2,1)S(1)} %fusion.79), channel_id=1, source_target_pairs={{0,2},{1,3},{2,0},{3,1},{4,6},{5,7},{6,4},{7,5},{8,10},{9,11},{10,... | collective-permute-start | bytes 1843208 | tf_op jit(solution)/shard_map/ppermute | solution.py:278
  466.0 32.7 %collective-permute-start.29 = (bf16[1,192,1600]{2,1,0:T(8,128)(2,1)}, bf16[1,192,1600]{2,1,0:T(8,128)(2,1)}, u32[]{:S(2)}, u32[]{:S(2)}) collective-permute-start(bf16[1,192,1600]{2,1,0:T(8,128)(2,1)} %bitcast.74), channel_id=1, source_target_pairs={{0,2},{1,3},{2,0},{3,1},{4,6},{5,7},{6,4},{7,5},{8,10},{9,11},{10,... | collective-permute-start | bytes 1843208 | tf_op jit(solution)/shard_map/ppermute | solution.py:278
  476.0 19.8 %collective-permute-start.32 = (bf16[1,192,512]{2,1,0:T(8,128)(2,1)}, bf16[1,192,512]{2,1,0:T(8,128)(2,1)S(1)}, u32[]{:S(2)}, u32[]{:S(2)}) collective-permute-start(bf16[1,192,512]{2,1,0:T(8,128)(2,1)} %get-tuple-element.217), channel_id=1, source_target_pairs={{0,2},{1,3},{2,0},{3,1},{4,6},{5,7},{6,4},{7,5},{8,10},{9,11},{10,... | collective-permute-start | bytes 589832 | tf_op jit(solution)/shard_map/ppermute | solution.py:278
  495.3 72.4 %collective-permute-start.28 = (bf16[1,192,1600]{2,1,0:T(8,128)(2,1)}, bf16[1,192,1600]{2,1,0:T(8,128)(2,1)}, u32[]{:S(2)}, u32[]{:S(2)}) collective-permute-start(bf16[1,192,1600]{2,1,0:T(8,128)(2,1)} %bitcast.74), channel_id=1, source_target_pairs={{0,1},{1,0},{2,3},{3,2},{4,5},{5,4},{6,7},{7,6},{8,9},{9,8},{10,11... | collective-permute-start | bytes 1843208 | tf_op jit(solution)/shard_map/ppermute | solution.py:278
  495.8 150.2 %collective-permute-start.56 = (bf16[2,8,200,448]{3,2,1,0:T(8,128)(2,1)}, bf16[2,8,200,448]{3,2,1,0:T(8,128)(2,1)}, u32[]{:S(2)}, u32[]{:S(2)}) collective-permute-start(bf16[2,8,200,448]{3,2,1,0:T(8,128)(2,1)} %pad_maximum_fusion.2), channel_id=1, source_target_pairs={{0,1},{1,0},{2,3},{3,2},{4,5},{5,4},{6,7},{7,6},{8,9},{9,8},{10,11... | collective-permute-start | bytes 8601608 | tf_op jit(solution)/shard_map/ppermute | solution.py:278
  498.7 71.4 %collective-permute-start.30 = (bf16[1,192,1600]{2,1,0:T(8,128)(2,1)}, bf16[1,192,1600]{2,1,0:T(8,128)(2,1)}, u32[]{:S(2)}, u32[]{:S(2)}) collective-permute-start(bf16[1,192,1600]{2,1,0:T(8,128)(2,1)} %collective-permute-done.29), channel_id=1, source_target_pairs={{0,1},{1,0},{2,3},{3,2},{4,5},{5,4},{6,7},{7,6},{8,9},{9,8},{10,11... | collective-permute-start | bytes 1843208 | tf_op jit(solution)/shard_map/ppermute | solution.py:278
  527.4 50.9 %collective-permute-start.37 = (bf16[2,192,1600]{2,1,0:T(8,128)(2,1)}, bf16[2,192,1600]{2,1,0:T(8,128)(2,1)}, u32[]{:S(2)}, u32[]{:S(2)}) collective-permute-start(bf16[2,192,1600]{2,1,0:T(8,128)(2,1)} %bitcast.116), channel_id=1, source_target_pairs={{0,1},{1,0},{2,3},{3,2},{4,5},{5,4},{6,7},{7,6},{8,9},{9,8},{10,11... | collective-permute-start | bytes 3686408 | tf_op jit(solution)/shard_map/ppermute | solution.py:278
  539.4 47.2 %collective-permute-start.49 = (bf16[3,2,200,448]{3,2,1,0:T(8,128)(2,1)}, bf16[3,2,200,448]{3,2,1,0:T(8,128)(2,1)}, u32[]{:S(2)}, u32[]{:S(2)}) collective-permute-start(bf16[3,2,200,448]{3,2,1,0:T(8,128)(2,1)} %bitcast.141), channel_id=1, source_target_pairs={{0,8},{8,16},{16,24},{24,0},{1,9},{9,17},{17,25},{25,1},{2,10},{10... | collective-permute-start | bytes 3225608 | tf_op jit(solution)/shard_map/ppermute | solution.py:278
  567.7 32.0 %collective-permute-start.35 = (bf16[2,192,1600]{2,1,0:T(8,128)(2,1)}, bf16[2,192,1600]{2,1,0:T(8,128)(2,1)}, u32[]{:S(2)}, u32[]{:S(2)}) collective-permute-start(bf16[2,192,1600]{2,1,0:T(8,128)(2,1)} %bitcast.101), channel_id=1, source_target_pairs={{0,1},{1,0},{2,3},{3,2},{4,5},{5,4},{6,7},{7,6},{8,9},{9,8},{10,11... | collective-permute-start | bytes 3686408 | tf_op jit(solution)/shard_map/ppermute | solution.py:278
  579.9 62.1 %collective-permute-start.38 = (bf16[1,192,1600]{2,1,0:T(8,128)(2,1)S(1)}, bf16[1,192,1600]{2,1,0:T(8,128)(2,1)S(1)}, u32[]{:S(2)}, u32[]{:S(2)}) collective-permute-start(bf16[1,192,1600]{2,1,0:T(8,128)(2,1)S(1)} %fusion.82), channel_id=1, source_target_pairs={{0,2},{1,3},{2,0},{3,1},{4,6},{5,7},{6,4},{7,5},{8,10},{9,11},{10,... | collective-permute-start | bytes 1843208 | tf_op jit(solution)/shard_map/ppermute | solution.py:278
  589.3 68.7 %collective-permute-start.50 = (bf16[3,2,200,448]{3,2,1,0:T(8,128)(2,1)}, bf16[3,2,200,448]{3,2,1,0:T(8,128)(2,1)}, u32[]{:S(2)}, u32[]{:S(2)}) collective-permute-start(bf16[3,2,200,448]{3,2,1,0:T(8,128)(2,1)} %fusion.36), channel_id=1, source_target_pairs={{0,8},{8,16},{16,24},{24,0},{1,9},{9,17},{17,25},{25,1},{2,10},{10... | collective-permute-start | bytes 3225608 | tf_op jit(solution)/shard_map/ppermute | solution.py:278
  600.9 62.5 %collective-permute-start.36 = (bf16[1,192,1600]{2,1,0:T(8,128)(2,1)S(1)}, bf16[1,192,1600]{2,1,0:T(8,128)(2,1)}, u32[]{:S(2)}, u32[]{:S(2)}) collective-permute-start(bf16[1,192,1600]{2,1,0:T(8,128)(2,1)S(1)} %fusion.80), channel_id=1, source_target_pairs={{0,2},{1,3},{2,0},{3,1},{4,6},{5,7},{6,4},{7,5},{8,10},{9,11},{10,... | collective-permute-start | bytes 1843208 | tf_op jit(solution)/shard_map/ppermute | solution.py:278
  612.1 137.1 %collective-permute-start.66 = (bf16[2,200,832]{2,1,0:T(8,128)(2,1)}, bf16[2,200,832]{2,1,0:T(8,128)(2,1)}, u32[]{:S(2)}, u32[]{:S(2)}) collective-permute-start(bf16[2,200,832]{2,1,0:T(8,128)(2,1)} %bitcast.498), channel_id=1, source_target_pairs={{0,4},{4,0},{1,5},{5,1},{2,6},{6,2},{3,7},{7,3},{8,12},{12,8},{9,1... | collective-permute-start | bytes 1996808 | tf_op jit(solution)/shard_map/ppermute | solution.py:278
  644.6 21.9 %collective-permute-start.39 = (bf16[1,192,1600]{2,1,0:T(8,128)(2,1)}, bf16[1,192,1600]{2,1,0:T(8,128)(2,1)}, u32[]{:S(2)}, u32[]{:S(2)}) collective-permute-start(bf16[1,192,1600]{2,1,0:T(8,128)(2,1)} %fusion.81), channel_id=1, source_target_pairs={{4,0},{5,1},{6,2},{7,3},{12,8},{13,9},{14,10},{15,11},{20,16},{21,... | collective-permute-start | bytes 1843208 | tf_op jit(solution)/shard_map/ppermute | solution.py:278
  653.1 33.4 %collective-permute-start.57 = (bf16[8,200,448]{2,1,0:T(8,128)(2,1)}, bf16[8,200,448]{2,1,0:T(8,128)(2,1)}, u32[]{:S(2)}, u32[]{:S(2)}) collective-permute-start(bf16[8,200,448]{2,1,0:T(8,128)(2,1)} %bitcast.157), channel_id=1, source_target_pairs={{0,2},{1,3},{2,0},{3,1},{4,6},{5,7},{6,4},{7,5},{8,10},{9,11},{10,... | collective-permute-start | bytes 4300808 | tf_op jit(solution)/shard_map/ppermute | solution.py:278
  660.9 59.4 %collective-permute-start.51 = (bf16[3,2,200,448]{3,2,1,0:T(8,128)(2,1)}, bf16[3,2,200,448]{3,2,1,0:T(8,128)(2,1)}, u32[]{:S(2)}, u32[]{:S(2)}) collective-permute-start(bf16[3,2,200,448]{3,2,1,0:T(8,128)(2,1)} %fusion.35), channel_id=1, source_target_pairs={{0,8},{8,16},{16,24},{24,0},{1,9},{9,17},{17,25},{25,1},{2,10},{10... | collective-permute-start | bytes 3225608 | tf_op jit(solution)/shard_map/ppermute | solution.py:278
  676.6 62.5 %collective-permute-start.41 = (bf16[1,192,1600]{2,1,0:T(8,128)(2,1)}, bf16[1,192,1600]{2,1,0:T(8,128)(2,1)}, u32[]{:S(2)}, u32[]{:S(2)}) collective-permute-start(bf16[1,192,1600]{2,1,0:T(8,128)(2,1)} %bitcast.123), channel_id=1, source_target_pairs={{0,2},{1,3},{2,0},{3,1},{4,6},{5,7},{6,4},{7,5},{8,10},{9,11},{10,... | collective-permute-start | bytes 1843208 | tf_op jit(solution)/shard_map/ppermute | solution.py:278
  682.1 25.1 %collective-permute-start.45 = (f32[1,8,1600]{2,1,0:T(8,128)S(1)}, f32[1,8,1600]{2,1,0:T(8,128)S(1)}, u32[]{:S(2)}, u32[]{:S(2)}) collective-permute-start(f32[1,8,1600]{2,1,0:T(8,128)S(1)} %fusion.175), channel_id=1, source_target_pairs={{0,2},{1,3},{2,0},{3,1},{4,6},{5,7},{6,4},{7,5},{8,10},{9,11},{10,... | collective-permute-start | bytes 153608 | tf_op jit(solution)/shard_map/ppermute | solution.py:278
  727.8 26.3 %collective-permute-start.65 = (bf16[2,200,832]{2,1,0:T(8,128)(2,1)}, bf16[2,200,832]{2,1,0:T(8,128)(2,1)S(1)}, u32[]{:S(2)}, u32[]{:S(2)}) collective-permute-start(bf16[2,200,832]{2,1,0:T(8,128)(2,1)} %bitcast.499), channel_id=1, source_target_pairs={{0,4},{4,0},{1,5},{5,1},{2,6},{6,2},{3,7},{7,3},{8,12},{12,8},{9,1... | collective-permute-start | bytes 1996808 | tf_op jit(solution)/shard_map/ppermute | solution.py:278
  736.9 33.9 %collective-permute-start.52 = (bf16[3,2,200,448]{3,2,1,0:T(8,128)(2,1)}, bf16[3,2,200,448]{3,2,1,0:T(8,128)(2,1)S(1)}, u32[]{:S(2)}, u32[]{:S(2)}) collective-permute-start(bf16[3,2,200,448]{3,2,1,0:T(8,128)(2,1)} %add_convert_fusion.2), channel_id=1, source_target_pairs={{0,4},{4,0},{1,5},{5,1},{2,6},{6,2},{3,7},{7,3},{8,12},{12,8},{9,1... | collective-permute-start | bytes 3225608 | tf_op jit(solution)/shard_map/ppermute | solution.py:278
  739.0 46.1 %collective-permute-start.40 = (bf16[1,192,1600]{2,1,0:T(8,128)(2,1)}, bf16[1,192,1600]{2,1,0:T(8,128)(2,1)}, u32[]{:S(2)}, u32[]{:S(2)}) collective-permute-start(bf16[1,192,1600]{2,1,0:T(8,128)(2,1)} %bitcast.123), channel_id=1, source_target_pairs={{0,1},{1,0},{2,3},{3,2},{4,5},{5,4},{6,7},{7,6},{8,9},{9,8},{10,11... | collective-permute-start | bytes 1843208 | tf_op jit(solution)/shard_map/ppermute | solution.py:278
  747.9 37.2 %collective-permute-start.42 = (bf16[1,192,1600]{2,1,0:T(8,128)(2,1)}, bf16[1,192,1600]{2,1,0:T(8,128)(2,1)}, u32[]{:S(2)}, u32[]{:S(2)}) collective-permute-start(bf16[1,192,1600]{2,1,0:T(8,128)(2,1)} %collective-permute-done.41), channel_id=1, source_target_pairs={{0,1},{1,0},{2,3},{3,2},{4,5},{5,4},{6,7},{7,6},{8,9},{9,8},{10,11... | collective-permute-start | bytes 1843208 | tf_op jit(solution)/shard_map/ppermute | solution.py:278
  749.2 27.1 %collective-permute-start.61 = (bf16[1,2,200,448]{3,2,1,0:T(8,128)(2,1)S(1)}, bf16[1,2,200,448]{3,2,1,0:T(8,128)(2,1)S(1)}, u32[]{:S(2)}, u32[]{:S(2)}) collective-permute-start(bf16[1,2,200,448]{3,2,1,0:T(8,128)(2,1)S(1)} %add_convert_fusion.6), channel_id=1, source_target_pairs={{0,4},{4,0},{1,5},{5,1},{2,6},{6,2},{3,7},{7,3},{8,12},{12,8},{9,1... | collective-permute-start | bytes 1075208 | tf_op jit(solution)/shard_map/ppermute | solution.py:278
  772.2 29.1 %collective-permute-start.54 = (bf16[3,2,200,448]{3,2,1,0:T(8,128)(2,1)}, bf16[3,2,200,448]{3,2,1,0:T(8,128)(2,1)}, u32[]{:S(2)}, u32[]{:S(2)}) collective-permute-start(bf16[3,2,200,448]{3,2,1,0:T(8,128)(2,1)} %add_convert_fusion.1), channel_id=1, source_target_pairs={{0,2},{1,3},{2,0},{3,1},{4,6},{5,7},{6,4},{7,5},{8,10},{9,11},{10,... | collective-permute-start | bytes 3225608 | tf_op jit(solution)/shard_map/ppermute | solution.py:278
  778.0 20.2 %collective-permute-start.63 = (bf16[1,2,200,448]{3,2,1,0:T(8,128)(2,1)}, bf16[1,2,200,448]{3,2,1,0:T(8,128)(2,1)}, u32[]{:S(2)}, u32[]{:S(2)}) collective-permute-start(bf16[1,2,200,448]{3,2,1,0:T(8,128)(2,1)} %add_convert_fusion.5), channel_id=1, source_target_pairs={{0,2},{1,3},{2,0},{3,1},{4,6},{5,7},{6,4},{7,5},{8,10},{9,11},{10,... | collective-permute-start | bytes 1075208 | tf_op jit(solution)/shard_map/ppermute | solution.py:278
  781.1 27.3 %collective-permute-start.67 = (bf16[2,200,832]{2,1,0:T(8,128)(2,1)}, bf16[2,200,832]{2,1,0:T(8,128)(2,1)}, u32[]{:S(2)}, u32[]{:S(2)}) collective-permute-start(bf16[2,200,832]{2,1,0:T(8,128)(2,1)} %bitcast.489), channel_id=1, source_target_pairs={{0,4},{4,0},{1,5},{5,1},{2,6},{6,2},{3,7},{7,3},{8,12},{12,8},{9,1... | collective-permute-start | bytes 1996808 | tf_op jit(solution)/shard_map/ppermute | solution.py:278
  (128 other events, 1435.7 us)
Sparse Core Ops, SparseCore 0:
  30.7 74.9 all-gather.2
  107.9 80.3 all-gather.4
  288.8 68.9 reduce-scatter.3
  432.5 69.2 reduce-scatter.5
  555.3 98.5 reduce-scatter.7

commit v2 on v1

--- a/solution.py
+++ b/solution.py
@@ -134,24 +134,26 @@
     g_ref,
     ot_ref,
     log_ref,
-    dq_ref,
-    dk_ref,
-    dv_ref,
+    o_ref,
     ktbuf,
     dkbuf,
     dvbuf,
 ):
     rows = q_ref.shape[0]
-    pair = pl.program_id(0)
+    pair, part = pl.program_id(0), pl.program_id(1)
     live = (pair < pl.num_programs(0) - 1) | (live_ref[0] > 0)
-    dkbuf[...] = jnp.zeros_like(dkbuf)
-    dvbuf[...] = jnp.zeros_like(dvbuf)
-
-    @pl.when(jnp.logical_not(live))
+
+    @pl.when(part == 0)
     def _():
-        dq_ref[...] = jnp.zeros_like(dq_ref)
-
-    @pl.when(live)
+        dkbuf[...] = jnp.zeros_like(dkbuf)
+        dvbuf[...] = jnp.zeros_like(dvbuf)
+        o_ref[:rows, :] = jnp.zeros((rows, PAIR), bf16)
+
+    @pl.when((part == 0) & jnp.logical_not(live))
+    def _():
+        o_ref[rows:, :] = jnp.zeros((rows, PAIR), bf16)
+
+    @pl.when((part == 0) & live)
     def _():
         ktbuf[...] = k_ref[...].astype(f32).T.astype(bf16)
         for qb in range(rows // BLOCK):
@@ -185,33 +187,38 @@
 
             empty = jnp.zeros((HEAD, BLOCK), f32)
             done = lax.fori_loop(low_ref[qb], rows // BLOCK + qb + 1, step, (empty, empty))
-            dq_ref[span, :] = (jnp.concatenate(done, 0) * SCALE).T.astype(bf16)
-
-    dk_ref[...] = dkbuf[...].astype(bf16)
-    dv_ref[...] = dvbuf[...].astype(bf16)
-
-
-def column_spec(rows):
-    return pl.BlockSpec((rows, PAIR), lambda p: (0, p))
-
-
-def attention_forward(low, live, start, queries, keys, values):
-    rows, width = queries.shape
-    pairs = width // PAIR
+            into = slice(rows + qb * BLOCK, rows + (qb + 1) * BLOCK)
+            o_ref[into, :] = (jnp.concatenate(done, 0) * SCALE).T.astype(bf16)
+
+    @pl.when(part == 1)
+    def _():
+        o_ref[...] = dkbuf[...].astype(bf16)
+
+    @pl.when(part == 2)
+    def _():
+        o_ref[...] = dvbuf[...].astype(bf16)
+
+
+def attention_specs(rows, pairs):
     smem = pl.BlockSpec(memory_space=pltpu.SMEM)
+    return [
+        smem,
+        smem,
+        pl.BlockSpec((1, rows), lambda p, *_: (0, 0)),
+        pl.BlockSpec((rows, PAIR), lambda p, *_: (1, p)),
+        pl.BlockSpec((2 * rows, PAIR), lambda p, *_: (0, pairs + p)),
+        pl.BlockSpec((2 * rows, PAIR), lambda p, *_: (0, 2 * pairs + p)),
+    ]
+
+
+def attention_forward(low, live, start, joined):
+    rows, pairs = joined.shape[0] // 2, joined.shape[1] // (3 * PAIR)
     return pl.pallas_call(
         forward_kernel,
         grid=(pairs,),
-        in_specs=[
-            smem,
-            smem,
-            pl.BlockSpec((1, rows), lambda p: (0, 0)),
-            column_spec(rows),
-            column_spec(2 * rows),
-            column_spec(2 * rows),
-        ],
+        in_specs=attention_specs(rows, pairs),
         out_specs=[
-            column_spec(rows),
+            pl.BlockSpec((rows, PAIR), lambda p: (0, p)),
             pl.BlockSpec((PAIR, rows), lambda p: (p, 0)),
             pl.BlockSpec((1, 2, rows), lambda p: (p, 0, 0)),
         ],
@@ -227,29 +234,22 @@
             transcendentals=rows * rows * pairs * 2,
         ),
         name="attention_forward",
-    )(low, live, start, queries, keys, values)
-
-
-def attention_backward(low, live, start, queries, keys, values, grad, turned, log_total):
-    rows, width = queries.shape
-    pairs = width // PAIR
-    smem = pl.BlockSpec(memory_space=pltpu.SMEM)
+    )(low, live, start, joined, joined, joined)
+
+
+def attention_backward(low, live, start, joined, grad, turned, log_total):
+    rows, pairs = joined.shape[0] // 2, joined.shape[1] // (3 * PAIR)
     return pl.pallas_call(
         backward_kernel,
-        grid=(pairs,),
-        in_specs=[
-            smem,
-            smem,
-            pl.BlockSpec((1, rows), lambda p: (0, 0)),
-            column_spec(rows),
-            column_spec(2 * rows),
-            column_spec(2 * rows),
-            column_spec(rows),
-            pl.BlockSpec((PAIR, rows), lambda p: (p, 0)),
-            pl.BlockSpec((1, 2, rows), lambda p: (p, 0, 0)),
+        grid=(pairs, 3),
+        in_specs=attention_specs(rows, pairs)
+        + [
+            pl.BlockSpec((rows, PAIR), lambda p, *_: (0, p)),
+            pl.BlockSpec((PAIR, rows), lambda p, *_: (p, 0)),
+            pl.BlockSpec((1, 2, rows), lambda p, *_: (p, 0, 0)),
         ],
-        out_specs=[column_spec(rows)] + [column_spec(2 * rows)] * 2,
-        out_shape=[jax.ShapeDtypeStruct((count, pairs * PAIR), bf16) for count in (rows, 2 * rows, 2 * rows)],
+        out_specs=pl.BlockSpec((2 * rows, PAIR), lambda p, part: (0, part * pairs + p)),
+        out_shape=jax.ShapeDtypeStruct(joined.shape, bf16),
         scratch_shapes=[
             pltpu.VMEM((PAIR, 2 * rows), bf16),
             pltpu.VMEM((2 * rows, PAIR), f32),
@@ -261,7 +261,7 @@
             transcendentals=rows * rows * pairs * 2,
         ),
         name="attention_backward",
-    )(low, live, start, queries, keys, values, grad, turned, log_total)
+    )(low, live, start, joined, joined, joined, grad, turned, log_total)
 
 
 def row_major(values):
@@ -313,36 +313,26 @@
     return out
 
 
-def gather_halves(shard, parts):
+def gather_halves(shard):
     size, here = lax.axis_size("fsdp"), lax.axis_index("fsdp")
     side = lax.axis_index("ctx")
     rows, columns = shard.shape
-    width = columns // parts
     halves = shard.reshape(2, rows // 2, columns)
     own = lax.dynamic_index_in_dim(halves, side, 0, False)
     if size > 4:
         mine = lax.all_gather(own, "fsdp", axis=0)
         theirs = across(mine, "ctx", 1)
         both = jnp.where(side == 0, jnp.stack([mine, theirs], 1), jnp.stack([theirs, mine], 1))
-        both = both.reshape(size * rows, columns)
-        return [both[:, i * width : (i + 1) * width] for i in range(parts)], [mine] * (size - 1)
-    whole = [
-        lax.dynamic_update_slice(
-            unfilled((2 * size, rows // 2, width), shard.dtype),
-            halves[:, :, i * width : (i + 1) * width],
-            (2 * here, 0, 0),
-        )
-        for i in range(parts)
-    ]
+        return both.reshape(size * rows, columns), [mine] * (size - 1)
+    whole = unfilled((2 * size, rows // 2, columns), shard.dtype)
+    whole = lax.dynamic_update_slice(whole, halves, (2 * here, 0, 0))
     pieces = ring(own, "fsdp")
     for back, piece in enumerate(pieces, 1):
         other = across(piece, "ctx", 1)
         at = 2 * ((here + size - back) % size)
-        for i in range(parts):
-            span = slice(i * width, (i + 1) * width)
-            whole[i] = place(whole[i], piece[:, span], at + side)
-            whole[i] = place(whole[i], other[:, span], at + 1 - side)
-    return [part.reshape(size * rows, width) for part in whole], pieces
+        whole = place(whole, piece, at + side)
+        whole = place(whole, other, at + 1 - side)
+    return whole.reshape(size * rows, columns), pieces
 
 
 def gather_direct(values):
@@ -361,12 +351,12 @@
     rows, columns = shard.shape
     own = tied(shard, *after)
     if size > 4:
-        return lax.all_gather(own, "fsdp", axis=0, tiled=True), [own] * (size - 1)
+        return lax.all_gather(own, "fsdp", axis=0, tiled=True)
     whole = place(unfilled((size, rows, columns), shard.dtype), own, here)
-    pieces = ring(own, "fsdp")
-    for back, piece in enumerate(pieces, 1):
+    for back in range(1, size):
+        piece = moved(own, "fsdp", [(i, (i + back) % size) for i in range(size)])
         whole = place(whole, piece, (here + size - back) % size)
-    return whole.reshape(size * rows, columns), pieces
+    return whole.reshape(size * rows, columns)
 
 
 def gather_pair(own, after=()):
@@ -375,8 +365,8 @@
     return mine, theirs
 
 
-def from_tp(own):
-    beside = across(own, "tp", 2)
+def from_tp(own, after=()):
+    beside = tied(across(own, "tp", 2), *after)
     return [own, across(own, "tp", 1), beside, across(beside, "tp", 1)]
 
 
@@ -437,54 +427,64 @@
     return row_major(lax.psum_scatter(row_major(both), "fsdp", scatter_dimension=0, tiled=True))
 
 
-def ring_sum(parts):
-    size, here = lax.axis_size("fsdp"), lax.axis_index("fsdp")
-    if size > 4:
-        return lax.psum_scatter(parts, "fsdp", scatter_dimension=1)
-    own = lambda back: lax.dynamic_index_in_dim(parts, (here + size - back) % size, 1, False)
-    held = own(1)
-    for back in range(2, size + 1):
-        come = moved(held.astype(bf16), "fsdp", [(i, (i + 1) % size) for i in range(size)])
-        held = come.astype(f32) + own(back % size).astype(f32)
-    return held.astype(bf16)
-
-
-def finish_rows(terms):
-    size = lax.axis_size("fsdp")
-    count, rows, columns = terms.shape
-    mine = ring_sum(terms.reshape(count, size, rows // size, columns))
-    return (mine.astype(f32) + across(mine, "ctx", 1).astype(f32)).astype(bf16)
-
-
-def join_kernel(step, index_ref, *refs):
+def finish_rows(terms, chunks):
+    mine = spread_fsdp(terms)
+    chunks = chunks if mine.shape[0] % (8 * chunks) == 0 else 1
+    rows, out = mine.shape[0] // chunks, []
+    for i in range(chunks):
+        piece = mine[i * rows : (i + 1) * rows]
+        out.append(from_tp((piece.astype(f32) + across(piece, "ctx", 1).astype(f32)).astype(bf16)))
+    return out
+
+
+def join_kernel(step, reach, index_ref, *refs):
     o_ref = refs[-1]
-    pieces = refs[:-1]
-    count = pieces[0].shape[0]
+    members = 4
+    chunks = (len(refs) - 1) // members
+    width = refs[0].shape[1]
     me = index_ref[0]
-    out = []
-    for part in range(count):
-        for s in range(len(pieces)):
-            value = pieces[0][part].astype(f32)
-            for j in range(1, len(pieces)):
-                value = jnp.where(me ^ s == j, pieces[j][part].astype(f32), value)
-            out.append(value if s == len(pieces) - 1 else value[:, :step])
-    o_ref[...] = jnp.concatenate(out, 1)
-
-
-def join_windows(pieces, index, step):
-    count, rows, reach = pieces[0].shape
-    width = count * (step * (len(pieces) - 1) + reach)
-    tall = rows // 5 if rows % 40 == 0 else rows
+    count = -(-width // (reach + PAIR))
+    window = width // count
+    for chunk in range(chunks):
+        pieces = refs[chunk * members : (chunk + 1) * members]
+
+        @pl.when(pl.program_id(0) // (pl.num_programs(0) // chunks) == chunk)
+        def _():
+            out = []
+            for s in range(members):
+                value = pieces[0][...].astype(f32)
+                for j in range(1, members):
+                    value = jnp.where(me ^ s == j, pieces[j][...].astype(f32), value)
+                out.append(value)
+            o_ref[...] = jnp.concatenate(
+                [
+                    out[s][:, part * window : part * window + (reach if s == members - 1 else step)]
+                    for part in range(count)
+                    for s in range(members)
+                ],
+                1,
+            )
+
+
+def join_windows(chunks, index, step, reach):
+    rows, width = chunks[0][0].shape
+    members = len(chunks[0])
+    whole = -(-width // (reach + PAIR)) * (step * (members - 1) + reach)
+    steps = next((n for n in (5, 1) if rows % (8 * n) == 0), 1)
+    tall = rows // steps
+
+    def spec(chunk):
+        return pl.BlockSpec((tall, width), lambda r: (jnp.clip(r - chunk * steps, 0, steps - 1), 0))
+
     return pl.pallas_call(
-        partial(join_kernel, step),
-        grid=(rows // tall,),
-        in_specs=[pl.BlockSpec(memory_space=pltpu.SMEM)]
-        + [pl.BlockSpec((count, tall, reach), lambda r: (0, r, 0))] * len(pieces),
-        out_specs=pl.BlockSpec((tall, width), lambda r: (r, 0)),
-        out_shape=jax.ShapeDtypeStruct((rows, width), f32),
-        cost_estimate=pl.CostEstimate(flops=0, bytes_accessed=6 * rows * width, transcendentals=0),
+        partial(join_kernel, step, reach),
+        grid=(len(chunks) * steps,),
+        in_specs=[pl.BlockSpec(memory_space=pltpu.SMEM)] + [spec(i) for i in range(len(chunks)) for _ in range(members)],
+        out_specs=pl.BlockSpec((tall, whole), lambda r: (r, 0)),
+        out_shape=jax.ShapeDtypeStruct((len(chunks) * rows, whole), f32),
+        cost_estimate=pl.CostEstimate(flops=0, bytes_accessed=6 * rows * whole, transcendentals=0),
         name="join_windows",
-    )(index.reshape(1), *pieces)
+    )(index.reshape(1), *[piece for chunk in chunks for piece in chunk])
 
 
 def scatter_vectors(vectors, extra):
@@ -552,13 +552,12 @@
         return jnp.concatenate([low[..., :cut], high], -1)
 
     windows_in = jnp.concatenate([window_in(part) for part in range(3)], 1)
-    (weight_q, weight_k, weight_v), pieces_in = gather_halves(windows_in, 3)
-    weight_out, _ = gather_whole(
-        lax.dynamic_slice_in_dim(output_weight, me * step, reach, 1), (pieces_in[1],)
-    )
+    weight_in, pieces_in = gather_halves(windows_in)
+    weight_out = gather_whole(lax.dynamic_slice_in_dim(output_weight, me * step, reach, 1), (pieces_in[1],))
     up_mine, up_theirs = gather_pair(halves(up_weight[:, :half], up_weight[:, cut:])[0], (pieces_in[0],))
-    down_mine, down_theirs = gather_pair(halves(down_weight[:half].T, down_weight[cut:].T)[0], (pieces_in[0],))
-    windows_out = from_tp(weight_out)
+    downs = jnp.stack(halves(down_weight[:half].T, down_weight[cut:].T))
+    downs = row_major(lax.all_gather(tied(downs, pieces_in[0]), "fsdp", axis=0))
+    down_mine, down_theirs = (downs[:, i].reshape(width, half) for i in range(2))
 
     small = [first_gain, first_bias, query_bias, value_bias, output_bias, second_gain, second_bias, up_bias, down_bias]
     small = jnp.stack(tied(small, windows_in))
@@ -581,12 +580,13 @@
         norm_forward(part.astype(f32), gain_one, bias_one)[0].astype(bf16) for part in (tokens, earlier)
     )
     normed_all = jnp.concatenate([normed_early, normed_one], 0)
-    keys = dot(normed_all, weight_k).astype(bf16)
-    values = (dot(normed_all, weight_v) + window_of(bias_value)).astype(bf16)
-    queries = (dot(normed_one, weight_q) + window_of(bias_query)).astype(bf16)
+    bias_in = jnp.concatenate([window_of(bias_query), jnp.zeros((window,), f32), window_of(bias_value)])
+    joined = (dot(normed_all, weight_in) + bias_in).astype(bf16)
     upstream = picked(tied(cotangent, pieces_in[1]).reshape(members, few, width), me)
-    queries, upstream = lax.optimization_barrier((queries, upstream))
-    mixed, turned, log_total = attention_forward(low, live, start, queries, keys, values)
+    joined, upstream = lax.optimization_barrier((joined, upstream))
+    mixed, turned, log_total = attention_forward(low, live, start, joined)
+
+    windows_out = from_tp(weight_out, (mixed,))
 
     def to_tp(pieces):
         come = [pieces[0]] + [across(pieces[j], "tp", j) for j in range(1, members)]
@@ -604,19 +604,20 @@
     normed_two = from_tp(normed.astype(bf16))
     normed_two = jnp.concatenate([normed_two[j] for j in FOLD], 0)
 
-    def hidden_half(weight_up, weight_down, bias):
+    def hidden_half(normed, weight_up, weight_down, bias):
         grad_activated = dot(upstream, weight_down)
-        preact = dot(normed_two, weight_up) + bias
+        preact = dot(normed, weight_up) + bias
         activated, gelu_pull = jax.vjp(gelu_tanh, preact)
         return activated.astype(bf16), gelu_pull(grad_activated)[0].astype(bf16)
 
-    act_mine, pre_mine = hidden_half(up_mine, down_mine, bias_mine)
-    act_theirs, pre_theirs = hidden_half(up_theirs, down_theirs, bias_theirs)
+    act_theirs, pre_theirs = hidden_half(normed_two, up_theirs, down_theirs, bias_theirs)
+    down_gone = row_major(cut_rows(dot_rows(upstream, act_theirs).astype(bf16)))
+    down_come = across(down_gone, "ctx", 1)
+    act_mine, pre_mine = hidden_half(tied(normed_two, down_gone), up_mine, down_mine, bias_mine)
     grad_normed = scatter_tp([(pre_mine, up_mine), (pre_theirs, up_theirs)])
-    down_gone = dot_rows(upstream, act_theirs).astype(bf16)
     up_gone = dot_rows(normed_two, pre_theirs).astype(bf16)
     up_kept = dot_rows(normed_two, pre_mine).astype(bf16)
-    grad_normed = tied(grad_normed, down_gone, up_gone, up_kept)
+    grad_normed = tied(grad_normed, up_gone, up_kept)
     own_upstream = upstream[:few].astype(f32)
     grad_two, grad_gain_two, grad_bias_two = norm_backward(grad_normed, unit_two, inverse_two, gain_two)
     grad_middle = own_upstream + grad_two
@@ -638,8 +639,9 @@
 
     up_gone, up_kept = spread_fsdp(up_gone), spread_fsdp(up_kept)
     other_gone, other_kept = across(up_gone, "ctx", 1), across(up_kept, "ctx", 1)
-    down_kept = dot_rows(upstream, act_mine) + across(down_gone, "ctx", 1).astype(f32)
-    down_kept = down_kept.astype(bf16)
+    late_mine = tied(act_mine, grad_mixture)
+    down_kept = row_major(cut_rows(dot_rows(upstream, late_mine))) + down_come.astype(f32)
+    down_kept = down_kept.astype(bf16).reshape(width, half)
     down_sum = spread_fsdp(down_kept)
     shard_down = whole_of(down_sum, across(down_sum, "ctx", 1)).astype(f32).T
     shard_up = whole_of(
@@ -648,43 +650,31 @@
     )
     late_mine, late_theirs = tied((act_mine, act_theirs), grad_mixture)
     result = scatter_tp([(late_mine, down_mine), (late_theirs, down_theirs)])
-    result = (middle + result + bias_down).astype(bf16)
-    result = natural(from_tp(result), me, bf16)
+    result = from_tp((middle + result + bias_down).astype(bf16))
+
+    grad_mixed = tied(grad_mixed, down_kept)
+    grads = attention_backward(low, live, start, joined, grad_mixed, turned, log_total)
+    grad_in = row_major(dot_rows(normed_all, grads).astype(bf16))
+    shard_in = join_windows(finish_rows(grad_in, 2), me, step, reach)
+
+    late_mixture, late_windows = tied((mixture, branch_windows), grads)
 
     def branch_product(j):
-        return dot_rows(mixture, branch_windows[j])
-
-    come = across(jnp.stack([branch_product(1), branch_product(3)]).astype(bf16), "tp", 1).astype(f32)
+        return row_major(cut_rows(dot_rows(late_mixture, late_windows[j])))
+
+    come = [across(branch_product(j).astype(bf16), "tp", 1).astype(f32) for j in (1, 3)]
     near = branch_product(0) + come[0]
     far = (branch_product(2) + come[1]).astype(bf16)
-    near = (near + across(far, "tp", 2).astype(f32)).astype(bf16)
-    shard_out = join_windows(from_tp(finish_rows(near[None])), me, step)
-
-    grad_mixed = tied(grad_mixed, down_kept)
-    grad_q, grad_k, grad_v = attention_backward(
-        low, live, start, queries, keys, values, grad_mixed, turned, log_total
-    )
-    grad_in = jnp.stack(
-        [
-            row_major(dot_rows(left, grad[:, :reach]).astype(bf16).reshape(4, -1, reach)).reshape(width, reach)
-            for left, grad in ((normed_one, grad_q), (normed_all, grad_k), (normed_all, grad_v))
-        ]
-    )
-    shard_in = join_windows(from_tp(finish_rows(grad_in)), me, step)
-
-    def turned_rows(grad):
-        return picked(grad.reshape(members, few, window), me)
-
-    grad_early = scatter_tp(
-        [(turned_rows(grad[:rows]), weight) for grad, weight in ((grad_k, weight_k), (grad_v, weight_v))]
-    )
-    grad_normed = scatter_tp(
-        [
-            (turned_rows(grad), weight)
-            for grad, weight in ((grad_q, weight_q), (grad_k[rows:], weight_k), (grad_v[rows:], weight_v))
-        ]
-    )
-    grad_normed += moved(grad_early.astype(bf16), "ctx", [(1, 0)]).astype(f32)
+    come = across(far, "tp", 2)
+    near = (near + come.astype(f32)).astype(bf16).reshape(width, reach)
+    shard_out = join_windows(finish_rows(tied(near, grad_in), 1), me, step, reach)
+    result = natural(tied(result, grads), me, bf16)
+
+    both = jnp.stack([grads[rows:].reshape(members, few, -1), grads[:rows].reshape(members, few, -1)], 1)
+    both = picked(tied(both, far).reshape(members, 2 * few, -1), me)
+    grad_normed = scatter_tp([(both, weight_in)])
+    grad_early = moved(grad_normed[few:].astype(bf16), "ctx", [(1, 0)])
+    grad_normed = grad_normed[:few] + grad_early.astype(f32)
     _, unit_one, inverse_one = norm_forward(own_tokens, gain_one, bias_one)
     grad_one, grad_gain_one, grad_bias_one = norm_backward(grad_normed, unit_one, inverse_one, gain_one)
     gradient = (grad_middle + grad_one).astype(bf16)
@@ -695,12 +685,13 @@
         columns = jnp.where(jnp.arange(window) < jnp.where(me == members - 1, reach, step), columns, 0.0)
         return lax.dynamic_update_slice_in_dim(wide, columns, me * step, 0)[:width]
 
+    grad_sums = jnp.sum(grads.astype(f32), 0)
     vectors = jnp.stack(
         [
             grad_gain_one,
             grad_bias_one,
-            spread(jnp.sum(grad_q.astype(f32), 0)),
-            spread(jnp.sum(grad_v.astype(f32), 0)),
+            spread(grad_sums[:window]),
+            spread(grad_sums[2 * window :]),
             jnp.sum(grad_branch.astype(f32), 0),
             grad_gain_two,
             grad_bias_two,

time: 836 us -> 760 us (0.909)
  starting transfers between devices: 165 us -> 104 us
  other arithmetic: 89.6 us -> 63.8 us
  waiting for transfers between devices: 297 us -> 322 us
  local copies, waits for them, and re-layouts: 76.8 us -> 52.8 us
  Pallas kernels: 50.3 us -> 59.8 us
    ppermute x61 -> x57, starting transfers between devices: 154 us -> 70.6 us  [moved(): lax.ppermute(row_major(cut_rows(values)), axis, pairs)]
    ppermute x3, starting transfers between devices: 2.22 us -> 23.7 us  [scatter_vectors(): lax.ppermute(piece, 'fsdp', [(i, (i + back) % size) for i in range(size)])]
    reduce_scatter x3 -> x5, waiting for transfers between devices: 0.01 us -> 18.9 us  [spread_fsdp(): lax.psum_scatter(row_major(both), 'fsdp', scatter_dimension=0, tiled=True)]
    dot_general x22 -> x14, matrix products: 57.4 us -> 44.6 us  [dot_lanes(): lax.dot_general(left, right, (((1,), (1,)), ((), ())), preferred_element_...]
    convert_element_type x3 -> x0, local copies, waits for them, and re-layouts: 12.6 us -> none  [the longest x2 7.32 us: on_device(): near = (near + across(far, 'tp', 2).astype(f32)).astype(bf16)]
    convert_element_type x12 -> x7, other arithmetic: 27.3 us -> 16 us  [the longest x1 4.76 us: on_device(): near = (near + come.astype(f32)).astype(bf16).reshape(width, reach)]
    dot_general x11 -> x9, matrix products: 39.9 us -> 50.4 us  [dot(): return jnp.dot(left, right, preferred_element_type=f32)]
    pallas_call x4, Pallas kernels: 43 us -> 52.3 us  [the longest x1 22.3 us: attention_backward(): pl.pallas_call(backward_kernel, grid=(pairs, 3), in_specs=attention_specs...]
  transfers between devices with their start and end apart: 73 -> 71, of which waited for: 25 -> 28; matrix products, arithmetic and copies ran while one was open for 35% -> 28% of each run, Pallas kernels for 5% -> 7%
where the time goes in v2:
time: 760 us; the launch traced here: 745 us
  waiting for transfers between devices  322 us (42%)
  matrix products  126 us (17%)
  starting transfers between devices  104 us (14%)
  other arithmetic  63.8 us (8%)
  Pallas kernels  59.8 us (8%)
  local copies, waits for them, and re-layouts  52.8 us (7%)
  between operations  16.5 us (2%)
    ppermute x57, waiting for transfers between devices, moved(): lax.ppermute(row_major(cut_rows(values)), axis, pairs)  302 us
    ppermute x57, starting transfers between devices, moved(): lax.ppermute(row_major(cut_rows(values)), axis, pairs)  70.6 us
    dot_general x9, matrix products, dot(): return jnp.dot(left, right, preferred_element_type=f32)  50.4 us
    dot_general x14, matrix products, dot_lanes(): lax.dot_general(left, right, (((1,), (1,)), ((), ())), preferred_element_...  44.6 us
    dot_general x9, matrix products, dot_rows(): lax.dot_general(left, right, (((0,), (0,)), ((), ())), preferred_element_...  31.4 us
    ppermute x3, starting transfers between devices, scatter_vectors(): lax.ppermute(piece, 'fsdp', [(i, (i + back) % size) for i in range(size)])  23.7 us
    pallas_call x1, Pallas kernels, attention_backward(): pl.pallas_call(backward_kernel, grid=(pairs, 3), in_specs=attention_specs...  22.3 us
    unnamed x168, local copies, waits for them, and re-layouts  19.1 us
  transfers between devices with their start and end apart: 71, of which 28 were waited for; matrix products, arithmetic and copies ran while one was open for 28% of the time, Pallas kernels for 7%

profile of v2, /device:TPU:0, one launch (start us, length us, event | category | flops | bytes accessed | tf_op | source)
XLA Modules:
  0.0 745.0 jit_solution(17047011615163051260)
XLA Ops:
  15.7 13.8 %collective-permute-done = bf16[1,200,1536]{2,1,0:T(8,128)(2,1)S(1)} collective-permute-done((bf16[1,200,1536]{2,1,0:T(8,128)(2,1)}, bf16[1,200,1536]{2,1,0:T(8,128)(2,1)S(1)}, u32[]{:S(2)}, u32[]{:S(2)}) %collective-permute-start) | collective-permute-done | bytes 614432 | tf_op jit(solution)/shard_map/ppermute | solution.py:278
  33.7 4.9 collective-permute-start.1
  51.3 27.4 %collective-permute-done.6 = bf16[1,200,1536]{2,1,0:T(8,128)(2,1)S(1)} collective-permute-done((bf16[1,200,1536]{2,1,0:T(8,128)(2,1)S(1)}, bf16[1,200,1536]{2,1,0:T(8,128)(2,1)S(1)}, u32[]{:S(2)}, u32[]{:S(2)}) %collective-permute-start.6) | collective-permute-done | bytes 614432 | tf_op jit(solution)/shard_map/ppermute | solution.py:278
  78.7 11.7 %collective-permute-start.13 = (bf16[2,200,448]{2,1,0:T(8,128)(2,1)S(1)}, bf16[2,200,448]{2,1,0:T(8,128)(2,1)}, u32[]{:S(2)}, u32[]{:S(2)}) collective-permute-start(bf16[2,200,448]{2,1,0:T(8,128)(2,1)S(1)} %bitcast.373), channel_id=1, source_target_pairs={{0,8},{8,16},{16,24},{24,0},{1,9},{9,17},{17,25},{25,1},{2,10},{10... | collective-permute-start | bytes 1075208 | tf_op jit(solution)/shard_map/ppermute | solution.py:278
  93.6 4.5 copy.88
  104.9 5.8 collective-permute-done.13
  112.9 27.7 %collective-permute-done.14 = bf16[2,200,448]{2,1,0:T(8,128)(2,1)} collective-permute-done((bf16[2,200,448]{2,1,0:T(8,128)(2,1)S(1)}, bf16[2,200,448]{2,1,0:T(8,128)(2,1)}, u32[]{:S(2)}, u32[]{:S(2)}) %collective-permute-start.14) | collective-permute-done | bytes 358432 | tf_op jit(solution)/shard_map/ppermute | solution.py:278
  155.5 6.6 collective-permute-done.9
  162.1 10.8 %add_convert_fusion.q_ref.k_ref.v_ref = bf16[1536,1536]{1,0:T(8,128)(2,1)} fusion(bf16[1600,1536]{1,0:T(8,128)(2,1)S(1)} %bitcast.354, f32[1536]{0:T(1024)S(1)} %pad_maximum_fusion.11, bf16[768,1600]{0,1:T(8,128)(2,1)S(1)} %get-tuple-element.260, bf16[768,1600]{0,1:T(8,128)(2,1)S(1)} %get-tuple-element.259), kind=kOutput, calls=%fused_computation.1 | convolution fusion | flops 7564296192 | bytes 14555136 | tf_op jit(solution)/shard_map/dot_general | solution.py:55
  172.9 15.0 %attention_forward.1 = (bf16[768,512]{1,0:T(8,128)(2,1)}, f32[512,768]{1,0:T(8,128)}, f32[4,2,768]{2,1,0:T(2,128)}) custom-call(s32[3]{0:T(128)} %and_select_fusion.low_ref, s32[1]{0:T(128)} %bitcast.3.live_ref, s32[1,768]{1,0:T(1,128)} %add.459.start_ref, bf16[1536,1536]{1,0:T(8,128)(2,1)} %add_convert_fusion.q_ref.k_ref.v_ref, ...), custom_call_target="tpu_custom_call" | custom-call | flops 1207959552 | bytes 6291456 | tf_op jit(solution)/shard_map/attention_forward/pallas_call | solution.py:216
  194.8 4.5 collective-permute-done.10
  199.3 4.4 collective-permute-done.11
  213.6 7.1 collective-permute-start.22
  224.3 14.3 %collective-permute-done.19 = bf16[1,192,1600]{2,1,0:T(8,128)(2,1)S(1)} collective-permute-done((bf16[1,192,1600]{2,1,0:T(8,128)(2,1)}, bf16[1,192,1600]{2,1,0:T(8,128)(2,1)S(1)}, u32[]{:S(2)}, u32[]{:S(2)}) %collective-permute-start.19) | collective-permute-done | bytes 614432 | tf_op jit(solution)/shard_map/ppermute | solution.py:278
  243.3 4.8 fusion.129
  250.9 32.2 %collective-permute-done.22 = bf16[8,200,832]{2,1,0:T(8,128)(2,1)} collective-permute-done((bf16[8,200,832]{2,1,0:T(8,128)(2,1)}, bf16[8,200,832]{2,1,0:T(8,128)(2,1)}, u32[]{:S(2)}, u32[]{:S(2)}) %collective-permute-start.22) | collective-permute-done | bytes 2662432 | tf_op jit(solution)/shard_map/ppermute | solution.py:278
  283.1 18.2 %convert_reduce_fusion.4 = (f32[832]{0:T(1024)S(1)}, bf16[768,832]{0,1:T(8,128)(2,1)S(1)}, bf16[768,832]{0,1:T(8,128)(2,1)}) fusion(f32[768,832]{0,1:T(8,128)S(1)} %fusion.135, f32[832]{0:T(1024)S(1)} %get-tuple-element.172, bf16[1600,832]{1,0:T(8,128)(2,1)} %bitcast.38, bf16[192,1600]{1,0:T(8,128)(2,1)S(1)} %bitcast.389, ...), kind=kOutput, calls=%fused_computation.70 | convolution fusion | flops 2070527232 | bytes 10238464 | tf_op jit(solution)/shard_map/dot_general | solution.py:55
  302.4 4.5 convolution_convert_fusion.2
  307.0 5.4 fusion.134
  312.4 5.4 convert_reduce_fusion.5
  319.6 4.6 fusion.15
  336.5 4.5 convolution_convert_fusion.3
  342.8 4.5 convolution_convert_fusion.1
  372.4 4.5 collective-permute-done.31
  378.1 27.6 %collective-permute-done.33 = bf16[8,1,200,832]{3,2,1,0:T(8,128)(2,1)} collective-permute-done((bf16[8,1,200,832]{3,2,1,0:T(8,128)(2,1)}, bf16[8,1,200,832]{3,2,1,0:T(8,128)(2,1)}, u32[]{:S(2)}, u32[]{:S(2)}) %collective-permute-start.33) | collective-permute-done | bytes 2662432 | tf_op jit(solution)/shard_map/ppermute | solution.py:278
  405.7 4.2 fusion.4
  409.9 22.3 %attention_backward.1 = bf16[1536,1536]{1,0:T(8,128)(2,1)} custom-call(s32[3]{0:T(128)} %and_select_fusion.low_ref, s32[1]{0:T(128)} %bitcast.3.live_ref, s32[1,768]{1,0:T(1,128)} %add.459.start_ref, bf16[1536,1536]{1,0:T(8,128)(2,1)} %add_convert_fusion.q_ref.k_ref.v_ref, bf16[1536,1536]{1,0:T(8,128)(2,1)} %add_convert_fusion.q_ref.k_ref.v_ref, ...), custom_call_target="tpu_custom_call" | custom-call | flops 3019898880 | bytes 9437184 | tf_op jit(solution)/shard_map/attention_backward/pallas_call | solution.py:242
  438.7 4.1 collective-permute-start.56
  442.9 9.6 %convolution_convert_fusion = bf16[1600,1536]{1,0:T(8,128)(2,1)} fusion(bf16[1536,1536]{1,0:T(8,128)(2,1)S(1)} %bitcast.337, bf16[768,1600]{0,1:T(8,128)(2,1)S(1)} %copy-done.28, bf16[768,1600]{0,1:T(8,128)(2,1)S(1)} %copy-done.26), kind=kOutput, calls=%fused_computation.2 | convolution fusion | flops 7562035200 | bytes 14548992 | tf_op jit(solution)/shard_map/dot_general | solution.py:47
  452.5 26.9 %collective-permute-done.56 = bf16[8,1,200,448]{3,2,1,0:T(8,128)(2,1)} collective-permute-done((bf16[8,1,200,448]{3,2,1,0:T(8,128)(2,1)S(1)}, bf16[8,1,200,448]{3,2,1,0:T(8,128)(2,1)}, u32[]{:S(2)}, u32[]{:S(2)}) %collective-permute-start.56) | collective-permute-done | bytes 1433632 | tf_op jit(solution)/shard_map/ppermute | solution.py:278
  479.4 4.8 fusion.13
  494.5 6.6 convolution_convert_fusion.4
  508.0 4.5 fusion.39
  516.5 7.0 collective-permute-done.26
  526.7 36.9 %collective-permute-done.28 = bf16[1,192,1600]{2,1,0:T(8,128)(2,1)S(1)} collective-permute-done((bf16[1,192,1600]{2,1,0:T(8,128)(2,1)S(1)}, bf16[1,192,1600]{2,1,0:T(8,128)(2,1)S(1)}, u32[]{:S(2)}, u32[]{:S(2)}) %collective-permute-start.28) | collective-permute-done | bytes 614432 | tf_op jit(solution)/shard_map/ppermute | solution.py:278
  563.7 6.9 collective-permute-start.61
  581.0 4.5 copy.95
  587.8 15.4 %collective-permute-done.62 = bf16[2,200,832]{2,1,0:T(8,128)(2,1)} collective-permute-done((bf16[2,200,832]{2,1,0:T(8,128)(2,1)}, bf16[2,200,832]{2,1,0:T(8,128)(2,1)}, u32[]{:S(2)}, u32[]{:S(2)}) %collective-permute-start.62) | collective-permute-done | bytes 665632 | tf_op jit(solution)/shard_map/ppermute | solution.py:278
  606.6 9.9 %collective-permute-done.37 = bf16[1,192,1600]{2,1,0:T(8,128)(2,1)S(1)} collective-permute-done((bf16[1,192,1600]{2,1,0:T(8,128)(2,1)}, bf16[1,192,1600]{2,1,0:T(8,128)(2,1)S(1)}, u32[]{:S(2)}, u32[]{:S(2)}) %collective-permute-start.37) | collective-permute-done | bytes 614432 | tf_op jit(solution)/shard_map/ppermute | solution.py:278
  617.5 4.8 collective-permute-done.41
  635.0 8.4 %collective-permute-done.43 = f32[1,8,1600]{2,1,0:T(8,128)} collective-permute-done((f32[1,8,1600]{2,1,0:T(8,128)}, f32[1,8,1600]{2,1,0:T(8,128)}, u32[]{:S(2)}, u32[]{:S(2)}) %collective-permute-start.43) | collective-permute-done | bytes 51232 | tf_op jit(solution)/shard_map/ppermute | solution.py:278
  644.5 18.8 %collective-permute-start.45 = (f32[9,400]{1,0:T(8,128)S(1)}, f32[9,400]{1,0:T(8,128)S(1)}, u32[]{:S(2)}, u32[]{:S(2)}) collective-permute-start(f32[9,400]{1,0:T(8,128)S(1)} %bitcast.404), channel_id=1, source_target_pairs={{0,16},{8,24},{16,0},{24,8},{1,17},{9,25},{17,1},{25,9},{2,18},{10... | collective-permute-start | bytes 43208 | tf_op jit(solution)/shard_map/ppermute | solution.py:505
  665.4 4.8 collective-permute-start.44
  675.0 16.6 %reduce-scatter.14.cloned.1.call-done = bf16[400,832]{1,0:T(8,128)(2,1)} async-done(((bf16[1600,832]{1,0:T(8,128)(2,1)}), bf16[400,832]{1,0:T(8,128)(2,1)}) %reduce-scatter.14.cloned.1.call-update) | async-done | bytes 665616 | tf_op jit(solution)/shard_map/reduce_scatter | solution.py:427
  697.5 12.2 %collective-permute-done.53 = bf16[1,200,1536]{2,1,0:T(8,128)(2,1)} collective-permute-done((bf16[1,200,1536]{2,1,0:T(8,128)(2,1)}, bf16[1,200,1536]{2,1,0:T(8,128)(2,1)}, u32[]{:S(2)}, u32[]{:S(2)}) %collective-permute-start.53) | collective-permute-done | bytes 614432 | tf_op jit(solution)/shard_map/ppermute | solution.py:278
  712.8 4.7 join_windows.3
  722.0 4.4 copy.96
  727.4 10.3 %join_windows.2 = f32[400,4800]{1,0:T(8,128)} custom-call(s32[1]{0:T(128)} %bitcast.index_ref, bf16[200,1536]{1,0:T(8,128)(2,1)} %get-tuple-element.216.refs_0_, bf16[200,1536]{1,0:T(8,128)(2,1)} %bitcast.395, bf16[200,1536]{1,0:T(8,128)(2,1)} %bitcast.110.refs_2_, bf16[200,1536]{1,0:T(8,128)(2,1)} %bitcast.112.refs_3_, ...), custom_call_target="tpu_custom_call" | custom-call | bytes 5760000 | tf_op jit(solution)/shard_map/join_windows/pallas_call | solution.py:479
  (470 shorter events, 205.4 us)
Async XLA Ops:
  7.2 206.4 %all-gather.4.cloned.1.call-start = ((), (), s32[]{:S(2)}) async-start(), calls=%async_computation.5 | async-start | bytes 3584000 | tf_op jit(solution)/shard_map/all_gather | solution.py:363
  10.4 19.1 %collective-permute-start = (bf16[1,200,1536]{2,1,0:T(8,128)(2,1)}, bf16[1,200,1536]{2,1,0:T(8,128)(2,1)S(1)}, u32[]{:S(2)}, u32[]{:S(2)}) collective-permute-start(bf16[1,200,1536]{2,1,0:T(8,128)(2,1)} %constant_dynamic-slice_fusion.12), channel_id=1, source_target_pairs={{0,8},{8,16},{16,24},{24,0},{1,9},{9,17},{17,25},{25,1},{2,10},{10... | collective-permute-start | bytes 1843208 | tf_op jit(solution)/shard_map/ppermute | solution.py:278
  29.5 213.8 %all-gather.6.cloned.1.call-start = ((), (), s32[]{:S(2)}) async-start(), calls=%async_computation.11 | async-start | bytes 7168000 | tf_op jit(solution)/shard_map/all_gather | solution.py:559
  29.8 16.3 %collective-permute-start.2 = (bf16[9,400]{1,0:T(8,128)(2,1)S(1)}, bf16[9,400]{1,0:T(8,128)(2,1)S(1)}, u32[]{:S(2)}, u32[]{:S(2)}) collective-permute-start(bf16[9,400]{1,0:T(8,128)(2,1)S(1)} %stack.75), channel_id=1, source_target_pairs={{0,8},{8,16},{16,24},{24,0},{1,9},{9,17},{17,25},{25,1},{2,10},{10... | collective-permute-start | bytes 21608 | tf_op jit(solution)/shard_map/ppermute | solution.py:344
  29.9 16.3 %collective-permute-start.3 = (bf16[9,400]{1,0:T(8,128)(2,1)S(1)}, bf16[9,400]{1,0:T(8,128)(2,1)S(1)}, u32[]{:S(2)}, u32[]{:S(2)}) collective-permute-start(bf16[9,400]{1,0:T(8,128)(2,1)S(1)} %stack.75), channel_id=1, source_target_pairs={{0,16},{8,24},{16,0},{24,8},{1,17},{9,25},{17,1},{25,9},{2,18},{10... | collective-permute-start | bytes 21608 | tf_op jit(solution)/shard_map/ppermute | solution.py:344
  33.7 113.5 %collective-permute-start.1 = (bf16[768,1600]{0,1:T(8,128)(2,1)}, bf16[768,1600]{0,1:T(8,128)(2,1)}, u32[]{:S(2)}, u32[]{:S(2)}) collective-permute-start(bf16[768,1600]{0,1:T(8,128)(2,1)} %param.16), channel_id=1, source_target_pairs={{0,4},{1,5},{2,6},{3,7},{8,12},{9,13},{10,14},{11,15},{16,20},{17,... | collective-permute-start | bytes 7372808 | tf_op jit(solution)/shard_map/ppermute | solution.py:578
  47.8 30.9 %collective-permute-start.6 = (bf16[1,200,1536]{2,1,0:T(8,128)(2,1)S(1)}, bf16[1,200,1536]{2,1,0:T(8,128)(2,1)S(1)}, u32[]{:S(2)}, u32[]{:S(2)}) collective-permute-start(bf16[1,200,1536]{2,1,0:T(8,128)(2,1)S(1)} %collective-permute-done), channel_id=1, source_target_pairs={{0,8},{8,16},{16,24},{24,0},{1,9},{9,17},{17,25},{25,1},{2,10},{10... | collective-permute-start | bytes 1843208 | tf_op jit(solution)/shard_map/ppermute | solution.py:278
  50.3 513.4 %reduce-scatter.12.cloned.1.call-start = ((), (), s32[]{:S(2)}) async-start(), calls=%async_computation.9 | async-start | bytes 3584000 | tf_op jit(solution)/shard_map/reduce_scatter | solution.py:427
  50.3 53.4 %collective-permute-start.5 = (bf16[1,200,1536]{2,1,0:T(8,128)(2,1)S(1)}, bf16[1,200,1536]{2,1,0:T(8,128)(2,1)}, u32[]{:S(2)}, u32[]{:S(2)}) collective-permute-start(bf16[1,200,1536]{2,1,0:T(8,128)(2,1)S(1)} %collective-permute-done), channel_id=1, source_target_pairs={{0,4},{4,0},{1,5},{5,1},{2,6},{6,2},{3,7},{7,3},{8,12},{12,8},{9,1... | collective-permute-start | bytes 1843208 | tf_op jit(solution)/shard_map/ppermute | solution.py:278
  78.7 32.0 %collective-permute-start.13 = (bf16[2,200,448]{2,1,0:T(8,128)(2,1)S(1)}, bf16[2,200,448]{2,1,0:T(8,128)(2,1)}, u32[]{:S(2)}, u32[]{:S(2)}) collective-permute-start(bf16[2,200,448]{2,1,0:T(8,128)(2,1)S(1)} %bitcast.373), channel_id=1, source_target_pairs={{0,8},{8,16},{16,24},{24,0},{1,9},{9,17},{17,25},{25,1},{2,10},{10... | collective-permute-start | bytes 1075208 | tf_op jit(solution)/shard_map/ppermute | solution.py:278
  90.3 50.3 %collective-permute-start.14 = (bf16[2,200,448]{2,1,0:T(8,128)(2,1)S(1)}, bf16[2,200,448]{2,1,0:T(8,128)(2,1)}, u32[]{:S(2)}, u32[]{:S(2)}) collective-permute-start(bf16[2,200,448]{2,1,0:T(8,128)(2,1)S(1)} %bitcast.374), channel_id=1, source_target_pairs={{0,16},{8,24},{16,0},{24,8},{1,17},{9,25},{17,1},{25,9},{2,18},{10... | collective-permute-start | bytes 1075208 | tf_op jit(solution)/shard_map/ppermute | solution.py:278
  102.5 44.6 %collective-permute-start.7 = (bf16[1,200,1536]{2,1,0:T(8,128)(2,1)S(1)}, bf16[1,200,1536]{2,1,0:T(8,128)(2,1)S(1)}, u32[]{:S(2)}, u32[]{:S(2)}) collective-permute-start(bf16[1,200,1536]{2,1,0:T(8,128)(2,1)S(1)} %copy-done.45), channel_id=1, source_target_pairs={{0,4},{4,0},{1,5},{5,1},{2,6},{6,2},{3,7},{7,3},{8,12},{12,8},{9,1... | collective-permute-start | bytes 1843208 | tf_op jit(solution)/shard_map/ppermute | solution.py:278
  103.7 42.1 %collective-permute-start.8 = (bf16[1,200,1536]{2,1,0:T(8,128)(2,1)S(1)}, bf16[1,200,1536]{2,1,0:T(8,128)(2,1)S(1)}, u32[]{:S(2)}, u32[]{:S(2)}) collective-permute-start(bf16[1,200,1536]{2,1,0:T(8,128)(2,1)S(1)} %copy-done.45), channel_id=1, source_target_pairs={{0,8},{8,16},{16,24},{24,0},{1,9},{9,17},{17,25},{25,1},{2,10},{10... | collective-permute-start | bytes 1843208 | tf_op jit(solution)/shard_map/ppermute | solution.py:278
  110.7 32.7 %collective-permute-start.15 = (bf16[2,200,448]{2,1,0:T(8,128)(2,1)S(1)}, bf16[2,200,448]{2,1,0:T(8,128)(2,1)S(1)}, u32[]{:S(2)}, u32[]{:S(2)}) collective-permute-start(bf16[2,200,448]{2,1,0:T(8,128)(2,1)S(1)} %bitcast.375), channel_id=1, source_target_pairs={{0,24},{8,0},{16,8},{24,16},{1,25},{9,1},{17,9},{25,17},{2,26},{10... | collective-permute-start | bytes 1075208 | tf_op jit(solution)/shard_map/ppermute | solution.py:278
  144.1 43.8 %collective-permute-start.16 = (bf16[8,200,448]{2,1,0:T(8,128)(2,1)}, bf16[8,200,448]{2,1,0:T(8,128)(2,1)}, u32[]{:S(2)}, u32[]{:S(2)}) collective-permute-start(bf16[8,200,448]{2,1,0:T(8,128)(2,1)} %bitcast.26), channel_id=1, source_target_pairs={{0,2},{1,3},{2,0},{3,1},{4,6},{5,7},{6,4},{7,5},{8,10},{9,11},{10,... | collective-permute-start | bytes 4300808 | tf_op jit(solution)/shard_map/ppermute | solution.py:278
  145.8 60.9 %collective-permute-start.18 = (bf16[8,200,448]{2,1,0:T(8,128)(2,1)}, bf16[8,200,448]{2,1,0:T(8,128)(2,1)}, u32[]{:S(2)}, u32[]{:S(2)}) collective-permute-start(bf16[8,200,448]{2,1,0:T(8,128)(2,1)} %bitcast.26), channel_id=1, source_target_pairs={{0,1},{1,0},{2,3},{3,2},{4,5},{5,4},{6,7},{7,6},{8,9},{9,8},{10,11... | collective-permute-start | bytes 4300808 | tf_op jit(solution)/shard_map/ppermute | solution.py:278
  145.8 16.3 %collective-permute-start.9 = (bf16[1,200,1536]{2,1,0:T(8,128)(2,1)S(1)}, bf16[1,200,1536]{2,1,0:T(8,128)(2,1)S(1)}, u32[]{:S(2)}, u32[]{:S(2)}) collective-permute-start(bf16[1,200,1536]{2,1,0:T(8,128)(2,1)S(1)} %collective-permute-done.8), channel_id=1, source_target_pairs={{0,4},{4,0},{1,5},{5,1},{2,6},{6,2},{3,7},{7,3},{8,12},{12,8},{9,1... | collective-permute-start | bytes 1843208 | tf_op jit(solution)/shard_map/ppermute | solution.py:278
  188.0 20.7 %collective-permute-start.17 = (bf16[8,200,448]{2,1,0:T(8,128)(2,1)}, bf16[8,200,448]{2,1,0:T(8,128)(2,1)}, u32[]{:S(2)}, u32[]{:S(2)}) collective-permute-start(bf16[8,200,448]{2,1,0:T(8,128)(2,1)} %bitcast.28), channel_id=1, source_target_pairs={{0,1},{1,0},{2,3},{3,2},{4,5},{5,4},{6,7},{7,6},{8,9},{9,8},{10,11... | collective-permute-start | bytes 4300808 | tf_op jit(solution)/shard_map/ppermute | solution.py:278
  213.6 69.4 %collective-permute-start.22 = (bf16[8,200,832]{2,1,0:T(8,128)(2,1)}, bf16[8,200,832]{2,1,0:T(8,128)(2,1)}, u32[]{:S(2)}, u32[]{:S(2)}) collective-permute-start(bf16[8,200,832]{2,1,0:T(8,128)(2,1)} %bitcast.421), channel_id=1, source_target_pairs={{0,4},{4,0},{1,5},{5,1},{2,6},{6,2},{3,7},{7,3},{8,12},{12,8},{9,1... | collective-permute-start | bytes 7987208 | tf_op jit(solution)/shard_map/ppermute | solution.py:278
  221.9 16.8 %collective-permute-start.19 = (bf16[1,192,1600]{2,1,0:T(8,128)(2,1)}, bf16[1,192,1600]{2,1,0:T(8,128)(2,1)S(1)}, u32[]{:S(2)}, u32[]{:S(2)}) collective-permute-start(bf16[1,192,1600]{2,1,0:T(8,128)(2,1)} %fusion.182), channel_id=1, source_target_pairs={{0,2},{1,3},{2,0},{3,1},{4,6},{5,7},{6,4},{7,5},{8,10},{9,11},{10,... | collective-permute-start | bytes 1843208 | tf_op jit(solution)/shard_map/ppermute | solution.py:278
  306.9 263.6 %reduce-scatter.10.cloned.1.call-start = ((), (), s32[]{:S(2)}) async-start(), calls=%async_computation.8 | async-start | bytes 3584000 | tf_op jit(solution)/shard_map/reduce_scatter | solution.py:427
  333.9 17.9 %collective-permute-start.24 = (bf16[1,192,1600]{2,1,0:T(8,128)(2,1)S(1)}, bf16[1,192,1600]{2,1,0:T(8,128)(2,1)}, u32[]{:S(2)}, u32[]{:S(2)}) collective-permute-start(bf16[1,192,1600]{2,1,0:T(8,128)(2,1)S(1)} %fusion.71), channel_id=1, source_target_pairs={{0,2},{1,3},{2,0},{3,1},{4,6},{5,7},{6,4},{7,5},{8,10},{9,11},{10,... | collective-permute-start | bytes 1843208 | tf_op jit(solution)/shard_map/ppermute | solution.py:278
  341.1 64.7 %collective-permute-start.33 = (bf16[8,1,200,832]{3,2,1,0:T(8,128)(2,1)}, bf16[8,1,200,832]{3,2,1,0:T(8,128)(2,1)}, u32[]{:S(2)}, u32[]{:S(2)}) collective-permute-start(bf16[8,1,200,832]{3,2,1,0:T(8,128)(2,1)} %bitcast.69), channel_id=1, source_target_pairs={{0,4},{4,0},{1,5},{5,1},{2,6},{6,2},{3,7},{7,3},{8,12},{12,8},{9,1... | collective-permute-start | bytes 7987208 | tf_op jit(solution)/shard_map/ppermute | solution.py:278
  347.4 279.8 %reduce-scatter.8.cloned.1.call-start = ((), (), s32[]{:S(2)}) async-start(), calls=%async_computation.7 | async-start | bytes 2048000 | tf_op jit(solution)/shard_map/reduce_scatter | solution.py:427
  434.7 17.8 %collective-permute-start.55 = (bf16[8,1,200,448]{3,2,1,0:T(8,128)(2,1)}, bf16[8,1,200,448]{3,2,1,0:T(8,128)(2,1)}, u32[]{:S(2)}, u32[]{:S(2)}) collective-permute-start(bf16[8,1,200,448]{3,2,1,0:T(8,128)(2,1)} %bitcast.282), channel_id=1, source_target_pairs={{0,1},{1,0},{2,3},{3,2},{4,5},{5,4},{6,7},{7,6},{8,9},{9,8},{10,11... | collective-permute-start | bytes 4300808 | tf_op jit(solution)/shard_map/ppermute | solution.py:278
  438.7 40.7 %collective-permute-start.56 = (bf16[8,1,200,448]{3,2,1,0:T(8,128)(2,1)S(1)}, bf16[8,1,200,448]{3,2,1,0:T(8,128)(2,1)}, u32[]{:S(2)}, u32[]{:S(2)}) collective-permute-start(bf16[8,1,200,448]{3,2,1,0:T(8,128)(2,1)S(1)} %bitcast.372), channel_id=1, source_target_pairs={{0,2},{1,3},{2,0},{3,1},{4,6},{5,7},{6,4},{7,5},{8,10},{9,11},{10,... | collective-permute-start | bytes 4300808 | tf_op jit(solution)/shard_map/ppermute | solution.py:278
  484.2 146.3 %reduce-scatter.6.cloned.1.call-start = ((), (), s32[]{:S(2)}) async-start(), calls=%async_computation.6 | async-start | bytes 6144000 | tf_op jit(solution)/shard_map/reduce_scatter | solution.py:427
  484.8 206.8 %reduce-scatter.14.cloned.1.call-start = ((), (), s32[]{:S(2)}) async-start(), calls=%async_computation.10 | async-start | bytes 3584000 | tf_op jit(solution)/shard_map/reduce_scatter | solution.py:427
  506.2 17.3 %collective-permute-start.26 = (bf16[1,192,1600]{2,1,0:T(8,128)(2,1)S(1)}, bf16[1,192,1600]{2,1,0:T(8,128)(2,1)S(1)}, u32[]{:S(2)}, u32[]{:S(2)}) collective-permute-start(bf16[1,192,1600]{2,1,0:T(8,128)(2,1)S(1)} %fusion.72), channel_id=1, source_target_pairs={{0,2},{1,3},{2,0},{3,1},{4,6},{5,7},{6,4},{7,5},{8,10},{9,11},{10,... | collective-permute-start | bytes 1843208 | tf_op jit(solution)/shard_map/ppermute | solution.py:278
  516.2 54.4 %collective-permute-start.36 = (bf16[2,192,1600]{2,1,0:T(8,128)(2,1)}, bf16[2,192,1600]{2,1,0:T(8,128)(2,1)}, u32[]{:S(2)}, u32[]{:S(2)}) collective-permute-start(bf16[2,192,1600]{2,1,0:T(8,128)(2,1)} %bitcast.89), channel_id=1, source_target_pairs={{0,2},{1,3},{2,0},{3,1},{4,6},{5,7},{6,4},{7,5},{8,10},{9,11},{10,... | collective-permute-start | bytes 3686408 | tf_op jit(solution)/shard_map/ppermute | solution.py:278
  523.9 39.8 %collective-permute-start.28 = (bf16[1,192,1600]{2,1,0:T(8,128)(2,1)S(1)}, bf16[1,192,1600]{2,1,0:T(8,128)(2,1)S(1)}, u32[]{:S(2)}, u32[]{:S(2)}) collective-permute-start(bf16[1,192,1600]{2,1,0:T(8,128)(2,1)S(1)} %bitcast.367), channel_id=1, source_target_pairs={{0,2},{1,3},{2,0},{3,1},{4,6},{5,7},{6,4},{7,5},{8,10},{9,11},{10,... | collective-permute-start | bytes 1843208 | tf_op jit(solution)/shard_map/ppermute | solution.py:278
  526.6 50.4 %collective-permute-start.27 = (bf16[1,192,1600]{2,1,0:T(8,128)(2,1)S(1)}, bf16[1,192,1600]{2,1,0:T(8,128)(2,1)}, u32[]{:S(2)}, u32[]{:S(2)}) collective-permute-start(bf16[1,192,1600]{2,1,0:T(8,128)(2,1)S(1)} %bitcast.368), channel_id=1, source_target_pairs={{0,1},{1,0},{2,3},{3,2},{4,5},{5,4},{6,7},{7,6},{8,9},{9,8},{10,11... | collective-permute-start | bytes 1843208 | tf_op jit(solution)/shard_map/ppermute | solution.py:278
  563.7 24.1 %collective-permute-start.61 = (bf16[2,200,832]{2,1,0:T(8,128)(2,1)}, bf16[2,200,832]{2,1,0:T(8,128)(2,1)}, u32[]{:S(2)}, u32[]{:S(2)}) collective-permute-start(bf16[2,200,832]{2,1,0:T(8,128)(2,1)} %bitcast.378), channel_id=1, source_target_pairs={{0,4},{4,0},{1,5},{5,1},{2,6},{6,2},{3,7},{7,3},{8,12},{12,8},{9,1... | collective-permute-start | bytes 1996808 | tf_op jit(solution)/shard_map/ppermute | solution.py:278
  570.5 32.6 %collective-permute-start.62 = (bf16[2,200,832]{2,1,0:T(8,128)(2,1)}, bf16[2,200,832]{2,1,0:T(8,128)(2,1)}, u32[]{:S(2)}, u32[]{:S(2)}) collective-permute-start(bf16[2,200,832]{2,1,0:T(8,128)(2,1)} %bitcast.379), channel_id=1, source_target_pairs={{0,4},{4,0},{1,5},{5,1},{2,6},{6,2},{3,7},{7,3},{8,12},{12,8},{9,1... | collective-permute-start | bytes 1996808 | tf_op jit(solution)/shard_map/ppermute | solution.py:278
  575.6 40.9 %collective-permute-start.37 = (bf16[1,192,1600]{2,1,0:T(8,128)(2,1)}, bf16[1,192,1600]{2,1,0:T(8,128)(2,1)S(1)}, u32[]{:S(2)}, u32[]{:S(2)}) collective-permute-start(bf16[1,192,1600]{2,1,0:T(8,128)(2,1)} %fusion.73), channel_id=1, source_target_pairs={{4,0},{5,1},{6,2},{7,3},{12,8},{13,9},{14,10},{15,11},{20,16},{21,... | collective-permute-start | bytes 1843208 | tf_op jit(solution)/shard_map/ppermute | solution.py:278
  625.3 71.0 %collective-permute-start.39 = (bf16[1,192,1600]{2,1,0:T(8,128)(2,1)S(1)}, bf16[1,192,1600]{2,1,0:T(8,128)(2,1)}, u32[]{:S(2)}, u32[]{:S(2)}) collective-permute-start(bf16[1,192,1600]{2,1,0:T(8,128)(2,1)S(1)} %bitcast.365), channel_id=1, source_target_pairs={{0,2},{1,3},{2,0},{3,1},{4,6},{5,7},{6,4},{7,5},{8,10},{9,11},{10,... | collective-permute-start | bytes 1843208 | tf_op jit(solution)/shard_map/ppermute | solution.py:278
  627.1 17.4 %collective-permute-start.57 = (bf16[2,200,448]{2,1,0:T(8,128)(2,1)}, bf16[2,200,448]{2,1,0:T(8,128)(2,1)}, u32[]{:S(2)}, u32[]{:S(2)}) collective-permute-start(bf16[2,200,448]{2,1,0:T(8,128)(2,1)} %bitcast.400), channel_id=1, source_target_pairs={{0,4},{4,0},{1,5},{5,1},{2,6},{6,2},{3,7},{7,3},{8,12},{12,8},{9,1... | collective-permute-start | bytes 1075208 | tf_op jit(solution)/shard_map/ppermute | solution.py:278
  633.0 32.4 %collective-permute-start.51 = (bf16[1,200,1536]{2,1,0:T(8,128)(2,1)}, bf16[1,200,1536]{2,1,0:T(8,128)(2,1)}, u32[]{:S(2)}, u32[]{:S(2)}) collective-permute-start(bf16[1,200,1536]{2,1,0:T(8,128)(2,1)} %get-tuple-element.217), channel_id=1, source_target_pairs={{0,4},{4,0},{1,5},{5,1},{2,6},{6,2},{3,7},{7,3},{8,12},{12,8},{9,1... | collective-permute-start | bytes 1843208 | tf_op jit(solution)/shard_map/ppermute | solution.py:278
  634.4 35.8 %collective-permute-start.47 = (bf16[1,200,1536]{2,1,0:T(8,128)(2,1)}, bf16[1,200,1536]{2,1,0:T(8,128)(2,1)}, u32[]{:S(2)}, u32[]{:S(2)}) collective-permute-start(bf16[1,200,1536]{2,1,0:T(8,128)(2,1)} %get-tuple-element.218), channel_id=1, source_target_pairs={{0,4},{4,0},{1,5},{5,1},{2,6},{6,2},{3,7},{7,3},{8,12},{12,8},{9,1... | collective-permute-start | bytes 1843208 | tf_op jit(solution)/shard_map/ppermute | solution.py:278
  644.4 28.5 %collective-permute-start.46 = (f32[9,400]{1,0:T(8,128)S(1)}, f32[9,400]{1,0:T(8,128)S(1)}, u32[]{:S(2)}, u32[]{:S(2)}) collective-permute-start(f32[9,400]{1,0:T(8,128)S(1)} %bitcast.405), channel_id=1, source_target_pairs={{0,24},{8,0},{16,8},{24,16},{1,25},{9,1},{17,9},{25,17},{2,26},{10... | collective-permute-start | bytes 43208 | tf_op jit(solution)/shard_map/ppermute | solution.py:505
  644.5 47.1 %collective-permute-start.45 = (f32[9,400]{1,0:T(8,128)S(1)}, f32[9,400]{1,0:T(8,128)S(1)}, u32[]{:S(2)}, u32[]{:S(2)}) collective-permute-start(f32[9,400]{1,0:T(8,128)S(1)} %bitcast.404), channel_id=1, source_target_pairs={{0,16},{8,24},{16,0},{24,8},{1,17},{9,25},{17,1},{25,9},{2,18},{10... | collective-permute-start | bytes 43208 | tf_op jit(solution)/shard_map/ppermute | solution.py:505
  665.4 27.7 %collective-permute-start.44 = (f32[9,400]{1,0:T(8,128)S(1)}, f32[9,400]{1,0:T(8,128)S(1)}, u32[]{:S(2)}, u32[]{:S(2)}) collective-permute-start(f32[9,400]{1,0:T(8,128)S(1)} %bitcast.403), channel_id=1, source_target_pairs={{0,8},{8,16},{16,24},{24,0},{1,9},{9,17},{17,25},{25,1},{2,10},{10... | collective-permute-start | bytes 43208 | tf_op jit(solution)/shard_map/ppermute | solution.py:505
  670.2 22.9 %collective-permute-start.59 = (bf16[2,200,448]{2,1,0:T(8,128)(2,1)}, bf16[2,200,448]{2,1,0:T(8,128)(2,1)}, u32[]{:S(2)}, u32[]{:S(2)}) collective-permute-start(bf16[2,200,448]{2,1,0:T(8,128)(2,1)} %bitcast.132), channel_id=1, source_target_pairs={{0,2},{1,3},{2,0},{3,1},{4,6},{5,7},{6,4},{7,5},{8,10},{9,11},{10,... | collective-permute-start | bytes 1075208 | tf_op jit(solution)/shard_map/ppermute | solution.py:278
  672.9 23.6 %collective-permute-start.49 = (bf16[1,200,1536]{2,1,0:T(8,128)(2,1)}, bf16[1,200,1536]{2,1,0:T(8,128)(2,1)}, u32[]{:S(2)}, u32[]{:S(2)}) collective-permute-start(bf16[1,200,1536]{2,1,0:T(8,128)(2,1)} %bitcast.108), channel_id=1, source_target_pairs={{0,2},{1,3},{2,0},{3,1},{4,6},{5,7},{6,4},{7,5},{8,10},{9,11},{10,... | collective-permute-start | bytes 1843208 | tf_op jit(solution)/shard_map/ppermute | solution.py:278
  691.6 18.1 %collective-permute-start.63 = (bf16[2,200,832]{2,1,0:T(8,128)(2,1)}, bf16[2,200,832]{2,1,0:T(8,128)(2,1)S(1)}, u32[]{:S(2)}, u32[]{:S(2)}) collective-permute-start(bf16[2,200,832]{2,1,0:T(8,128)(2,1)} %bitcast.369), channel_id=1, source_target_pairs={{0,4},{4,0},{1,5},{5,1},{2,6},{6,2},{3,7},{7,3},{8,12},{12,8},{9,1... | collective-permute-start | bytes 1996808 | tf_op jit(solution)/shard_map/ppermute | solution.py:278
  693.1 17.1 %collective-permute-start.38 = (bf16[1,192,1600]{2,1,0:T(8,128)(2,1)S(1)}, bf16[1,192,1600]{2,1,0:T(8,128)(2,1)S(1)}, u32[]{:S(2)}, u32[]{:S(2)}) collective-permute-start(bf16[1,192,1600]{2,1,0:T(8,128)(2,1)S(1)} %bitcast.366), channel_id=1, source_target_pairs={{0,1},{1,0},{2,3},{3,2},{4,5},{5,4},{6,7},{7,6},{8,9},{9,8},{10,11... | collective-permute-start | bytes 1843208 | tf_op jit(solution)/shard_map/ppermute | solution.py:278
  693.1 16.6 %collective-permute-start.53 = (bf16[1,200,1536]{2,1,0:T(8,128)(2,1)}, bf16[1,200,1536]{2,1,0:T(8,128)(2,1)}, u32[]{:S(2)}, u32[]{:S(2)}) collective-permute-start(bf16[1,200,1536]{2,1,0:T(8,128)(2,1)} %bitcast.115), channel_id=1, source_target_pairs={{0,2},{1,3},{2,0},{3,1},{4,6},{5,7},{6,4},{7,5},{8,10},{9,11},{10,... | collective-permute-start | bytes 1843208 | tf_op jit(solution)/shard_map/ppermute | solution.py:278
  709.7 16.7 %collective-permute-start.48 = (bf16[1,200,1536]{2,1,0:T(8,128)(2,1)}, bf16[1,200,1536]{2,1,0:T(8,128)(2,1)S(1)}, u32[]{:S(2)}, u32[]{:S(2)}) collective-permute-start(bf16[1,200,1536]{2,1,0:T(8,128)(2,1)} %bitcast.108), channel_id=1, source_target_pairs={{0,1},{1,0},{2,3},{3,2},{4,5},{5,4},{6,7},{7,6},{8,9},{9,8},{10,11... | collective-permute-start | bytes 1843208 | tf_op jit(solution)/shard_map/ppermute | solution.py:278
  (104 other events, 1399.8 us)
Sparse Core Ops, SparseCore 0:
  29.7 106.6 all-gather.3
  137.9 105.3 all-gather.5
  307.1 66.9 reduce-scatter.11
  376.2 55.9 reduce-scatter.9
  484.3 56.5 reduce-scatter.7
  543.1 87.3 reduce-scatter.5
  632.8 58.7 reduce-scatter.13

commit v3 on v2

--- a/solution.py
+++ b/solution.py
@@ -427,8 +427,8 @@
     return row_major(lax.psum_scatter(row_major(both), "fsdp", scatter_dimension=0, tiled=True))
 
 
-def finish_rows(terms, chunks):
-    mine = spread_fsdp(terms)
+def finish_rows(terms, chunks, after=()):
+    mine = tied(spread_fsdp(terms), *after)
     chunks = chunks if mine.shape[0] % (8 * chunks) == 0 else 1
     rows, out = mine.shape[0] // chunks, []
     for i in range(chunks):
@@ -655,7 +655,8 @@
     grad_mixed = tied(grad_mixed, down_kept)
     grads = attention_backward(low, live, start, joined, grad_mixed, turned, log_total)
     grad_in = row_major(dot_rows(normed_all, grads).astype(bf16))
-    shard_in = join_windows(finish_rows(grad_in, 2), me, step, reach)
+    chunks_in = finish_rows(grad_in, 2)
+    shard_in = join_windows(chunks_in, me, step, reach)
 
     late_mixture, late_windows = tied((mixture, branch_windows), grads)
 
@@ -667,7 +668,9 @@
     far = (branch_product(2) + come[1]).astype(bf16)
     come = across(far, "tp", 2)
     near = (near + come.astype(f32)).astype(bf16).reshape(width, reach)
-    shard_out = join_windows(finish_rows(tied(near, grad_in), 1), me, step, reach)
+    shard_out = join_windows(
+        finish_rows(tied(near, grad_in), 1, (chunks_in[-1][0],)), me, step, reach
+    )
     result = natural(tied(result, grads), me, bf16)
 
     both = jnp.stack([grads[rows:].reshape(members, few, -1), grads[:rows].reshape(members, few, -1)], 1)

time: 760 us -> 744 us (0.979)
  matrix products: 126 us -> 116 us
    ppermute x57, waiting for transfers between devices: 302 us -> 321 us  [moved(): lax.ppermute(row_major(cut_rows(values)), axis, pairs)]
    reduce_scatter x5, waiting for transfers between devices: 18.9 us -> 0.01 us  [spread_fsdp(): lax.psum_scatter(row_major(both), 'fsdp', scatter_dimension=0, tiled=True)]
    dot_general x9, matrix products: 50.4 us -> 40.1 us  [dot(): return jnp.dot(left, right, preferred_element_type=f32)]
    unnamed x168 -> x166, local copies, waits for them, and re-layouts: 19.1 us -> 18.2 us
  transfers between devices with their start and end apart: 71 -> 71, of which waited for: 28 -> 31; matrix products, arithmetic and copies ran while one was open for 28% -> 28% of each run, Pallas kernels for 7% -> 7%
where the time goes in v3:
time: 744 us; the launch traced here: 729 us
  waiting for transfers between devices  324 us (44%)
  matrix products  116 us (16%)
  starting transfers between devices  99.7 us (13%)
  other arithmetic  61.7 us (8%)
  Pallas kernels  59.6 us (8%)
  local copies, waits for them, and re-layouts  52.5 us (7%)
  between operations  16.3 us (2%)
    ppermute x57, waiting for transfers between devices, moved(): lax.ppermute(row_major(cut_rows(values)), axis, pairs)  321 us
    ppermute x57, starting transfers between devices, moved(): lax.ppermute(row_major(cut_rows(values)), axis, pairs)  72.3 us
    dot_general x14, matrix products, dot_lanes(): lax.dot_general(left, right, (((1,), (1,)), ((), ())), preferred_element_...  44.6 us
    dot_general x9, matrix products, dot(): return jnp.dot(left, right, preferred_element_type=f32)  40.1 us
    dot_general x9, matrix products, dot_rows(): lax.dot_general(left, right, (((0,), (0,)), ((), ())), preferred_element_...  31.2 us
    pallas_call x1, Pallas kernels, attention_backward(): pl.pallas_call(backward_kernel, grid=(pairs, 3), in_specs=attention_specs...  22.2 us
    unnamed x166, local copies, waits for them, and re-layouts  18.2 us
    ppermute x3, starting transfers between devices, scatter_vectors(): lax.ppermute(piece, 'fsdp', [(i, (i + back) % size) for i in range(size)])  17.7 us
  transfers between devices with their start and end apart: 71, of which 31 were waited for; matrix products, arithmetic and copies ran while one was open for 28% of the time, Pallas kernels for 7%

profile of v3, /device:TPU:0, one launch (start us, length us, event | category | flops | bytes accessed | tf_op | source)
XLA Modules:
  0.0 729.4 jit_solution(14368639911825870049)
XLA Ops:
  15.7 13.8 %collective-permute-done = bf16[1,200,1536]{2,1,0:T(8,128)(2,1)S(1)} collective-permute-done((bf16[1,200,1536]{2,1,0:T(8,128)(2,1)}, bf16[1,200,1536]{2,1,0:T(8,128)(2,1)S(1)}, u32[]{:S(2)}, u32[]{:S(2)}) %collective-permute-start) | collective-permute-done | bytes 614432 | tf_op jit(solution)/shard_map/ppermute | solution.py:278
  33.7 4.8 collective-permute-start.1
  50.7 27.4 %collective-permute-done.6 = bf16[1,200,1536]{2,1,0:T(8,128)(2,1)S(1)} collective-permute-done((bf16[1,200,1536]{2,1,0:T(8,128)(2,1)S(1)}, bf16[1,200,1536]{2,1,0:T(8,128)(2,1)S(1)}, u32[]{:S(2)}, u32[]{:S(2)}) %collective-permute-start.6) | collective-permute-done | bytes 614432 | tf_op jit(solution)/shard_map/ppermute | solution.py:278
  78.1 11.7 %collective-permute-start.13 = (bf16[2,200,448]{2,1,0:T(8,128)(2,1)S(1)}, bf16[2,200,448]{2,1,0:T(8,128)(2,1)}, u32[]{:S(2)}, u32[]{:S(2)}) collective-permute-start(bf16[2,200,448]{2,1,0:T(8,128)(2,1)S(1)} %bitcast.376), channel_id=1, source_target_pairs={{0,8},{8,16},{16,24},{24,0},{1,9},{9,17},{17,25},{25,1},{2,10},{10... | collective-permute-start | bytes 1075208 | tf_op jit(solution)/shard_map/ppermute | solution.py:278
  93.0 4.5 copy.88
  105.9 4.8 collective-permute-done.13
  113.2 27.4 %collective-permute-done.14 = bf16[2,200,448]{2,1,0:T(8,128)(2,1)} collective-permute-done((bf16[2,200,448]{2,1,0:T(8,128)(2,1)S(1)}, bf16[2,200,448]{2,1,0:T(8,128)(2,1)}, u32[]{:S(2)}, u32[]{:S(2)}) %collective-permute-start.14) | collective-permute-done | bytes 358432 | tf_op jit(solution)/shard_map/ppermute | solution.py:278
  155.8 6.4 collective-permute-done.9
  162.2 10.9 %add_convert_fusion.q_ref.k_ref.v_ref = bf16[1536,1536]{1,0:T(8,128)(2,1)} fusion(bf16[1600,1536]{1,0:T(8,128)(2,1)S(1)} %bitcast.354, f32[1536]{0:T(1024)S(1)} %pad_maximum_fusion.11, bf16[768,1600]{0,1:T(8,128)(2,1)S(1)} %get-tuple-element.262, bf16[768,1600]{0,1:T(8,128)(2,1)S(1)} %get-tuple-element.261), kind=kOutput, calls=%fused_computation.1 | convolution fusion | flops 7564296192 | bytes 14555136 | tf_op jit(solution)/shard_map/dot_general | solution.py:55
  173.1 14.9 %attention_forward.1 = (bf16[768,512]{1,0:T(8,128)(2,1)}, f32[512,768]{1,0:T(8,128)}, f32[4,2,768]{2,1,0:T(2,128)}) custom-call(s32[3]{0:T(128)} %and_select_fusion.low_ref, s32[1]{0:T(128)} %bitcast.3.live_ref, s32[1,768]{1,0:T(1,128)} %add.459.start_ref, bf16[1536,1536]{1,0:T(8,128)(2,1)} %add_convert_fusion.q_ref.k_ref.v_ref, ...), custom_call_target="tpu_custom_call" | custom-call | flops 1207959552 | bytes 6291456 | tf_op jit(solution)/shard_map/attention_forward/pallas_call | solution.py:216
  194.8 4.5 collective-permute-done.10
  199.3 4.4 collective-permute-done.11
  212.7 7.4 %collective-permute-start.22 = (bf16[8,200,832]{2,1,0:T(8,128)(2,1)}, bf16[8,200,832]{2,1,0:T(8,128)(2,1)}, u32[]{:S(2)}, u32[]{:S(2)}) collective-permute-start(bf16[8,200,832]{2,1,0:T(8,128)(2,1)} %bitcast.423), channel_id=1, source_target_pairs={{0,4},{4,0},{1,5},{5,1},{2,6},{6,2},{3,7},{7,3},{8,12},{12,8},{9,1... | collective-permute-start | bytes 7987208 | tf_op jit(solution)/shard_map/ppermute | solution.py:278
  223.7 14.4 %collective-permute-done.19 = bf16[1,192,1600]{2,1,0:T(8,128)(2,1)S(1)} collective-permute-done((bf16[1,192,1600]{2,1,0:T(8,128)(2,1)}, bf16[1,192,1600]{2,1,0:T(8,128)(2,1)S(1)}, u32[]{:S(2)}, u32[]{:S(2)}) %collective-permute-start.19) | collective-permute-done | bytes 614432 | tf_op jit(solution)/shard_map/ppermute | solution.py:278
  244.0 4.8 fusion.129
  251.6 30.9 %collective-permute-done.22 = bf16[8,200,832]{2,1,0:T(8,128)(2,1)} collective-permute-done((bf16[8,200,832]{2,1,0:T(8,128)(2,1)}, bf16[8,200,832]{2,1,0:T(8,128)(2,1)}, u32[]{:S(2)}, u32[]{:S(2)}) %collective-permute-start.22) | collective-permute-done | bytes 2662432 | tf_op jit(solution)/shard_map/ppermute | solution.py:278
  282.5 7.8 %convert_reduce_fusion.4 = (f32[832]{0:T(1024)S(1)}, bf16[768,832]{0,1:T(8,128)(2,1)S(1)}, bf16[768,832]{0,1:T(8,128)(2,1)}) fusion(f32[768,832]{0,1:T(8,128)S(1)} %fusion.135, f32[832]{0:T(1024)S(1)} %get-tuple-element.174, bf16[1600,832]{1,0:T(8,128)(2,1)} %bitcast.38, bf16[192,1600]{1,0:T(8,128)(2,1)S(1)} %bitcast.392, ...), kind=kOutput, calls=%fused_computation.70 | convolution fusion | flops 2070527232 | bytes 10238464 | tf_op jit(solution)/shard_map/dot_general | solution.py:55
  291.3 4.5 convolution_convert_fusion.2
  296.0 5.4 fusion.134
  301.4 5.4 convert_reduce_fusion.5
  308.6 4.5 fusion.15
  325.4 4.4 convolution_convert_fusion.3
  331.6 4.4 convolution_convert_fusion.1
  336.3 4.2 collective-permute-done.24
  361.2 4.5 collective-permute-done.31
  366.9 27.5 %collective-permute-done.33 = bf16[8,1,200,832]{3,2,1,0:T(8,128)(2,1)} collective-permute-done((bf16[8,1,200,832]{3,2,1,0:T(8,128)(2,1)}, bf16[8,1,200,832]{3,2,1,0:T(8,128)(2,1)}, u32[]{:S(2)}, u32[]{:S(2)}) %collective-permute-start.33) | collective-permute-done | bytes 2662432 | tf_op jit(solution)/shard_map/ppermute | solution.py:278
  394.4 4.2 fusion.4
  398.6 22.2 %attention_backward.1 = bf16[1536,1536]{1,0:T(8,128)(2,1)} custom-call(s32[3]{0:T(128)} %and_select_fusion.low_ref, s32[1]{0:T(128)} %bitcast.3.live_ref, s32[1,768]{1,0:T(1,128)} %add.459.start_ref, bf16[1536,1536]{1,0:T(8,128)(2,1)} %add_convert_fusion.q_ref.k_ref.v_ref, bf16[1536,1536]{1,0:T(8,128)(2,1)} %add_convert_fusion.q_ref.k_ref.v_ref, ...), custom_call_target="tpu_custom_call" | custom-call | flops 3019898880 | bytes 9437184 | tf_op jit(solution)/shard_map/attention_backward/pallas_call | solution.py:242
  420.8 12.5 %convolution_convert_fusion = bf16[1600,1536]{1,0:T(8,128)(2,1)} fusion(bf16[1536,1536]{1,0:T(8,128)(2,1)} %attention_backward.1, bf16[768,1600]{0,1:T(8,128)(2,1)} %copy-done.26, bf16[768,1600]{0,1:T(8,128)(2,1)} %copy-done.25), kind=kOutput, calls=%fused_computation.2 | convolution fusion | flops 7562035200 | bytes 14548992 | tf_op jit(solution)/shard_map/dot_general | solution.py:47
  448.5 6.6 convolution_convert_fusion.4
  456.9 4.1 collective-permute-start.56
  461.3 6.8 fusion.39
  468.1 29.6 %collective-permute-done.56 = bf16[8,1,200,448]{3,2,1,0:T(8,128)(2,1)S(1)} collective-permute-done((bf16[8,1,200,448]{3,2,1,0:T(8,128)(2,1)S(1)}, bf16[8,1,200,448]{3,2,1,0:T(8,128)(2,1)S(1)}, u32[]{:S(2)}, u32[]{:S(2)}) %collective-permute-start.56) | collective-permute-done | bytes 1433632 | tf_op jit(solution)/shard_map/ppermute | solution.py:278
  506.4 5.1 collective-permute-done.26
  516.2 36.1 %collective-permute-done.28 = bf16[1,192,1600]{2,1,0:T(8,128)(2,1)S(1)} collective-permute-done((bf16[1,192,1600]{2,1,0:T(8,128)(2,1)S(1)}, bf16[1,192,1600]{2,1,0:T(8,128)(2,1)S(1)}, u32[]{:S(2)}, u32[]{:S(2)}) %collective-permute-start.28) | collective-permute-done | bytes 614432 | tf_op jit(solution)/shard_map/ppermute | solution.py:278
  552.3 6.8 collective-permute-start.61
  569.5 4.5 copy.95
  576.4 15.4 %collective-permute-done.62 = bf16[2,200,832]{2,1,0:T(8,128)(2,1)} collective-permute-done((bf16[2,200,832]{2,1,0:T(8,128)(2,1)}, bf16[2,200,832]{2,1,0:T(8,128)(2,1)}, u32[]{:S(2)}, u32[]{:S(2)}) %collective-permute-start.62) | collective-permute-done | bytes 665632 | tf_op jit(solution)/shard_map/ppermute | solution.py:278
  595.2 9.9 %collective-permute-done.37 = bf16[1,192,1600]{2,1,0:T(8,128)(2,1)S(1)} collective-permute-done((bf16[1,192,1600]{2,1,0:T(8,128)(2,1)}, bf16[1,192,1600]{2,1,0:T(8,128)(2,1)S(1)}, u32[]{:S(2)}, u32[]{:S(2)}) %collective-permute-start.37) | collective-permute-done | bytes 614432 | tf_op jit(solution)/shard_map/ppermute | solution.py:278
  606.1 4.8 collective-permute-done.41
  620.6 10.8 %collective-permute-done.43 = f32[1,8,1600]{2,1,0:T(8,128)} collective-permute-done((f32[1,8,1600]{2,1,0:T(8,128)}, f32[1,8,1600]{2,1,0:T(8,128)}, u32[]{:S(2)}, u32[]{:S(2)}) %collective-permute-start.43) | collective-permute-done | bytes 51232 | tf_op jit(solution)/shard_map/ppermute | solution.py:278
  635.6 12.2 %collective-permute-done.47 = bf16[1,200,1536]{2,1,0:T(8,128)(2,1)} collective-permute-done((bf16[1,200,1536]{2,1,0:T(8,128)(2,1)}, bf16[1,200,1536]{2,1,0:T(8,128)(2,1)}, u32[]{:S(2)}, u32[]{:S(2)}) %collective-permute-start.47) | collective-permute-done | bytes 614432 | tf_op jit(solution)/shard_map/ppermute | solution.py:278
  654.2 15.3 %collective-permute-start.45 = (f32[9,400]{1,0:T(8,128)S(1)}, f32[9,400]{1,0:T(8,128)S(1)}, u32[]{:S(2)}, u32[]{:S(2)}) collective-permute-start(f32[9,400]{1,0:T(8,128)S(1)} %bitcast.407), channel_id=1, source_target_pairs={{0,16},{8,24},{16,0},{24,8},{1,17},{9,25},{17,1},{25,9},{2,18},{10... | collective-permute-start | bytes 43208 | tf_op jit(solution)/shard_map/ppermute | solution.py:505
  679.2 9.7 %collective-permute-done.53 = bf16[1,200,1536]{2,1,0:T(8,128)(2,1)} collective-permute-done((bf16[1,200,1536]{2,1,0:T(8,128)(2,1)}, bf16[1,200,1536]{2,1,0:T(8,128)(2,1)}, u32[]{:S(2)}, u32[]{:S(2)}) %collective-permute-start.53) | collective-permute-done | bytes 614432 | tf_op jit(solution)/shard_map/ppermute | solution.py:278
  690.9 4.1 collective-permute-done.59
  701.4 4.4 copy.96
  706.5 4.7 join_windows.3
  712.1 10.3 %join_windows.2 = f32[400,4800]{1,0:T(8,128)} custom-call(s32[1]{0:T(128)} %bitcast.index_ref, bf16[200,1536]{1,0:T(8,128)(2,1)} %get-tuple-element.218.refs_0_, bf16[200,1536]{1,0:T(8,128)(2,1)} %bitcast.109.refs_1_, bf16[200,1536]{1,0:T(8,128)(2,1)} %bitcast.110.refs_2_, bf16[200,1536]{1,0:T(8,128)(2,1)} %bitcast.112.refs_3_, ...), custom_call_target="tpu_custom_call" | custom-call | bytes 5760000 | tf_op jit(solution)/shard_map/join_windows/pallas_call | solution.py:479
  (468 shorter events, 207.2 us)
Async XLA Ops:
  7.2 205.5 %all-gather.4.cloned.1.call-start = ((), (), s32[]{:S(2)}) async-start(), calls=%async_computation.5 | async-start | bytes 3584000 | tf_op jit(solution)/shard_map/all_gather | solution.py:363
  10.4 19.1 %collective-permute-start = (bf16[1,200,1536]{2,1,0:T(8,128)(2,1)}, bf16[1,200,1536]{2,1,0:T(8,128)(2,1)S(1)}, u32[]{:S(2)}, u32[]{:S(2)}) collective-permute-start(bf16[1,200,1536]{2,1,0:T(8,128)(2,1)} %constant_dynamic-slice_fusion.12), channel_id=1, source_target_pairs={{0,8},{8,16},{16,24},{24,0},{1,9},{9,17},{17,25},{25,1},{2,10},{10... | collective-permute-start | bytes 1843208 | tf_op jit(solution)/shard_map/ppermute | solution.py:278
  29.5 214.5 %all-gather.6.cloned.1.call-start = ((), (), s32[]{:S(2)}) async-start(), calls=%async_computation.11 | async-start | bytes 7168000 | tf_op jit(solution)/shard_map/all_gather | solution.py:559
  29.8 16.3 %collective-permute-start.2 = (bf16[9,400]{1,0:T(8,128)(2,1)S(1)}, bf16[9,400]{1,0:T(8,128)(2,1)S(1)}, u32[]{:S(2)}, u32[]{:S(2)}) collective-permute-start(bf16[9,400]{1,0:T(8,128)(2,1)S(1)} %stack.75), channel_id=1, source_target_pairs={{0,8},{8,16},{16,24},{24,0},{1,9},{9,17},{17,25},{25,1},{2,10},{10... | collective-permute-start | bytes 21608 | tf_op jit(solution)/shard_map/ppermute | solution.py:344
  29.9 16.3 %collective-permute-start.3 = (bf16[9,400]{1,0:T(8,128)(2,1)S(1)}, bf16[9,400]{1,0:T(8,128)(2,1)S(1)}, u32[]{:S(2)}, u32[]{:S(2)}) collective-permute-start(bf16[9,400]{1,0:T(8,128)(2,1)S(1)} %stack.75), channel_id=1, source_target_pairs={{0,16},{8,24},{16,0},{24,8},{1,17},{9,25},{17,1},{25,9},{2,18},{10... | collective-permute-start | bytes 21608 | tf_op jit(solution)/shard_map/ppermute | solution.py:344
  33.7 113.7 %collective-permute-start.1 = (bf16[768,1600]{0,1:T(8,128)(2,1)}, bf16[768,1600]{0,1:T(8,128)(2,1)}, u32[]{:S(2)}, u32[]{:S(2)}) collective-permute-start(bf16[768,1600]{0,1:T(8,128)(2,1)} %param.16), channel_id=1, source_target_pairs={{0,4},{1,5},{2,6},{3,7},{8,12},{9,13},{10,14},{11,15},{16,20},{17,... | collective-permute-start | bytes 7372808 | tf_op jit(solution)/shard_map/ppermute | solution.py:578
  47.2 30.8 %collective-permute-start.6 = (bf16[1,200,1536]{2,1,0:T(8,128)(2,1)S(1)}, bf16[1,200,1536]{2,1,0:T(8,128)(2,1)S(1)}, u32[]{:S(2)}, u32[]{:S(2)}) collective-permute-start(bf16[1,200,1536]{2,1,0:T(8,128)(2,1)S(1)} %collective-permute-done), channel_id=1, source_target_pairs={{0,8},{8,16},{16,24},{24,0},{1,9},{9,17},{17,25},{25,1},{2,10},{10... | collective-permute-start | bytes 1843208 | tf_op jit(solution)/shard_map/ppermute | solution.py:278
  49.7 502.6 %reduce-scatter.12.cloned.1.call-start = ((), (), s32[]{:S(2)}) async-start(), calls=%async_computation.9 | async-start | bytes 3584000 | tf_op jit(solution)/shard_map/reduce_scatter | solution.py:427
  49.7 54.5 %collective-permute-start.5 = (bf16[1,200,1536]{2,1,0:T(8,128)(2,1)S(1)}, bf16[1,200,1536]{2,1,0:T(8,128)(2,1)}, u32[]{:S(2)}, u32[]{:S(2)}) collective-permute-start(bf16[1,200,1536]{2,1,0:T(8,128)(2,1)S(1)} %collective-permute-done), channel_id=1, source_target_pairs={{0,4},{4,0},{1,5},{5,1},{2,6},{6,2},{3,7},{7,3},{8,12},{12,8},{9,1... | collective-permute-start | bytes 1843208 | tf_op jit(solution)/shard_map/ppermute | solution.py:278
  78.1 32.7 %collective-permute-start.13 = (bf16[2,200,448]{2,1,0:T(8,128)(2,1)S(1)}, bf16[2,200,448]{2,1,0:T(8,128)(2,1)}, u32[]{:S(2)}, u32[]{:S(2)}) collective-permute-start(bf16[2,200,448]{2,1,0:T(8,128)(2,1)S(1)} %bitcast.376), channel_id=1, source_target_pairs={{0,8},{8,16},{16,24},{24,0},{1,9},{9,17},{17,25},{25,1},{2,10},{10... | collective-permute-start | bytes 1075208 | tf_op jit(solution)/shard_map/ppermute | solution.py:278
  89.7 50.8 %collective-permute-start.14 = (bf16[2,200,448]{2,1,0:T(8,128)(2,1)S(1)}, bf16[2,200,448]{2,1,0:T(8,128)(2,1)}, u32[]{:S(2)}, u32[]{:S(2)}) collective-permute-start(bf16[2,200,448]{2,1,0:T(8,128)(2,1)S(1)} %bitcast.377), channel_id=1, source_target_pairs={{0,16},{8,24},{16,0},{24,8},{1,17},{9,25},{17,1},{25,9},{2,18},{10... | collective-permute-start | bytes 1075208 | tf_op jit(solution)/shard_map/ppermute | solution.py:278
  102.0 45.3 %collective-permute-start.7 = (bf16[1,200,1536]{2,1,0:T(8,128)(2,1)S(1)}, bf16[1,200,1536]{2,1,0:T(8,128)(2,1)S(1)}, u32[]{:S(2)}, u32[]{:S(2)}) collective-permute-start(bf16[1,200,1536]{2,1,0:T(8,128)(2,1)S(1)} %copy-done.45), channel_id=1, source_target_pairs={{0,4},{4,0},{1,5},{5,1},{2,6},{6,2},{3,7},{7,3},{8,12},{12,8},{9,1... | collective-permute-start | bytes 1843208 | tf_op jit(solution)/shard_map/ppermute | solution.py:278
  104.2 41.7 %collective-permute-start.8 = (bf16[1,200,1536]{2,1,0:T(8,128)(2,1)S(1)}, bf16[1,200,1536]{2,1,0:T(8,128)(2,1)S(1)}, u32[]{:S(2)}, u32[]{:S(2)}) collective-permute-start(bf16[1,200,1536]{2,1,0:T(8,128)(2,1)S(1)} %copy-done.45), channel_id=1, source_target_pairs={{0,8},{8,16},{16,24},{24,0},{1,9},{9,17},{17,25},{25,1},{2,10},{10... | collective-permute-start | bytes 1843208 | tf_op jit(solution)/shard_map/ppermute | solution.py:278
  110.7 32.7 %collective-permute-start.15 = (bf16[2,200,448]{2,1,0:T(8,128)(2,1)S(1)}, bf16[2,200,448]{2,1,0:T(8,128)(2,1)S(1)}, u32[]{:S(2)}, u32[]{:S(2)}) collective-permute-start(bf16[2,200,448]{2,1,0:T(8,128)(2,1)S(1)} %bitcast.378), channel_id=1, source_target_pairs={{0,24},{8,0},{16,8},{24,16},{1,25},{9,1},{17,9},{25,17},{2,26},{10... | collective-permute-start | bytes 1075208 | tf_op jit(solution)/shard_map/ppermute | solution.py:278
  144.2 43.8 %collective-permute-start.16 = (bf16[8,200,448]{2,1,0:T(8,128)(2,1)}, bf16[8,200,448]{2,1,0:T(8,128)(2,1)}, u32[]{:S(2)}, u32[]{:S(2)}) collective-permute-start(bf16[8,200,448]{2,1,0:T(8,128)(2,1)} %bitcast.26), channel_id=1, source_target_pairs={{0,2},{1,3},{2,0},{3,1},{4,6},{5,7},{6,4},{7,5},{8,10},{9,11},{10,... | collective-permute-start | bytes 4300808 | tf_op jit(solution)/shard_map/ppermute | solution.py:278
  145.9 59.9 %collective-permute-start.18 = (bf16[8,200,448]{2,1,0:T(8,128)(2,1)}, bf16[8,200,448]{2,1,0:T(8,128)(2,1)}, u32[]{:S(2)}, u32[]{:S(2)}) collective-permute-start(bf16[8,200,448]{2,1,0:T(8,128)(2,1)} %bitcast.26), channel_id=1, source_target_pairs={{0,1},{1,0},{2,3},{3,2},{4,5},{5,4},{6,7},{7,6},{8,9},{9,8},{10,11... | collective-permute-start | bytes 4300808 | tf_op jit(solution)/shard_map/ppermute | solution.py:278
  188.0 19.7 %collective-permute-start.17 = (bf16[8,200,448]{2,1,0:T(8,128)(2,1)}, bf16[8,200,448]{2,1,0:T(8,128)(2,1)}, u32[]{:S(2)}, u32[]{:S(2)}) collective-permute-start(bf16[8,200,448]{2,1,0:T(8,128)(2,1)} %bitcast.28), channel_id=1, source_target_pairs={{0,1},{1,0},{2,3},{3,2},{4,5},{5,4},{6,7},{7,6},{8,9},{9,8},{10,11... | collective-permute-start | bytes 4300808 | tf_op jit(solution)/shard_map/ppermute | solution.py:278
  212.7 69.7 %collective-permute-start.22 = (bf16[8,200,832]{2,1,0:T(8,128)(2,1)}, bf16[8,200,832]{2,1,0:T(8,128)(2,1)}, u32[]{:S(2)}, u32[]{:S(2)}) collective-permute-start(bf16[8,200,832]{2,1,0:T(8,128)(2,1)} %bitcast.423), channel_id=1, source_target_pairs={{0,4},{4,0},{1,5},{5,1},{2,6},{6,2},{3,7},{7,3},{8,12},{12,8},{9,1... | collective-permute-start | bytes 7987208 | tf_op jit(solution)/shard_map/ppermute | solution.py:278
  221.3 16.8 %collective-permute-start.19 = (bf16[1,192,1600]{2,1,0:T(8,128)(2,1)}, bf16[1,192,1600]{2,1,0:T(8,128)(2,1)S(1)}, u32[]{:S(2)}, u32[]{:S(2)}) collective-permute-start(bf16[1,192,1600]{2,1,0:T(8,128)(2,1)} %fusion.182), channel_id=1, source_target_pairs={{0,2},{1,3},{2,0},{3,1},{4,6},{5,7},{6,4},{7,5},{8,10},{9,11},{10,... | collective-permute-start | bytes 1843208 | tf_op jit(solution)/shard_map/ppermute | solution.py:278
  295.9 263.3 %reduce-scatter.10.cloned.1.call-start = ((), (), s32[]{:S(2)}) async-start(), calls=%async_computation.8 | async-start | bytes 3584000 | tf_op jit(solution)/shard_map/reduce_scatter | solution.py:427
  322.7 17.8 %collective-permute-start.24 = (bf16[1,192,1600]{2,1,0:T(8,128)(2,1)S(1)}, bf16[1,192,1600]{2,1,0:T(8,128)(2,1)}, u32[]{:S(2)}, u32[]{:S(2)}) collective-permute-start(bf16[1,192,1600]{2,1,0:T(8,128)(2,1)S(1)} %fusion.71), channel_id=1, source_target_pairs={{0,2},{1,3},{2,0},{3,1},{4,6},{5,7},{6,4},{7,5},{8,10},{9,11},{10,... | collective-permute-start | bytes 1843208 | tf_op jit(solution)/shard_map/ppermute | solution.py:278
  329.8 64.6 %collective-permute-start.33 = (bf16[8,1,200,832]{3,2,1,0:T(8,128)(2,1)}, bf16[8,1,200,832]{3,2,1,0:T(8,128)(2,1)}, u32[]{:S(2)}, u32[]{:S(2)}) collective-permute-start(bf16[8,1,200,832]{3,2,1,0:T(8,128)(2,1)} %bitcast.69), channel_id=1, source_target_pairs={{0,4},{4,0},{1,5},{5,1},{2,6},{6,2},{3,7},{7,3},{8,12},{12,8},{9,1... | collective-permute-start | bytes 7987208 | tf_op jit(solution)/shard_map/ppermute | solution.py:278
  336.0 280.0 %reduce-scatter.6.cloned.1.call-start = ((), (), s32[]{:S(2)}) async-start(), calls=%async_computation.6 | async-start | bytes 6144000 | tf_op jit(solution)/shard_map/reduce_scatter | solution.py:427
  433.3 218.8 %reduce-scatter.8.cloned.1.call-start = ((), (), s32[]{:S(2)}) async-start(), calls=%async_computation.7 | async-start | bytes 2048000 | tf_op jit(solution)/shard_map/reduce_scatter | solution.py:427
  444.0 17.0 %collective-permute-start.25 = (bf16[2,192,1600]{2,1,0:T(8,128)(2,1)S(1)}, bf16[2,192,1600]{2,1,0:T(8,128)(2,1)S(1)}, u32[]{:S(2)}, u32[]{:S(2)}) collective-permute-start(bf16[2,192,1600]{2,1,0:T(8,128)(2,1)S(1)} %bitcast.424), channel_id=1, source_target_pairs={{0,1},{1,0},{2,3},{3,2},{4,5},{5,4},{6,7},{7,6},{8,9},{9,8},{10,11... | collective-permute-start | bytes 3686408 | tf_op jit(solution)/shard_map/ppermute | solution.py:278
  455.1 44.6 %collective-permute-start.35 = (bf16[4,192,1600]{2,1,0:T(8,128)(2,1)}, bf16[4,192,1600]{2,1,0:T(8,128)(2,1)}, u32[]{:S(2)}, u32[]{:S(2)}) collective-permute-start(bf16[4,192,1600]{2,1,0:T(8,128)(2,1)} %bitcast.86), channel_id=1, source_target_pairs={{0,1},{1,0},{2,3},{3,2},{4,5},{5,4},{6,7},{7,6},{8,9},{9,8},{10,11... | collective-permute-start | bytes 7372808 | tf_op jit(solution)/shard_map/ppermute | solution.py:278
  456.9 40.8 %collective-permute-start.56 = (bf16[8,1,200,448]{3,2,1,0:T(8,128)(2,1)S(1)}, bf16[8,1,200,448]{3,2,1,0:T(8,128)(2,1)S(1)}, u32[]{:S(2)}, u32[]{:S(2)}) collective-permute-start(bf16[8,1,200,448]{3,2,1,0:T(8,128)(2,1)S(1)} %bitcast.373), channel_id=1, source_target_pairs={{0,2},{1,3},{2,0},{3,1},{4,6},{5,7},{6,4},{7,5},{8,10},{9,11},{10,... | collective-permute-start | bytes 4300808 | tf_op jit(solution)/shard_map/ppermute | solution.py:278
  461.2 50.3 %collective-permute-start.26 = (bf16[1,192,1600]{2,1,0:T(8,128)(2,1)S(1)}, bf16[1,192,1600]{2,1,0:T(8,128)(2,1)}, u32[]{:S(2)}, u32[]{:S(2)}) collective-permute-start(bf16[1,192,1600]{2,1,0:T(8,128)(2,1)S(1)} %fusion.72), channel_id=1, source_target_pairs={{0,2},{1,3},{2,0},{3,1},{4,6},{5,7},{6,4},{7,5},{8,10},{9,11},{10,... | collective-permute-start | bytes 1843208 | tf_op jit(solution)/shard_map/ppermute | solution.py:278
  499.6 174.3 %reduce-scatter.14.cloned.1.call-start = ((), (), s32[]{:S(2)}) async-start(), calls=%async_computation.10 | async-start | bytes 3584000 | tf_op jit(solution)/shard_map/reduce_scatter | solution.py:427
  504.4 54.9 %collective-permute-start.36 = (bf16[2,192,1600]{2,1,0:T(8,128)(2,1)}, bf16[2,192,1600]{2,1,0:T(8,128)(2,1)}, u32[]{:S(2)}, u32[]{:S(2)}) collective-permute-start(bf16[2,192,1600]{2,1,0:T(8,128)(2,1)} %bitcast.89), channel_id=1, source_target_pairs={{0,2},{1,3},{2,0},{3,1},{4,6},{5,7},{6,4},{7,5},{8,10},{9,11},{10,... | collective-permute-start | bytes 3686408 | tf_op jit(solution)/shard_map/ppermute | solution.py:278
  513.0 39.3 %collective-permute-start.28 = (bf16[1,192,1600]{2,1,0:T(8,128)(2,1)S(1)}, bf16[1,192,1600]{2,1,0:T(8,128)(2,1)S(1)}, u32[]{:S(2)}, u32[]{:S(2)}) collective-permute-start(bf16[1,192,1600]{2,1,0:T(8,128)(2,1)S(1)} %bitcast.367), channel_id=1, source_target_pairs={{0,2},{1,3},{2,0},{3,1},{4,6},{5,7},{6,4},{7,5},{8,10},{9,11},{10,... | collective-permute-start | bytes 1843208 | tf_op jit(solution)/shard_map/ppermute | solution.py:278
  516.1 49.5 %collective-permute-start.27 = (bf16[1,192,1600]{2,1,0:T(8,128)(2,1)S(1)}, bf16[1,192,1600]{2,1,0:T(8,128)(2,1)}, u32[]{:S(2)}, u32[]{:S(2)}) collective-permute-start(bf16[1,192,1600]{2,1,0:T(8,128)(2,1)S(1)} %bitcast.368), channel_id=1, source_target_pairs={{0,1},{1,0},{2,3},{3,2},{4,5},{5,4},{6,7},{7,6},{8,9},{9,8},{10,11... | collective-permute-start | bytes 1843208 | tf_op jit(solution)/shard_map/ppermute | solution.py:278
  552.3 24.1 %collective-permute-start.61 = (bf16[2,200,832]{2,1,0:T(8,128)(2,1)}, bf16[2,200,832]{2,1,0:T(8,128)(2,1)}, u32[]{:S(2)}, u32[]{:S(2)}) collective-permute-start(bf16[2,200,832]{2,1,0:T(8,128)(2,1)} %bitcast.381), channel_id=1, source_target_pairs={{0,4},{4,0},{1,5},{5,1},{2,6},{6,2},{3,7},{7,3},{8,12},{12,8},{9,1... | collective-permute-start | bytes 1996808 | tf_op jit(solution)/shard_map/ppermute | solution.py:278
  559.1 32.6 %collective-permute-start.62 = (bf16[2,200,832]{2,1,0:T(8,128)(2,1)}, bf16[2,200,832]{2,1,0:T(8,128)(2,1)}, u32[]{:S(2)}, u32[]{:S(2)}) collective-permute-start(bf16[2,200,832]{2,1,0:T(8,128)(2,1)} %bitcast.382), channel_id=1, source_target_pairs={{0,4},{4,0},{1,5},{5,1},{2,6},{6,2},{3,7},{7,3},{8,12},{12,8},{9,1... | collective-permute-start | bytes 1996808 | tf_op jit(solution)/shard_map/ppermute | solution.py:278
  564.1 41.0 %collective-permute-start.37 = (bf16[1,192,1600]{2,1,0:T(8,128)(2,1)}, bf16[1,192,1600]{2,1,0:T(8,128)(2,1)S(1)}, u32[]{:S(2)}, u32[]{:S(2)}) collective-permute-start(bf16[1,192,1600]{2,1,0:T(8,128)(2,1)} %fusion.73), channel_id=1, source_target_pairs={{4,0},{5,1},{6,2},{7,3},{12,8},{13,9},{14,10},{15,11},{20,16},{21,... | collective-permute-start | bytes 1843208 | tf_op jit(solution)/shard_map/ppermute | solution.py:278
  613.3 58.6 %collective-permute-start.39 = (bf16[1,192,1600]{2,1,0:T(8,128)(2,1)S(1)}, bf16[1,192,1600]{2,1,0:T(8,128)(2,1)}, u32[]{:S(2)}, u32[]{:S(2)}) collective-permute-start(bf16[1,192,1600]{2,1,0:T(8,128)(2,1)S(1)} %bitcast.365), channel_id=1, source_target_pairs={{0,2},{1,3},{2,0},{3,1},{4,6},{5,7},{6,4},{7,5},{8,10},{9,11},{10,... | collective-permute-start | bytes 1843208 | tf_op jit(solution)/shard_map/ppermute | solution.py:278
  618.5 17.0 %collective-permute-start.51 = (bf16[1,200,1536]{2,1,0:T(8,128)(2,1)}, bf16[1,200,1536]{2,1,0:T(8,128)(2,1)}, u32[]{:S(2)}, u32[]{:S(2)}) collective-permute-start(bf16[1,200,1536]{2,1,0:T(8,128)(2,1)} %get-tuple-element.219), channel_id=1, source_target_pairs={{0,4},{4,0},{1,5},{5,1},{2,6},{6,2},{3,7},{7,3},{8,12},{12,8},{9,1... | collective-permute-start | bytes 1843208 | tf_op jit(solution)/shard_map/ppermute | solution.py:278
  618.8 29.0 %collective-permute-start.47 = (bf16[1,200,1536]{2,1,0:T(8,128)(2,1)}, bf16[1,200,1536]{2,1,0:T(8,128)(2,1)}, u32[]{:S(2)}, u32[]{:S(2)}) collective-permute-start(bf16[1,200,1536]{2,1,0:T(8,128)(2,1)} %get-tuple-element.220), channel_id=1, source_target_pairs={{0,4},{4,0},{1,5},{5,1},{2,6},{6,2},{3,7},{7,3},{8,12},{12,8},{9,1... | collective-permute-start | bytes 1843208 | tf_op jit(solution)/shard_map/ppermute | solution.py:278
  632.5 37.1 %collective-permute-start.46 = (f32[9,400]{1,0:T(8,128)S(1)}, f32[9,400]{1,0:T(8,128)S(1)}, u32[]{:S(2)}, u32[]{:S(2)}) collective-permute-start(f32[9,400]{1,0:T(8,128)S(1)} %bitcast.405), channel_id=1, source_target_pairs={{0,24},{8,0},{16,8},{24,16},{1,25},{9,1},{17,9},{25,17},{2,26},{10... | collective-permute-start | bytes 43208 | tf_op jit(solution)/shard_map/ppermute | solution.py:505
  650.4 27.8 %collective-permute-start.49 = (bf16[1,200,1536]{2,1,0:T(8,128)(2,1)}, bf16[1,200,1536]{2,1,0:T(8,128)(2,1)}, u32[]{:S(2)}, u32[]{:S(2)}) collective-permute-start(bf16[1,200,1536]{2,1,0:T(8,128)(2,1)} %bitcast.108), channel_id=1, source_target_pairs={{0,2},{1,3},{2,0},{3,1},{4,6},{5,7},{6,4},{7,5},{8,10},{9,11},{10,... | collective-permute-start | bytes 1843208 | tf_op jit(solution)/shard_map/ppermute | solution.py:278
  652.0 24.4 %collective-permute-start.57 = (bf16[2,200,448]{2,1,0:T(8,128)(2,1)}, bf16[2,200,448]{2,1,0:T(8,128)(2,1)}, u32[]{:S(2)}, u32[]{:S(2)}) collective-permute-start(bf16[2,200,448]{2,1,0:T(8,128)(2,1)} %bitcast.402), channel_id=1, source_target_pairs={{0,4},{4,0},{1,5},{5,1},{2,6},{6,2},{3,7},{7,3},{8,12},{12,8},{9,1... | collective-permute-start | bytes 1075208 | tf_op jit(solution)/shard_map/ppermute | solution.py:278
  654.2 19.8 %collective-permute-start.45 = (f32[9,400]{1,0:T(8,128)S(1)}, f32[9,400]{1,0:T(8,128)S(1)}, u32[]{:S(2)}, u32[]{:S(2)}) collective-permute-start(f32[9,400]{1,0:T(8,128)S(1)} %bitcast.407), channel_id=1, source_target_pairs={{0,16},{8,24},{16,0},{24,8},{1,17},{9,25},{17,1},{25,9},{2,18},{10... | collective-permute-start | bytes 43208 | tf_op jit(solution)/shard_map/ppermute | solution.py:505
  671.9 17.0 %collective-permute-start.53 = (bf16[1,200,1536]{2,1,0:T(8,128)(2,1)}, bf16[1,200,1536]{2,1,0:T(8,128)(2,1)}, u32[]{:S(2)}, u32[]{:S(2)}) collective-permute-start(bf16[1,200,1536]{2,1,0:T(8,128)(2,1)} %bitcast.115), channel_id=1, source_target_pairs={{0,2},{1,3},{2,0},{3,1},{4,6},{5,7},{6,4},{7,5},{8,10},{9,11},{10,... | collective-permute-start | bytes 1843208 | tf_op jit(solution)/shard_map/ppermute | solution.py:278
  674.0 16.3 %collective-permute-start.63 = (bf16[2,200,832]{2,1,0:T(8,128)(2,1)}, bf16[2,200,832]{2,1,0:T(8,128)(2,1)S(1)}, u32[]{:S(2)}, u32[]{:S(2)}) collective-permute-start(bf16[2,200,832]{2,1,0:T(8,128)(2,1)} %bitcast.369), channel_id=1, source_target_pairs={{0,4},{4,0},{1,5},{5,1},{2,6},{6,2},{3,7},{7,3},{8,12},{12,8},{9,1... | collective-permute-start | bytes 1996808 | tf_op jit(solution)/shard_map/ppermute | solution.py:278
  678.2 16.9 %collective-permute-start.59 = (bf16[2,200,448]{2,1,0:T(8,128)(2,1)S(1)}, bf16[2,200,448]{2,1,0:T(8,128)(2,1)}, u32[]{:S(2)}, u32[]{:S(2)}) collective-permute-start(bf16[2,200,448]{2,1,0:T(8,128)(2,1)S(1)} %bitcast.371), channel_id=1, source_target_pairs={{0,2},{1,3},{2,0},{3,1},{4,6},{5,7},{6,4},{7,5},{8,10},{9,11},{10,... | collective-permute-start | bytes 1075208 | tf_op jit(solution)/shard_map/ppermute | solution.py:278
  690.3 20.9 %collective-permute-start.48 = (bf16[1,200,1536]{2,1,0:T(8,128)(2,1)}, bf16[1,200,1536]{2,1,0:T(8,128)(2,1)}, u32[]{:S(2)}, u32[]{:S(2)}) collective-permute-start(bf16[1,200,1536]{2,1,0:T(8,128)(2,1)} %bitcast.108), channel_id=1, source_target_pairs={{0,1},{1,0},{2,3},{3,2},{4,5},{5,4},{6,7},{7,6},{8,9},{9,8},{10,11... | collective-permute-start | bytes 1843208 | tf_op jit(solution)/shard_map/ppermute | solution.py:278
  690.3 20.9 %collective-permute-start.52 = (bf16[1,200,1536]{2,1,0:T(8,128)(2,1)}, bf16[1,200,1536]{2,1,0:T(8,128)(2,1)S(1)}, u32[]{:S(2)}, u32[]{:S(2)}) collective-permute-start(bf16[1,200,1536]{2,1,0:T(8,128)(2,1)} %bitcast.115), channel_id=1, source_target_pairs={{0,1},{1,0},{2,3},{3,2},{4,5},{5,4},{6,7},{7,6},{8,9},{9,8},{10,11... | collective-permute-start | bytes 1843208 | tf_op jit(solution)/shard_map/ppermute | solution.py:278
  690.8 20.4 %collective-permute-start.50 = (bf16[1,200,1536]{2,1,0:T(8,128)(2,1)}, bf16[1,200,1536]{2,1,0:T(8,128)(2,1)}, u32[]{:S(2)}, u32[]{:S(2)}) collective-permute-start(bf16[1,200,1536]{2,1,0:T(8,128)(2,1)} %bitcast.111), channel_id=1, source_target_pairs={{0,1},{1,0},{2,3},{3,2},{4,5},{5,4},{6,7},{7,6},{8,9},{9,8},{10,11... | collective-permute-start | bytes 1843208 | tf_op jit(solution)/shard_map/ppermute | solution.py:278
  (103 other events, 1370.5 us)
Sparse Core Ops, SparseCore 0:
  29.7 106.8 all-gather.3
  138.1 105.8 all-gather.5
  296.0 66.6 reduce-scatter.11
  364.8 55.9 reduce-scatter.9
  433.4 110.7 reduce-scatter.5
  546.9 36.9 reduce-scatter.7
  586.2 55.1 reduce-scatter.13
